TPU v7x, 32 devices: a whole 2x2x4 slice. The times are simulated.
32 devices in a mesh: dp: 8 (over y, x, core), seq: 4 (over z).
Axes of the slice: x: 2, y: 2, z: 4, core: 2. Of those that a mesh axis runs over, the one named last changes fastest.
Arguments:
- hidden_in: bfloat16 [8192, 768], P(('dp', 'seq')), may hold values from -6 to 6
- skip_values: bfloat16 [8192, 384], P(('dp', 'seq')), may hold values from -6 to 6
- out_grad: bfloat16 [8192, 768], P(('dp', 'seq')), may hold values from -6 to 6
- doc_lens: int32 [8, 3], P('dp'), may hold values from 0 to 1024, as said below
- valid: int32 [8192], P('dp'), may hold values from 0 to 1, as said below
- norm1_gain: float32 [768], replicated, may hold values from 0.5 to 1.5
- norm1_shift: float32 [768], replicated, may hold values from -1.25 to 1.25
- query_w: bfloat16 [768, 768], replicated, may hold values from -0.3125 to 0.3125
- query_b: float32 [768], replicated, may hold values from -1.25 to 1.25
- key_w: bfloat16 [768, 768], replicated, may hold values from -0.3125 to 0.3125
- value_w: bfloat16 [768, 384], replicated, may hold values from -0.21875 to 0.21875
- value_b: float32 [384], replicated, may hold values from -1.25 to 1.25
- proj_w: bfloat16 [768, 768], replicated, may hold values from -0.625 to 0.625
- proj_b: float32 [768], replicated, may hold values from -1.25 to 1.25
- norm2_gain: float32 [768], replicated, may hold values from 0.5 to 1.5
- norm2_shift: float32 [768], replicated, may hold values from -1.25 to 1.25
- fc_w: bfloat16 [768, 3072], replicated, may hold values from -0.21875 to 0.21875
- fc_b: float32 [3072], replicated, may hold values from -1.25 to 1.25
- out_w: bfloat16 [3072, 768], replicated, may hold values from -0.109375 to 0.109375
- out_b: float32 [768], replicated, may hold values from -1.25 to 1.25
Outputs:
- output: bfloat16 [8192, 768], P(('dp', 'seq'))
- grad_input: bfloat16 [8192, 768], P(('dp', 'seq'))
- grad_skip: bfloat16 [8192, 384], P(('dp', 'seq'))
- grad_norm1_gain: float32 [768], replicated
- grad_norm1_shift: float32 [768], replicated
- grad_query_w: float32 [768, 768], replicated
- grad_query_b: float32 [768], replicated
- grad_key_w: float32 [768, 768], replicated
- grad_value_w: float32 [768, 384], replicated
- grad_value_b: float32 [384], replicated
- grad_proj_w: float32 [768, 768], replicated
- grad_proj_b: float32 [768], replicated
- grad_norm2_gain: float32 [768], replicated
- grad_norm2_shift: float32 [768], replicated
- grad_fc_w: float32 [768, 3072], replicated
- grad_fc_b: float32 [3072], replicated
- grad_out_w: float32 [3072, 768], replicated
- grad_out_b: float32 [768], replicated
- norms: float32 [8, 3], P('dp')
Inputs may be any that keep to these rules, and one draw needn't show every extreme that they name: `doc_lens`: row g lists the lengths of the sequences packed in order into group g and sums to 1024. In 8 // 2 groups one sequence fills the whole group and the other entries are 0; every other group holds three sequences, the longest of 512 tokens. Of the two tokens 2 i and 2 i + 1, at least one has valid = 1.
All inputs are finite; a program needn't handle non-finite values.
Results may differ from a plain program's by a relative error of at most 0.014.
The roundings to bfloat16 on the way count: a program that leaves them out, or rounds other values in their place, can miss the bound.
Values may be sent and summed in bfloat16 or wider, within the bound.
A program may use at most 192 MiB of HBM per device.

v0:
```python
import functools
import math

import jax
import jax.numpy as jnp
from jax import lax
from jax.experimental import pallas as pl
from jax.experimental.pallas import tpu as pltpu
from jax.sharding import PartitionSpec as P

D = 768
HEADS = 12
HDIM = 64
VFRESH = 384


norm_eps = 1e-05
square_eps = 1e-06
tanh_coef = 0.7978845608028654
masked_score = -1e30


MESH = pl.DeviceIdType.MESH
SUB = 16
WID = 768
UNIT_BYTES = SUB * WID * 2
SHARES = ("ababzababzab", "ababab")


def bits_of(n):
    return n.bit_length() - 1


def partner(dim, dp, sq):
    kind, j = dim
    step = 1 << j
    if kind == "dp":
        bit = (dp // step) % 2
        return bit, (dp + step - 2 * step * bit, sq)
    bit = (sq // step) % 2
    return bit, (dp, sq + step - 2 * step * bit)


def plan_streams(n_dp, n_seq, phases, starts):
    dpb = [("dp", j) for j in range(1, bits_of(n_dp))]
    sqb = [("seq", j) for j in range(bits_of(n_seq))]
    mid = len(dpb) // 2
    orders = {"a": dpb + sqb, "b": dpb[mid:] + dpb[:mid] + sqb, "z": sqb + dpb}
    quantum = (n_dp // 2) * n_seq
    streams = []
    for phase, (half_units, kinds) in enumerate(phases):
        total = half_units // quantum
        first = used = 0
        for i, kind in enumerate(kinds):
            upto = round(total * (i + 1) / len(kinds))
            n = (upto - used) * quantum
            used = upto
            if n:
                streams.append((phase, first, n, orders[kind], starts[phase]))
                first += n
    return streams


def schedule(streams, busy=()):
    free = {}
    for res, upto in busy:
        free[res] = upto
    out = []
    stages = []
    for phase, first, n, order, start in streams:
        seq = []
        size = n
        seq.append((("dp", 0), size))
        for d in order:
            size //= 2
            seq.append((d, size))
        for d in reversed(order):
            seq.append((d, size))
            size *= 2
        seq.append((("dp", 0), size))
        stages.append(seq)
    at = [0] * len(streams)
    waiting = [(st[4], s) for s, st in enumerate(streams)]
    pending = []

    def launch(s, t):
        d, size = stages[s][at[s]]
        b = size * UNIT_BYTES / 1e6
        if d == ("dp", 0):
            res, dur = "c", b / 0.5
        elif d[0] == "dp":
            res, dur = d, b / 0.045
        else:
            res, dur = "seq", b / 0.045 * (1 << d[1])
        st = max(t, free.get(res, 0.0))
        free[res] = st + dur
        pending.append((st + dur + 2.0, s))

    while pending or waiting:
        pending.sort()
        waiting.sort()
        if waiting and (not pending or waiting[0][0] <= pending[0][0]):
            t, s = waiting.pop(0)
            launch(s, t)
            continue
        t, s = pending.pop(0)
        out.append((t, s, at[s]))
        at[s] += 1
        if at[s] < len(stages[s]):
            launch(s, t + 0.3)
    return out


class Exchange:
    def __init__(self, streams, halves, dp, sq, parts, out, acc, recv, gat, sems):
        self.streams, self.halves = streams, halves
        self.dp, self.sq = dp, sq
        self.parts, self.out, self.acc, self.recv, self.gat = parts, out, acc, recv, gat
        self.send_sem, self.recv_sem, self.local_sem = sems
        self.cbit, self.cdev = partner(("dp", 0), dp, sq)
        self.base = [sum(halves[:p]) for p in range(len(halves))]
        self.off = [[self.base[s[0]] + s[1]] for s in streams]
        self.roff = []
        r = sum(halves)
        for phase, first, n, order, _ in streams:
            rows = [self.base[phase] + first]
            size = n
            for _ in order:
                size //= 2
                rows.append(r)
                r += size
            self.roff.append(rows)

    @staticmethod
    def recv_total(streams, halves):
        r = sum(halves)
        for phase, first, n, order, _ in streams:
            size = n
            for _ in order:
                size //= 2
                r += size
        return r

    def n_stages(self, s):
        return 2 * (len(self.streams[s][3]) + 1)

    def remote(self, s, k, src, dst, dev):
        return pltpu.make_async_remote_copy(
            src_ref=src, dst_ref=dst, send_sem=self.send_sem.at[s, k], recv_sem=self.recv_sem.at[s, k],
            device_id=dev, device_id_type=MESH)

    def copies(self, s, k):
        phase, first, n, order, _ = self.streams[s]
        depth = len(order)
        half_units, base = self.halves[phase], self.base[phase]
        here = base + first
        if k == 0:
            part = self.parts[phase]
            other = (1 - self.cbit) * half_units + first
            mine = self.cbit * half_units + first
            return (self.remote(s, k, part.at[pl.ds(other, n)], self.recv.at[pl.ds(here, n)], self.cdev),
                    pltpu.make_async_copy(part.at[pl.ds(mine, n)], self.acc.at[pl.ds(here, n)], self.local_sem.at[s, 0]))
        if k <= depth:
            half = n >> k
            bit, dev = partner(order[k - 1], self.dp, self.sq)
            at = self.off[s][k - 1]
            return (self.remote(s, k, self.acc.at[pl.ds(at + (1 - bit) * half, half)],
                                self.recv.at[pl.ds(self.roff[s][k], half)], dev), None)
        g = 2 * depth + 1 - k
        if g >= 1:
            half = n >> g
            bit, dev = partner(order[g - 1], self.dp, self.sq)
            piece = self.gat.at[pl.ds(self.off[s][g], half)]
            return (self.remote(s, k, piece, piece, dev), None)
        piece = self.gat.at[pl.ds(here, n)]
        there = self.out.at[pl.ds(2 * base + self.cbit * half_units + first, n)]
        return (self.remote(s, k, piece, there, self.cdev),
                pltpu.make_async_copy(piece, there, self.local_sem.at[s, 1]))

    def start(self, s, k):
        for c in self.copies(s, k):
            if c is not None:
                c.start()

    def finish(self, s, k):
        phase, first, n, order, _ = self.streams[s]
        depth = len(order)
        remote, local = self.copies(s, k)
        remote.wait()
        if local is not None:
            local.wait()
        if k <= depth:
            half = n >> k
            if k == 0:
                off = self.off[s][0]
            else:
                bit, _ = partner(order[k - 1], self.dp, self.sq)
                off = self.off[s][k - 1] + bit * half
                self.off[s].append(off)
            self.add(off, self.roff[s][k], half, self.gat if k == depth else self.acc)

    def add(self, off, roff, n, to):
        acc, recv = self.acc, self.recv
        step = 4 if n % 4 == 0 else (3 if n % 3 == 0 else (2 if n % 2 == 0 else 1))

        def body(i, c):
            a = pl.ds(off + i * step, step)
            b = pl.ds(roff + i * step, step)
            to[a] = acc[a] + recv[b]
            return c

        lax.fori_loop(0, n // step, body, 0)

    def step(self, s, k):
        self.finish(s, k)
        if k + 1 < self.n_stages(s):
            self.start(s, k + 1)


class Small:
    def __init__(self, n_dp, n_seq, dp, sq, buf, ssend, srecv, small_z, small_out):
        self.dims = [("seq", j) for j in range(bits_of(n_seq))] + [("dp", j) for j in range(bits_of(n_dp))]
        self.nz = bits_of(n_seq)
        self.dp, self.sq, self.buf, self.ssend, self.srecv = dp, sq, buf, ssend, srecv
        self.small_z, self.small_out = small_z, small_out
        self.done = 0

    def copy(self, i):
        _, dev = partner(self.dims[i], self.dp, self.sq)
        return pltpu.make_async_remote_copy(
            src_ref=self.buf.at[2 * i], dst_ref=self.buf.at[2 * i + 1], send_sem=self.ssend.at[i],
            recv_sem=self.srecv.at[i], device_id=dev, device_id_type=MESH)

    def begin(self, value):
        self.buf[0] = value
        self.copy(0).start()

    def step(self):
        i = self.done
        if i == len(self.dims):
            return
        self.copy(i).wait()
        total = self.buf[2 * i] + self.buf[2 * i + 1]
        self.done = i + 1
        if self.done == self.nz:
            self.small_z[...] = total
        if self.done < len(self.dims):
            self.buf[2 * self.done] = total
            self.copy(self.done).start()
        else:
            self.small_out[...] = total

    def rest(self):
        while self.done < len(self.dims):
            self.step()


def entry_barrier(n_dp, n_seq, dp, sq, all_seq):
    barrier = pltpu.get_barrier_semaphore()
    peers = [partner(("dp", j), dp, sq)[1] for j in range(bits_of(n_dp))]
    if all_seq:
        peers += [(dp, (sq + d) % n_seq) for d in range(1, n_seq)]
    else:
        peers += [partner(("seq", j), dp, sq)[1] for j in range(bits_of(n_seq))]
    for dev in peers:
        pl.semaphore_signal(barrier, inc=1, device_id=dev, device_id_type=MESH)
    return barrier, len(peers)


def gelu_tanh(values):
    inner_arg = tanh_coef * (values + 0.044715 * values * values * values)
    return 0.5 * values * (1.0 + jnp.tanh(inner_arg))


def layer_norm(values, norm_gain, norm_shift):
    centre = jnp.mean(values, axis=-1, keepdims=True)
    spread = values - centre
    second = jnp.mean(spread * spread, axis=-1, keepdims=True)
    return spread * lax.rsqrt(second + norm_eps) * norm_gain + norm_shift


def matmul(former, latter):
    return jnp.dot(former, latter, preferred_element_type=jnp.float32)


def matmul_right_t(former, latter):
    return lax.dot_general(
        former, latter, (((1,), (1,)), ((), ())), preferred_element_type=jnp.float32
    )


def matmul_left_t(former, latter):
    return lax.dot_general(
        former, latter, (((0,), (0,)), ((), ())), preferred_element_type=jnp.float32
    )


def segment_ids(lengths, row_count):
    bounds = jnp.cumsum(lengths)[:-1]
    places = jnp.arange(row_count, dtype=jnp.int32)
    return jnp.sum((places[:, None] >= bounds[None, :]).astype(jnp.int32), axis=1)


def block_scores(query_block, key_heads, segments, valid_row, first_row, score_scale):
    block_rows = query_block.shape[0]
    total_rows = key_heads.shape[0]
    scores = (
        jnp.einsum("qhd,khd->hqk", query_block, key_heads, preferred_element_type=jnp.float32)
        * score_scale
    )
    row_index = first_row + jnp.arange(block_rows, dtype=jnp.int32)
    columns = jnp.arange(total_rows, dtype=jnp.int32)
    row_segments = lax.dynamic_slice_in_dim(segments, first_row, block_rows, 0)
    allowed = (row_segments[:, None] == segments[None, :]) & (
        columns[None, :] <= row_index[:, None]
    )
    allowed = allowed & ((valid_row[None, :] > 0) | (columns[None, :] == row_index[:, None]))
    return (jnp.where(allowed[None], scores, masked_score), allowed)


def attend_forward(
    query_heads, key_heads, value_heads, segments, valid_row, block_rows, score_scale
):
    total_rows = query_heads.shape[0]

    def one_block(block):
        first_row = block * block_rows
        query_block = lax.dynamic_slice_in_dim(query_heads, first_row, block_rows, 0)
        scores, allowed = block_scores(
            query_block, key_heads, segments, valid_row, first_row, score_scale
        )
        row_top = jnp.max(scores, axis=-1, keepdims=True)
        powered = jnp.where(allowed[None], jnp.exp(scores - row_top), 0.0)
        row_totals = jnp.sum(powered, axis=-1, keepdims=True)
        weights = (powered / row_totals).astype(jnp.bfloat16)
        mixed_block = jnp.einsum(
            "hqk,khd->qhd", weights, value_heads, preferred_element_type=jnp.float32
        )
        return (mixed_block.astype(jnp.bfloat16), (row_top + jnp.log(row_totals))[..., 0])

    mixed_blocks, log_totals = lax.map(
        one_block, jnp.arange(total_rows // block_rows, dtype=jnp.int32)
    )
    return (mixed_blocks.reshape(total_rows, -1), log_totals)


def attend_backward(
    query_heads,
    key_heads,
    value_heads,
    grad_heads,
    log_totals,
    segments,
    valid_row,
    block_rows,
    score_scale,
):
    total_rows = query_heads.shape[0]

    def one_block(carry, element):
        key_acc, value_acc = carry
        block, block_totals = element
        first_row = block * block_rows
        query_block = lax.dynamic_slice_in_dim(query_heads, first_row, block_rows, 0)
        grad_block = lax.dynamic_slice_in_dim(grad_heads, first_row, block_rows, 0)
        scores, allowed = block_scores(
            query_block, key_heads, segments, valid_row, first_row, score_scale
        )
        probs = jnp.where(allowed[None], jnp.exp(scores - block_totals[:, :, None]), 0.0)
        prob_grad = jnp.einsum(
            "qhd,khd->hqk", grad_block, value_heads, preferred_element_type=jnp.float32
        )
        centre = jnp.sum(probs * prob_grad, axis=-1, keepdims=True)
        score_grad = (probs * (prob_grad - centre)).astype(jnp.bfloat16)
        query_part = (
            jnp.einsum("hqk,khd->qhd", score_grad, key_heads, preferred_element_type=jnp.float32)
            * score_scale
        )
        key_acc = (
            key_acc
            + jnp.einsum(
                "hqk,qhd->khd", score_grad, query_block, preferred_element_type=jnp.float32
            )
            * score_scale
        )
        value_acc = value_acc + jnp.einsum(
            "hqk,qhd->khd",
            probs.astype(jnp.bfloat16),
            grad_block,
            preferred_element_type=jnp.float32,
        )
        return ((key_acc, value_acc), query_part.astype(jnp.bfloat16))

    zero_heads = jnp.zeros(key_heads.shape, jnp.float32)
    block_ids = jnp.arange(total_rows // block_rows, dtype=jnp.int32)
    (key_acc, value_acc), query_parts = lax.scan(
        one_block, (zero_heads, zero_heads), (block_ids, log_totals)
    )
    flat_shape = (total_rows, key_heads.shape[1] * key_heads.shape[2])
    return (
        query_parts.reshape(flat_shape),
        key_acc.astype(jnp.bfloat16).reshape(flat_shape),
        value_acc.astype(jnp.bfloat16).reshape(flat_shape),
    )


FCH = 768
GELU_A = 0.044715


def row_sum(v):
    return jnp.sum(v, axis=0, keepdims=True)


def mlp_kernel(steps, mixed, hidden, og, valid, proj_w, proj_b, n2g, n2s, fc_w, fc_b, out_w, out_b,
               output, mid_grad, mixed_grad, part, proj_part, small,
               nt_ref, xhat_ref, inv_ref, mid_ref, mlp_acc, two_acc):
    j = pl.program_id(0)

    @pl.when(j == 0)
    def _():
        x = hidden[...].astype(jnp.float32)
        attn = matmul(mixed[...], proj_w[...]) + proj_b[...]
        middle = x + attn
        mid_ref[...] = middle
        v = valid[...]
        spread = middle - jnp.mean(middle, axis=-1, keepdims=True)
        inv = lax.rsqrt(jnp.mean(spread * spread, axis=-1, keepdims=True) + norm_eps)
        xhat = spread * inv
        xhat_ref[...] = xhat
        inv_ref[...] = jnp.broadcast_to(inv, inv_ref.shape)
        nt_ref[...] = (xhat * n2g[...] + n2s[...]).astype(jnp.bfloat16)
        small[...] = jnp.zeros_like(small)
        s0 = row_sum(jnp.sum(x * x, axis=-1, keepdims=True) * v)
        s1 = row_sum(jnp.sum(attn * attn, axis=-1, keepdims=True) * v)
        s3 = row_sum(v)
        lane = lax.broadcasted_iota(jnp.int32, (1, WID), 1)
        small[12:13, :] = jnp.where(lane == 0, s0, jnp.where(lane == 1, s1, jnp.where(lane == 3, s3, 0.0)))
        small[7:8, :] = row_sum(og[...].astype(jnp.float32))

    nt = nt_ref[...]
    fw = fc_w[...]
    ow = out_w[...]
    g_low = og[...]
    pre = matmul(nt, fw) + fc_b[...]
    sq = pre * pre
    t = jnp.tanh(tanh_coef * (pre + GELU_A * sq * pre))
    act = (0.5 * pre * (1.0 + t)).astype(jnp.bfloat16)
    slope = 0.5 * (1.0 + t) + 0.5 * pre * (1.0 - t * t) * (tanh_coef * (1.0 + 3.0 * GELU_A * sq))
    pre_grad = matmul_right_t(g_low, ow) * slope
    fcb = row_sum(pre_grad)
    for i in range(steps):
        @pl.when(j == i)
        def _():
            small[8 + i : 9 + i, :] = fcb
    low = pre_grad.astype(jnp.bfloat16)
    part[0, 0] = matmul_left_t(act, g_low).astype(jnp.bfloat16)
    part[0, 1] = matmul_left_t(nt, low).astype(jnp.bfloat16)
    mlp = matmul(act, ow)
    two = matmul_right_t(low, fw)

    @pl.when(j == 0)
    def _():
        mlp_acc[...] = mlp
        two_acc[...] = two

    @pl.when(j > 0)
    def _():
        mlp_acc[...] = mlp_acc[...] + mlp
        two_acc[...] = two_acc[...] + two

    @pl.when(j == steps - 1)
    def _():
        mlp_out = mlp_acc[...] + out_b[...]
        output[...] = (mid_ref[...] + mlp_out).astype(jnp.bfloat16)
        s2 = row_sum(jnp.sum(mlp_out * mlp_out, axis=-1, keepdims=True) * valid[...])
        lane = lax.broadcasted_iota(jnp.int32, (1, WID), 1)
        small[12:13, :] = small[12:13, :] + jnp.where(lane == 2, s2, 0.0)
        two_grad = two_acc[...]
        xhat = xhat_ref[...]
        small[5:6, :] = row_sum(two_grad * xhat)
        small[6:7, :] = row_sum(two_grad)
        e = two_grad * n2g[...]
        centre = jnp.mean(e, axis=-1, keepdims=True)
        along = jnp.mean(e * xhat, axis=-1, keepdims=True)
        grad = og[...].astype(jnp.float32) + (e - centre - xhat * along) * inv_ref[:, 0:1]
        mid_grad[...] = grad
        small[4:5, :] = row_sum(grad)
        grad_low = grad.astype(jnp.bfloat16)
        mixed_grad[...] = matmul_right_t(grad_low, proj_w[...]).astype(jnp.bfloat16)
        proj_part[...] = matmul_left_t(mixed[...], grad_low).astype(jnp.bfloat16)


def mlp_block(mixed, hidden, og, valid_col, proj_w, proj_b, n2g, n2s, fc_w, fc_b, out_w, out_b):
    rows, d = hidden.shape
    ff = fc_w.shape[1]
    steps = ff // FCH
    whole = lambda shape: pl.BlockSpec(shape, lambda j: (0,) * len(shape))
    vec = lambda v: v.reshape(1, -1)
    f32, bf = jnp.float32, jnp.bfloat16
    return pl.pallas_call(
        functools.partial(mlp_kernel, steps),
        grid=(steps,),
        in_specs=[whole((rows, d)), whole((rows, d)), whole((rows, d)), whole((rows, 1)), whole((d, d)), whole((1, d)),
                  whole((1, d)), whole((1, d)), pl.BlockSpec((d, FCH), lambda j: (0, j)), pl.BlockSpec((1, FCH), lambda j: (0, j)),
                  pl.BlockSpec((FCH, d), lambda j: (j, 0)), whole((1, d))],
        out_specs=(whole((rows, d)), whole((rows, d)), whole((rows, d)), pl.BlockSpec((1, 2, FCH, d), lambda j: (j, 0, 0, 0)),
                   whole((d, d)), whole((16, d))),
        out_shape=(jax.ShapeDtypeStruct((rows, d), bf), jax.ShapeDtypeStruct((rows, d), f32), jax.ShapeDtypeStruct((rows, d), bf),
                   jax.ShapeDtypeStruct((steps, 2, FCH, d), bf), jax.ShapeDtypeStruct((d, d), bf), jax.ShapeDtypeStruct((16, d), f32)),
        scratch_shapes=[pltpu.VMEM((rows, d), bf), pltpu.VMEM((rows, d), f32), pltpu.VMEM((rows, 128), f32),
                        pltpu.VMEM((rows, d), f32), pltpu.VMEM((rows, d), f32), pltpu.VMEM((rows, d), f32)],
        compiler_params=pltpu.CompilerParams(vmem_limit_bytes=48 * 2**20, dimension_semantics=("arbitrary",)),
        name="mlp_block",
    )(mixed, hidden, og, valid_col, proj_w, vec(proj_b), vec(n2g), vec(n2s), fc_w, vec(fc_b), out_w, vec(out_b))


PIECE = 384


def widen_kernel(pieces, src, *refs):
    n_out = 6
    outs, (inbuf, stage, in_sem, out_sem) = refs[:n_out], refs[n_out:]
    depth = inbuf.shape[0]

    def fetch(i):
        return pltpu.make_async_copy(src.at[pl.ds(pieces[i][0], PIECE)], inbuf.at[i % depth], in_sem.at[i % depth])

    def put(i):
        slot = i % depth
        _, which, row, col, half = pieces[i]
        out = outs[which]
        if half:
            return [pltpu.make_async_copy(stage.at[slot, :, pl.ds(h * PIECE, PIECE)],
                                          out.at[pl.ds(h * PIECE, PIECE)], out_sem.at[slot, h]) for h in range(2)]
        return [pltpu.make_async_copy(stage.at[slot], out.at[pl.ds(row, PIECE), pl.ds(col, WID)], out_sem.at[slot, 0])]

    n = len(pieces)
    for i in range(min(depth, n)):
        fetch(i).start()
    for i in range(n):
        slot = i % depth
        fetch(i).wait()
        if i >= depth:
            for c in put(i - depth):
                c.wait()

        def body(r, c):
            rows = pl.ds(r * 32, 32)
            stage[slot, rows] = inbuf[slot, rows].astype(jnp.float32)
            return c

        lax.fori_loop(0, PIECE // 32, body, 0)
        for c in put(i):
            c.start()
        if i + depth < n:
            fetch(i + depth).start()
    for i in range(max(0, n - depth), n):
        for c in put(i):
            c.wait()


def widen(summed, row0, d, ff, vf):
    pieces = []
    for j in range(ff // FCH):
        for h in range(2):
            pieces.append((j * 2 * FCH + h * PIECE, 0, j * FCH + h * PIECE, 0, False))
        for h in range(2):
            pieces.append((j * 2 * FCH + FCH + h * PIECE, 1, h * PIECE, j * FCH, False))
    for w in range(3):
        for h in range(2):
            pieces.append((row0 + w * d + h * PIECE, 2 + w, h * PIECE, 0, False))
    pieces.append((row0 + 3 * d, 5, 0, 0, True))
    f32 = jnp.float32
    depth = 3
    hbm = pl.BlockSpec(memory_space=pl.ANY)
    shapes = [(ff, d), (d, ff), (d, d), (d, d), (d, d), (d, vf)]
    return pl.pallas_call(
        functools.partial(widen_kernel, pieces),
        in_specs=[hbm], out_specs=(hbm,) * 6, out_shape=tuple(jax.ShapeDtypeStruct(s, f32) for s in shapes),
        scratch_shapes=[pltpu.VMEM((depth, PIECE, WID), jnp.bfloat16), pltpu.VMEM((depth, PIECE, WID), f32),
                        pltpu.SemaphoreType.DMA((depth,)), pltpu.SemaphoreType.DMA((depth, 2))],
        compiler_params=pltpu.CompilerParams(vmem_limit_bytes=32 * 2**20),
        name="widen",
    )(summed)


def ar_kernel(cfg, part1, part2, small, out, small_z, small_out, acc, recv, gat, sbuf, send_sem, recv_sem, local_sem, ssend, srecv_sem):
    n_dp, n_seq, halves, streams, order = cfg
    dp, sq = lax.axis_index("dp"), lax.axis_index("seq")
    barrier, count = entry_barrier(n_dp, n_seq, dp, sq, False)
    pl.semaphore_wait(barrier, count)
    ex = Exchange(streams, halves, dp, sq, (part1, part2), out, acc, recv, gat, (send_sem, recv_sem, local_sem))
    tiny = Small(n_dp, n_seq, dp, sq, sbuf, ssend, srecv_sem, small_z, small_out)
    for s in range(len(streams)):
        ex.start(s, 0)
    tiny.begin(small[...])
    gap = max(1, len(order) // (len(tiny.dims) + 2))
    for idx, (_, s, k) in enumerate(order):
        ex.step(s, k)
        if idx % gap == gap - 1:
            tiny.step()
    tiny.rest()


def all_reduce(mesh, part1, part2, small, shares, collective_id):
    n_dp, n_seq = mesh.shape["dp"], mesh.shape["seq"]
    halves = (part1.shape[0] // 2, part2.shape[0] // 2)
    streams = plan_streams(n_dp, n_seq, list(zip(halves, shares)), (0.0, 0.0))
    order = schedule(streams)
    n_st = 2 * (bits_of(n_dp) + bits_of(n_seq))
    n_small = bits_of(n_dp) + bits_of(n_seq)
    vmem = pl.BlockSpec(memory_space=pltpu.VMEM)
    hbm = pl.BlockSpec(memory_space=pl.ANY)
    ns = len(streams)
    bf = jnp.bfloat16
    units = lambda n: pltpu.VMEM((n, SUB, WID), bf)
    sshape = jax.ShapeDtypeStruct(small.shape, small.dtype)
    return pl.pallas_call(
        functools.partial(ar_kernel, (n_dp, n_seq, halves, streams, order)),
        out_shape=(jax.ShapeDtypeStruct((2 * sum(halves), SUB, WID), bf), sshape, sshape),
        in_specs=[hbm, hbm, vmem], out_specs=(hbm, vmem, vmem),
        scratch_shapes=[
            units(sum(halves)), units(Exchange.recv_total(streams, halves)), units(sum(halves)),
            pltpu.VMEM((2 * n_small,) + small.shape, small.dtype),
            pltpu.SemaphoreType.DMA((ns, n_st)), pltpu.SemaphoreType.DMA((ns, n_st)), pltpu.SemaphoreType.DMA((ns, 2)),
            pltpu.SemaphoreType.DMA((n_small,)), pltpu.SemaphoreType.DMA((n_small,))],
        compiler_params=pltpu.CompilerParams(collective_id=collective_id, has_side_effects=True, vmem_limit_bytes=60 * 2**20),
        name="grad_all_reduce",
    )(part1, part2, small)


def local(
    mesh,
    hidden_in,
    skip_values,
    out_grad,
    doc_lens,
    valid,
    norm1_gain,
    norm1_shift,
    query_w,
    query_b,
    key_w,
    value_w,
    value_b,
    proj_w,
    proj_b,
    norm2_gain,
    norm2_shift,
    fc_w,
    fc_b,
    out_w,
    out_b,
):
    tok_rows = hidden_in.shape[0]
    seq_size = lax.axis_size("seq")
    seq_rank = lax.axis_index("seq")
    group_rows = tok_rows * seq_size
    heads_here = HEADS // seq_size
    block_rows = min(512, group_rows)
    score_scale = 1.0 / math.sqrt(HDIM)
    head_shape = (group_rows, heads_here, HDIM)
    segments = segment_ids(doc_lens[0], group_rows)
    hidden = hidden_in.astype(jnp.float32)
    normed, norm1_pull = jax.vjp(layer_norm, hidden, norm1_gain, norm1_shift)
    normed_low = normed.astype(jnp.bfloat16)
    fresh_values = (matmul(normed_low, value_w) + value_b).astype(jnp.bfloat16)
    value_rows = jnp.concatenate([fresh_values, skip_values], axis=1)
    query_rows = (matmul(normed_low, query_w) + query_b).astype(jnp.bfloat16)
    key_rows = matmul(normed_low, key_w).astype(jnp.bfloat16)
    query_heads, key_heads, value_heads = (
        lax.all_to_all(query_rows, "seq", split_axis=1, concat_axis=0, tiled=True),
        lax.all_to_all(key_rows, "seq", split_axis=1, concat_axis=0, tiled=True),
        lax.all_to_all(value_rows, "seq", split_axis=1, concat_axis=0, tiled=True),
    )
    query_split = query_heads.reshape(head_shape)
    key_split = key_heads.reshape(head_shape)
    value_split = value_heads.reshape(head_shape)
    mixed_heads, log_totals = attend_forward(
        query_split, key_split, value_split, segments, valid, block_rows, score_scale
    )
    mixed_rows = lax.all_to_all(mixed_heads, "seq", split_axis=0, concat_axis=1, tiled=True)
    valid_col = lax.dynamic_slice_in_dim(valid, seq_rank * tok_rows, tok_rows, 0).astype(jnp.float32)[:, None]
    output, middle_grad, mixed_grad, part, proj_part, small = mlp_block(
        mixed_rows, hidden_in, out_grad, valid_col, proj_w, proj_b, norm2_gain, norm2_shift, fc_w, fc_b, out_w, out_b
    )
    grad_heads = lax.all_to_all(mixed_grad, "seq", split_axis=1, concat_axis=0, tiled=True)
    query_grad, key_grad, value_grad = attend_backward(
        query_split,
        key_split,
        value_split,
        grad_heads.reshape(head_shape),
        log_totals,
        segments,
        valid,
        block_rows,
        score_scale,
    )
    query_grad_rows, key_grad_rows, value_grad_rows = (
        lax.all_to_all(query_grad, "seq", split_axis=0, concat_axis=1, tiled=True),
        lax.all_to_all(key_grad, "seq", split_axis=0, concat_axis=1, tiled=True),
        lax.all_to_all(value_grad, "seq", split_axis=0, concat_axis=1, tiled=True),
    )
    grad_query_w = matmul_left_t(normed_low, query_grad_rows)
    grad_key_w = matmul_left_t(normed_low, key_grad_rows)
    grad_query_b = jnp.sum(query_grad_rows.astype(jnp.float32), axis=0)
    normed_grad = matmul_right_t(query_grad_rows, query_w) + matmul_right_t(key_grad_rows, key_w)
    fresh_grad = value_grad_rows[:, :VFRESH]
    grad_skip = value_grad_rows[:, VFRESH:]
    grad_value_w = matmul_left_t(normed_low, fresh_grad)
    grad_value_b = jnp.sum(fresh_grad.astype(jnp.float32), axis=0)
    normed_grad = normed_grad + matmul_right_t(fresh_grad, value_w)
    hidden_part, grad_norm1_gain, grad_norm1_shift = norm1_pull(normed_grad)
    grad_input = (middle_grad + hidden_part).astype(jnp.bfloat16)
    n_dev = lax.axis_size("dp") * seq_size
    half = D // 2
    value_part = jnp.concatenate([grad_value_w[:half], grad_value_w[half:]], axis=1)
    low = jnp.bfloat16
    part2 = [proj_part, grad_query_w.astype(low), grad_key_w.astype(low), value_part.astype(low)]
    rows = sum(g.shape[0] for g in part2)
    quantum = n_dev * SUB
    padded = -(-rows // quantum) * quantum
    part2 = jnp.concatenate(part2 + [jnp.zeros((padded - rows, WID), low)]).reshape(-1, SUB, WID)
    part1 = part.reshape(-1, SUB, WID)
    head = jnp.stack([grad_norm1_gain, grad_norm1_shift, grad_query_b, jnp.pad(grad_value_b, (0, half))])
    small = small + jnp.pad(head, ((0, 12), (0, 0)))
    summed, small_z, small_all = all_reduce(mesh, part1, part2, small, SHARES, 0)
    row0 = part1.shape[0] * SUB
    grad_out_w, grad_fc_w, grad_proj_w, grad_query_w, grad_key_w, grad_value_w = widen(
        summed.reshape(-1, WID), row0, D, fc_w.shape[1], VFRESH
    )
    grad_norm1_gain, grad_norm1_shift, grad_query_b = small_all[0], small_all[1], small_all[2]
    grad_value_b = small_all[3, :VFRESH]
    grad_proj_b, grad_norm2_gain, grad_norm2_shift, grad_out_b = (small_all[i] for i in (4, 5, 6, 7))
    grad_fc_b = small_all[8:12].reshape(-1)
    sums = small_z[12, :4]
    norm_values = jnp.sqrt(sums[:3] / (sums[3] * D) + square_eps)[None, :]
    return (
        output,
        grad_input,
        grad_skip,
        grad_norm1_gain,
        grad_norm1_shift,
        grad_query_w,
        grad_query_b,
        grad_key_w,
        grad_value_w,
        grad_value_b,
        grad_proj_w,
        grad_proj_b,
        grad_norm2_gain,
        grad_norm2_shift,
        grad_fc_w,
        grad_fc_b,
        grad_out_w,
        grad_out_b,
        norm_values,
    )


def solution(mesh):
    placed = (
        P(("dp", "seq"), None),
        P(("dp", "seq"), None),
        P(("dp", "seq"), None),
        P("dp", None),
        P("dp"),
        P(),
        P(),
        P(),
        P(),
        P(),
        P(),
        P(),
        P(),
        P(),
        P(),
        P(),
        P(),
        P(),
        P(),
        P(),
    )
    return jax.shard_map(
        functools.partial(local, mesh),
        mesh=mesh,
        in_specs=placed,
        out_specs=(
            P(("dp", "seq"), None),
            P(("dp", "seq"), None),
            P(("dp", "seq"), None),
            P(),
            P(),
            P(),
            P(),
            P(),
            P(),
            P(),
            P(),
            P(),
            P(),
            P(),
            P(),
            P(),
            P(),
            P(),
            P("dp", None),
        ),
        check_vma=False,
    )
```

profile of v0, /device:TPU:0, one launch (start us, length us, event | category | flops | bytes accessed | tf_op | source)
XLA Modules:
  0.0 384.0 jit_solution(7859704318558144467)
XLA Ops:
  6.8 6.3 %all-to-all-start.2 = ((bf16[256,4,192]{0,2,1:T(8,128)(2,1)}), bf16[256,4,192]{0,2,1:T(8,128)(2,1)S(1)}, u32[]{:S(2)}, u32[]{:S(2)}) async-start(bf16[256,4,192]{0,2,1:T(8,128)(2,1)} %bitcast.10), calls=%async_computation.2 | async-start | bytes 786432 | tf_op jit(solution)/shard_map/all_to_all | solution.py:675
  15.4 9.5 %all-to-all-done.2 = bf16[256,4,192]{0,2,1:T(8,128)(2,1)S(1)} async-done(((bf16[256,4,192]{0,2,1:T(8,128)(2,1)}), bf16[256,4,192]{0,2,1:T(8,128)(2,1)S(1)}, u32[]{:S(2)}, u32[]{:S(2)}) %all-to-all-start.2) | async-done | bytes 393248 | tf_op jit(solution)/shard_map/all_to_all | solution.py:675
  24.9 3.5 all-to-all-start.1
  30.5 9.0 %all-to-all-done.1 = bf16[256,4,192]{0,2,1:T(8,128)(2,1)S(1)} async-done(((bf16[256,4,192]{0,2,1:T(8,128)(2,1)}), bf16[256,4,192]{0,2,1:T(8,128)(2,1)S(1)}, u32[]{:S(2)}, u32[]{:S(2)}) %all-to-all-start.1) | async-done | bytes 393248 | tf_op jit(solution)/shard_map/all_to_all | solution.py:674
  39.5 3.5 all-to-all-start
  46.6 7.6 %all-to-all-done = bf16[256,4,192]{0,2,1:T(8,128)(2,1)S(1)} async-done(((bf16[256,4,192]{0,2,1:T(8,128)(2,1)}), bf16[256,4,192]{0,2,1:T(8,128)(2,1)S(1)}, u32[]{:S(2)}, u32[]{:S(2)}) %all-to-all-start) | async-done | bytes 393248 | tf_op jit(solution)/shard_map/all_to_all | solution.py:673
  55.6 21.0 %while.27 = (s32[]{:T(128)}, bf16[2,512,3,64]{1,3,2,0:T(8,128)(2,1)S(1)}, f32[2,3,512]{2,1,0:T(4,128)S(1)}, s32[2]{0:T(128)S(1)}, s32[1024]{0:T(1024)S(1)}, /*in...) while((s32[]{:T(128)}, ...), condition=%wide.region_7.8_spmd, body=%wide.region_4.7_spmd.sunk | while | flops 427917312 | bytes 22231252 | solution.py:341
  62.6 3.5 fusion.111
  73.2 3.5 fusion.111
  79.8 3.6 all-to-all-start.3
  83.8 10.7 %all-to-all-done.3 = bf16[4,256,192]{1,2,0:T(8,128)(2,1)S(1)} async-done(((bf16[4,256,192]{1,2,0:T(8,128)(2,1)}), bf16[4,256,192]{1,2,0:T(8,128)(2,1)S(1)}, u32[]{:S(2)}, u32[]{:S(2)}) %all-to-all-start.3) | async-done | bytes 393248 | tf_op jit(solution)/shard_map/all_to_all | solution.py:683
  97.4 15.3 %mlp_block.1 = (bf16[256,768]{1,0:T(8,128)(2,1)}, f32[256,768]{1,0:T(8,128)S(1)}, bf16[256,768]{1,0:T(8,128)(2,1)S(1)}, bf16[4,2,768,768]{3,2,1,0:T(8,128)(2,1)}...) custom-call(bf16[256,768]{1,0:T(8,128)(2,1)S(1)} %copy.103.mixed, bf16[256,768]{1,0:T(8,128)(2,1)S(1)} %copy-done.1, ...), custom_call_target="tpu_custom_call" | custom-call | tf_op jit(solution)/shard_map/mlp_block/pallas_call | solution.py:501
  120.8 11.2 %all-to-all-done.4 = bf16[256,4,192]{0,2,1:T(8,128)(2,1)S(1)} async-done(((bf16[256,4,192]{0,2,1:T(8,128)(2,1)}), bf16[256,4,192]{0,2,1:T(8,128)(2,1)S(1)}, u32[]{:S(2)}, u32[]{:S(2)}) %all-to-all-start.4) | async-done | bytes 393248 | tf_op jit(solution)/shard_map/all_to_all | solution.py:688
  134.1 33.1 %while.28 = (s32[]{:T(128)}, f32[1024,3,64]{0,2,1:T(8,128)}, f32[1024,3,64]{0,2,1:T(8,128)}, bf16[2,512,3,64]{1,3,2,0:T(8,128)(2,1)}, s32[2]{0:T(128)S(1)}, /*in...) while((s32[]{:T(128)}, f32[1024,3,64]{0,2,1:T(8,128)}, ...), condition=%wide.region_10.11_spmd.clone, body=%wide.region_8.10_spmd.clone.sunk | while | flops 1026686976 | bytes 56740148 | solution.py:396
  138.4 4.0 %multiply_reduce_fusion.2 = (f32[3,512]{1,0:T(4,128)S(1)}, f32[3,512,1024]{2,1,0:T(8,128)S(1)}) fusion(f32[3,512,1024]{2,1,0:T(8,128)S(1)} %fusion.121, f32[3,512]{1,0:T(4,128)S(1)} %dynamic-slice_bitcast_fusion.2, bf16[1024,3,64]{0,2,1:T(8,128)(2,1)} %get-tuple-element.556, bf16[1024,3,64]{0,2,1:T(8,128)(2,1)} %get-tuple-element.553, ...), kind=kOutput, calls=%fused_computation.24.clone.1 | convolution fusion | flops 210762240 | bytes 13709316 | tf_op jit(solution)/shard_map/while/body/eval_jaxpr/qhd,khd->hqk/dot_general | solution.py:308
  154.7 4.0 %multiply_reduce_fusion.2 = (f32[3,512]{1,0:T(4,128)S(1)}, f32[3,512,1024]{2,1,0:T(8,128)S(1)}) fusion(f32[3,512,1024]{2,1,0:T(8,128)S(1)} %fusion.121, f32[3,512]{1,0:T(4,128)S(1)} %dynamic-slice_bitcast_fusion.2, bf16[1024,3,64]{0,2,1:T(8,128)(2,1)} %get-tuple-element.556, bf16[1024,3,64]{0,2,1:T(8,128)(2,1)} %get-tuple-element.553, ...), kind=kOutput, calls=%fused_computation.24.clone.1 | convolution fusion | flops 210762240 | bytes 13709316 | tf_op jit(solution)/shard_map/while/body/eval_jaxpr/qhd,khd->hqk/dot_general | solution.py:308
  171.3 3.6 all-to-all-start.7
  180.7 5.4 %all-to-all-done.7 = bf16[4,256,192]{1,2,0:T(8,128)(2,1)S(1)} async-done(((bf16[4,256,192]{1,2,0:T(8,128)(2,1)}), bf16[4,256,192]{1,2,0:T(8,128)(2,1)S(1)}, u32[]{:S(2)}, u32[]{:S(2)}) %all-to-all-start.7) | async-done | bytes 393248 | tf_op jit(solution)/shard_map/all_to_all | solution.py:703
  195.3 6.3 %all-to-all-done.5 = bf16[4,256,192]{1,2,0:T(8,128)(2,1)S(1)} async-done(((bf16[4,256,192]{1,2,0:T(8,128)(2,1)}), bf16[4,256,192]{1,2,0:T(8,128)(2,1)S(1)}, u32[]{:S(2)}, u32[]{:S(2)}) %all-to-all-start.5) | async-done | bytes 393248 | tf_op jit(solution)/shard_map/all_to_all | solution.py:701
  201.5 4.3 %all-to-all-start.6 = ((bf16[4,256,192]{1,2,0:T(8,128)(2,1)}), bf16[4,256,192]{1,2,0:T(8,128)(2,1)}, u32[]{:S(2)}, u32[]{:S(2)}) async-start(bf16[4,256,192]{1,2,0:T(8,128)(2,1)} %copy.109), calls=%async_computation.6 | async-start | bytes 786432 | tf_op jit(solution)/shard_map/all_to_all | solution.py:702
  207.8 9.2 %all-to-all-done.6 = bf16[4,256,192]{1,2,0:T(8,128)(2,1)} async-done(((bf16[4,256,192]{1,2,0:T(8,128)(2,1)}), bf16[4,256,192]{1,2,0:T(8,128)(2,1)}, u32[]{:S(2)}, u32[]{:S(2)}) %all-to-all-start.6) | async-done | bytes 393248 | tf_op jit(solution)/shard_map/all_to_all | solution.py:702
  227.7 131.9 %grad_all_reduce.1 = (bf16[576,16,768]{2,1,0:T(8,128)(2,1)}, f32[16,768]{1,0:T(8,128)}, f32[16,768]{1,0:T(8,128)}) custom-call(bf16[384,16,768]{2,1,0:T(8,128)(2,1)} %bitcast.121, bf16[192,16,768]{2,1,0:T(8,128)(2,1)} %bitcast.122, f32[16,768]{1,0:T(8,128)} %fusion.57.small), custom_call_target="tpu_custom_call" | custom-call | tf_op jit(solution)/shard_map/grad_all_reduce/pallas_call | solution.py:619
  368.0 5.0 %copy-done.2 = bf16[576,16,768]{2,1,0:T(8,128)(2,1)S(1)} copy-done((bf16[576,16,768]{2,1,0:T(8,128)(2,1)S(1)}, bf16[576,16,768]{2,1,0:T(8,128)(2,1)}, u32[]{:S(2)}) %copy-start.2) | copy-done | bytes 14155800
  373.1 9.9 %widen.1 = (f32[3072,768]{1,0:T(8,128)}, f32[768,3072]{1,0:T(8,128)}, f32[768,768]{1,0:T(8,128)}, f32[768,768]{1,0:T(8,128)}, f32[768,768]{1,0:T(8,128)}, /*index=5*/f32[768,384]{1,0:T(8,128)}) custom-call(bf16[9216,768]{1,0:T(8,128)(2,1)S(1)} %bitcast.119), custom_call_target="tpu_custom_call" | custom-call | tf_op jit(solution)/shard_map/widen/pallas_call | solution.py:578
  (190 shorter events, 108.5 us)
Async XLA Ops:
  0.7 27.7 %copy-start = (bf16[768,768]{1,0:T(8,128)(2,1)S(1)}, bf16[768,768]{1,0:T(8,128)(2,1)}, u32[]{:S(2)}) copy-start(bf16[768,768]{1,0:T(8,128)(2,1)} %param.31) | copy-start | bytes 3538948
  0.7 27.6 %copy-start.32 = (f32[768]{0:T(1024)S(1)}, f32[768]{0:T(1024)}, u32[]{:S(2)}) copy-start(f32[768]{0:T(1024)} %param.32) | copy-start | bytes 9220
  2.0 27.6 %copy-start.22 = (f32[256]{0:T(256)}, f32[256]{0:T(256)S(1)}, u32[]{:S(2)}) copy-start(f32[256]{0:T(256)S(1)} %broadcast_multiply_fusion) | copy-start | bytes 3076
  3.3 26.3 %copy-start.24 = (f32[256]{0:T(256)}, f32[256]{0:T(256)S(1)}, u32[]{:S(2)}) copy-start(f32[256]{0:T(256)S(1)} %fusion.59) | copy-start | bytes 3076
  6.8 18.0 %all-to-all-start.2 = ((bf16[256,4,192]{0,2,1:T(8,128)(2,1)}), bf16[256,4,192]{0,2,1:T(8,128)(2,1)S(1)}, u32[]{:S(2)}, u32[]{:S(2)}) async-start(bf16[256,4,192]{0,2,1:T(8,128)(2,1)} %bitcast.10), calls=%async_computation.2 | async-start | bytes 786432 | tf_op jit(solution)/shard_map/all_to_all | solution.py:675
  24.9 14.7 %all-to-all-start.1 = ((bf16[256,4,192]{0,2,1:T(8,128)(2,1)}), bf16[256,4,192]{0,2,1:T(8,128)(2,1)S(1)}, u32[]{:S(2)}, u32[]{:S(2)}) async-start(bf16[256,4,192]{0,2,1:T(8,128)(2,1)} %bitcast.8), calls=%async_computation.1 | async-start | bytes 786432 | tf_op jit(solution)/shard_map/all_to_all | solution.py:674
  28.4 27.2 %copy-start.19 = (s32[1024]{0:T(1024)S(1)}, s32[1024]{0:T(1024)}, u32[]{:S(2)}) copy-start(s32[1024]{0:T(1024)} %param.28) | copy-start | bytes 12292
  39.5 14.7 %all-to-all-start = ((bf16[256,4,192]{0,2,1:T(8,128)(2,1)}), bf16[256,4,192]{0,2,1:T(8,128)(2,1)S(1)}, u32[]{:S(2)}, u32[]{:S(2)}) async-start(bf16[256,4,192]{0,2,1:T(8,128)(2,1)} %bitcast.6), calls=%async_computation | async-start | bytes 786432 | tf_op jit(solution)/shard_map/all_to_all | solution.py:673
  55.6 27.9 %copy-start.28 = (f32[768]{0:T(1024)S(1)}, f32[768]{0:T(1024)}, u32[]{:S(2)}) copy-start(f32[768]{0:T(1024)} %param.37) | copy-start | bytes 9220
  55.6 27.9 %copy-start.29 = (f32[768]{0:T(1024)S(1)}, f32[768]{0:T(1024)}, u32[]{:S(2)}) copy-start(f32[768]{0:T(1024)} %param.38) | copy-start | bytes 9220
  55.6 27.9 %copy-start.30 = (f32[768]{0:T(1024)S(1)}, f32[768]{0:T(1024)}, u32[]{:S(2)}) copy-start(f32[768]{0:T(1024)} %param.39) | copy-start | bytes 9220
  55.6 27.9 %copy-start.31 = (f32[768]{0:T(1024)S(1)}, f32[768]{0:T(1024)}, u32[]{:S(2)}) copy-start(f32[768]{0:T(1024)} %param.43) | copy-start | bytes 9220
  55.6 40.8 %copy-start.10 = (f32[3072]{0:T(1024)S(1)}, f32[3072]{0:T(1024)}, u32[]{:S(2)}) copy-start(f32[3072]{0:T(1024)} %param.41) | copy-start | bytes 36868
  76.7 19.7 %copy-start.3 = (bf16[768,768]{1,0:T(8,128)(2,1)S(1)}, bf16[768,768]{1,0:T(8,128)(2,1)}, u32[]{:S(2)}) copy-start(bf16[768,768]{1,0:T(8,128)(2,1)} %proj_w.1) | copy-start | bytes 3538948
  79.8 14.7 %all-to-all-start.3 = ((bf16[4,256,192]{1,2,0:T(8,128)(2,1)}), bf16[4,256,192]{1,2,0:T(8,128)(2,1)S(1)}, u32[]{:S(2)}, u32[]{:S(2)}) async-start(bf16[4,256,192]{1,2,0:T(8,128)(2,1)} %copy.102), calls=%async_computation.3 | async-start | bytes 786432 | tf_op jit(solution)/shard_map/all_to_all | solution.py:683
  117.3 14.7 %all-to-all-start.4 = ((bf16[256,4,192]{0,2,1:T(8,128)(2,1)}), bf16[256,4,192]{0,2,1:T(8,128)(2,1)S(1)}, u32[]{:S(2)}, u32[]{:S(2)}) async-start(bf16[256,4,192]{0,2,1:T(8,128)(2,1)} %bitcast.16), calls=%async_computation.4 | async-start | bytes 786432 | tf_op jit(solution)/shard_map/all_to_all | solution.py:688
  167.2 23.2 %copy-start.5 = (bf16[768,768]{1,0:T(8,128)(2,1)S(1)}, bf16[768,768]{1,0:T(8,128)(2,1)}, u32[]{:S(2)}) copy-start(bf16[768,768]{1,0:T(8,128)(2,1)} %copy-done.4) | copy-start | bytes 3538948
  171.3 22.5 %copy-start.21 = (f32[768]{0:T(1024)S(1)}, f32[768]{0:T(1024)}, u32[]{:S(2)}) copy-start(f32[768]{0:T(1024)} %param.29) | copy-start | bytes 9220
  171.3 22.5 %copy-start.23 = (f32[256]{0:T(256)S(1)}, f32[256]{0:T(256)}, u32[]{:S(2)}) copy-start(f32[256]{0:T(256)} %copy-done.22) | copy-start | bytes 3076
  171.3 22.5 %copy-start.25 = (f32[256]{0:T(256)S(1)}, f32[256]{0:T(256)}, u32[]{:S(2)}) copy-start(f32[256]{0:T(256)} %copy-done.24) | copy-start | bytes 3076
  171.3 22.5 %copy-start.33 = (f32[768]{0:T(1024)S(1)}, f32[768]{0:T(1024)}, u32[]{:S(2)}) copy-start(f32[768]{0:T(1024)} %param.30) | copy-start | bytes 9220
  171.3 14.8 %all-to-all-start.7 = ((bf16[4,256,192]{1,2,0:T(8,128)(2,1)}), bf16[4,256,192]{1,2,0:T(8,128)(2,1)S(1)}, u32[]{:S(2)}, u32[]{:S(2)}) async-start(bf16[4,256,192]{1,2,0:T(8,128)(2,1)} %copy.110), calls=%async_computation.7 | async-start | bytes 786432 | tf_op jit(solution)/shard_map/all_to_all | solution.py:703
  186.9 14.7 %all-to-all-start.5 = ((bf16[4,256,192]{1,2,0:T(8,128)(2,1)}), bf16[4,256,192]{1,2,0:T(8,128)(2,1)S(1)}, u32[]{:S(2)}, u32[]{:S(2)}) async-start(bf16[4,256,192]{1,2,0:T(8,128)(2,1)} %copy.108), calls=%async_computation.5 | async-start | bytes 786432 | tf_op jit(solution)/shard_map/all_to_all | solution.py:701
  201.5 15.4 %all-to-all-start.6 = ((bf16[4,256,192]{1,2,0:T(8,128)(2,1)}), bf16[4,256,192]{1,2,0:T(8,128)(2,1)}, u32[]{:S(2)}, u32[]{:S(2)}) async-start(bf16[4,256,192]{1,2,0:T(8,128)(2,1)} %copy.109), calls=%async_computation.6 | async-start | bytes 786432 | tf_op jit(solution)/shard_map/all_to_all | solution.py:702
  (20 other events, 114.1 us)
where the time goes:
time: 386 us; the launch traced here: 384 us
  Pallas kernels  157 us (41%)
  waiting for transfers between devices  68.9 us (18%)
  matrix products  53.4 us (14%)
  local copies, waits for them, and re-layouts  46.5 us (12%)
  starting transfers between devices  31.7 us (8%)
  other arithmetic  21.7 us (6%)
    pallas_call x1, Pallas kernels, all_reduce(): pl.pallas_call(functools.partial(ar_kernel, (n_dp, n_seq, halves, streams...  132 us
    pallas_call x1, Pallas kernels, mlp_block(): pl.pallas_call(functools.partial(mlp_kernel, steps), grid=(steps,), in_sp...  15.3 us
    dot_general x4, matrix products, block_scores(): jnp.einsum('qhd,khd->hqk', query_block, key_heads, preferred_element_type...  12.9 us
    unnamed x66, local copies, waits for them, and re-layouts  12.2 us
    all_to_all x1, waiting for transfers between devices, local(): lax.all_to_all(mixed_grad, 'seq', split_axis=1, concat_axis=0, tiled=True)  11.2 us
    all_to_all x1, waiting for transfers between devices, local(): lax.all_to_all(mixed_heads, 'seq', split_axis=0, concat_axis=1, tiled=True)  10.7 us
    pallas_call x1, Pallas kernels, widen(): pl.pallas_call(functools.partial(widen_kernel, pieces), in_specs=[hbm], o...  9.91 us
    all_to_all x1, waiting for transfers between devices, local(): lax.all_to_all(value_rows, 'seq', split_axis=1, concat_axis=0, tiled=True)  9.51 us
  transfers between devices with their start and end apart: 8, of which 8 were waited for; matrix products, arithmetic and copies ran while one was open for 5% of the time, Pallas kernels for 0%

commit v1 on v0

--- a/solution.py
+++ b/solution.py
@@ -25,6 +25,8 @@
 WID = 768
 UNIT_BYTES = SUB * WID * 2
 SHARES = ("ababzababzab", "ababab")
+STARTS = (3.0, 50.0)
+MARKS = (8.0, 13.0, 16.0, 18.0, 19.0, 22.0, 25.0, 27.0, 28.0, 40.0, 50.0)
 
 
 def bits_of(n):
@@ -267,18 +269,6 @@
     return barrier, len(peers)
 
 
-def gelu_tanh(values):
-    inner_arg = tanh_coef * (values + 0.044715 * values * values * values)
-    return 0.5 * values * (1.0 + jnp.tanh(inner_arg))
-
-
-def layer_norm(values, norm_gain, norm_shift):
-    centre = jnp.mean(values, axis=-1, keepdims=True)
-    spread = values - centre
-    second = jnp.mean(spread * spread, axis=-1, keepdims=True)
-    return spread * lax.rsqrt(second + norm_eps) * norm_gain + norm_shift
-
-
 def matmul(former, latter):
     return jnp.dot(former, latter, preferred_element_type=jnp.float32)
 
@@ -292,115 +282,6 @@
 def matmul_left_t(former, latter):
     return lax.dot_general(
         former, latter, (((0,), (0,)), ((), ())), preferred_element_type=jnp.float32
-    )
-
-
-def segment_ids(lengths, row_count):
-    bounds = jnp.cumsum(lengths)[:-1]
-    places = jnp.arange(row_count, dtype=jnp.int32)
-    return jnp.sum((places[:, None] >= bounds[None, :]).astype(jnp.int32), axis=1)
-
-
-def block_scores(query_block, key_heads, segments, valid_row, first_row, score_scale):
-    block_rows = query_block.shape[0]
-    total_rows = key_heads.shape[0]
-    scores = (
-        jnp.einsum("qhd,khd->hqk", query_block, key_heads, preferred_element_type=jnp.float32)
-        * score_scale
-    )
-    row_index = first_row + jnp.arange(block_rows, dtype=jnp.int32)
-    columns = jnp.arange(total_rows, dtype=jnp.int32)
-    row_segments = lax.dynamic_slice_in_dim(segments, first_row, block_rows, 0)
-    allowed = (row_segments[:, None] == segments[None, :]) & (
-        columns[None, :] <= row_index[:, None]
-    )
-    allowed = allowed & ((valid_row[None, :] > 0) | (columns[None, :] == row_index[:, None]))
-    return (jnp.where(allowed[None], scores, masked_score), allowed)
-
-
-def attend_forward(
-    query_heads, key_heads, value_heads, segments, valid_row, block_rows, score_scale
-):
-    total_rows = query_heads.shape[0]
-
-    def one_block(block):
-        first_row = block * block_rows
-        query_block = lax.dynamic_slice_in_dim(query_heads, first_row, block_rows, 0)
-        scores, allowed = block_scores(
-            query_block, key_heads, segments, valid_row, first_row, score_scale
-        )
-        row_top = jnp.max(scores, axis=-1, keepdims=True)
-        powered = jnp.where(allowed[None], jnp.exp(scores - row_top), 0.0)
-        row_totals = jnp.sum(powered, axis=-1, keepdims=True)
-        weights = (powered / row_totals).astype(jnp.bfloat16)
-        mixed_block = jnp.einsum(
-            "hqk,khd->qhd", weights, value_heads, preferred_element_type=jnp.float32
-        )
-        return (mixed_block.astype(jnp.bfloat16), (row_top + jnp.log(row_totals))[..., 0])
-
-    mixed_blocks, log_totals = lax.map(
-        one_block, jnp.arange(total_rows // block_rows, dtype=jnp.int32)
-    )
-    return (mixed_blocks.reshape(total_rows, -1), log_totals)
-
-
-def attend_backward(
-    query_heads,
-    key_heads,
-    value_heads,
-    grad_heads,
-    log_totals,
-    segments,
-    valid_row,
-    block_rows,
-    score_scale,
-):
-    total_rows = query_heads.shape[0]
-
-    def one_block(carry, element):
-        key_acc, value_acc = carry
-        block, block_totals = element
-        first_row = block * block_rows
-        query_block = lax.dynamic_slice_in_dim(query_heads, first_row, block_rows, 0)
-        grad_block = lax.dynamic_slice_in_dim(grad_heads, first_row, block_rows, 0)
-        scores, allowed = block_scores(
-            query_block, key_heads, segments, valid_row, first_row, score_scale
-        )
-        probs = jnp.where(allowed[None], jnp.exp(scores - block_totals[:, :, None]), 0.0)
-        prob_grad = jnp.einsum(
-            "qhd,khd->hqk", grad_block, value_heads, preferred_element_type=jnp.float32
-        )
-        centre = jnp.sum(probs * prob_grad, axis=-1, keepdims=True)
-        score_grad = (probs * (prob_grad - centre)).astype(jnp.bfloat16)
-        query_part = (
-            jnp.einsum("hqk,khd->qhd", score_grad, key_heads, preferred_element_type=jnp.float32)
-            * score_scale
-        )
-        key_acc = (
-            key_acc
-            + jnp.einsum(
-                "hqk,qhd->khd", score_grad, query_block, preferred_element_type=jnp.float32
-            )
-            * score_scale
-        )
-        value_acc = value_acc + jnp.einsum(
-            "hqk,qhd->khd",
-            probs.astype(jnp.bfloat16),
-            grad_block,
-            preferred_element_type=jnp.float32,
-        )
-        return ((key_acc, value_acc), query_part.astype(jnp.bfloat16))
-
-    zero_heads = jnp.zeros(key_heads.shape, jnp.float32)
-    block_ids = jnp.arange(total_rows // block_rows, dtype=jnp.int32)
-    (key_acc, value_acc), query_parts = lax.scan(
-        one_block, (zero_heads, zero_heads), (block_ids, log_totals)
-    )
-    flat_shape = (total_rows, key_heads.shape[1] * key_heads.shape[2])
-    return (
-        query_parts.reshape(flat_shape),
-        key_acc.astype(jnp.bfloat16).reshape(flat_shape),
-        value_acc.astype(jnp.bfloat16).reshape(flat_shape),
     )
 
 
@@ -585,49 +466,439 @@
     )(summed)
 
 
-def ar_kernel(cfg, part1, part2, small, out, small_z, small_out, acc, recv, gat, sbuf, send_sem, recv_sem, local_sem, ssend, srecv_sem):
-    n_dp, n_seq, halves, streams, order = cfg
+LANES = 128
+PAIR_TILE = (0, 2, 3, 5)
+THIRD_TILE = (1, 1, 4, 4)
+
+
+def low_lanes():
+    return lax.broadcasted_iota(jnp.int32, (1, LANES), 1) < HDIM
+
+
+def turn(v):
+    return pltpu.roll(v, HDIM, 1)
+
+
+def pack_third(first, second, upper):
+    first, second = first.astype(jnp.float32), second.astype(jnp.float32)
+    if upper:
+        both = jnp.where(low_lanes(), turn(first), second)
+    else:
+        both = jnp.where(low_lanes(), first, turn(second))
+    return both.astype(jnp.bfloat16)
+
+
+def unpack_third(both):
+    wide = both.astype(jnp.float32)
+    low = low_lanes()
+    first = jnp.where(low, wide, 0.0).astype(jnp.bfloat16)
+    second = jnp.where(low, turn(wide), 0.0).astype(jnp.bfloat16)
+    return first, second
+
+
+def join_thirds(one, two):
+    one, two = one.astype(jnp.float32), two.astype(jnp.float32)
+    low = low_lanes()
+    first = jnp.where(low, one, turn(two)).astype(jnp.bfloat16)
+    second = jnp.where(low, turn(one), two).astype(jnp.bfloat16)
+    return first, second
+
+
+def split_tiles(tiles, pair_dst, third_dst, rows, n_seq):
+    half = rows // 2
+    for r in range(n_seq):
+        pair_dst(r, tiles[PAIR_TILE[r]])
+        t = tiles[THIRD_TILE[r]]
+        third_dst(r, pack_third(t[:half], t[half:], r % 2))
+
+
+def mask_bias(lens, valid_row, first, rows, cols):
+    one = lens[0, 0]
+    two = one + lens[0, 1]
+    i = first + lax.broadcasted_iota(jnp.int32, (rows, 1), 0)
+    j = lax.broadcasted_iota(jnp.int32, (1, cols), 1)
+    seg_i = (i >= one).astype(jnp.int32) + (i >= two).astype(jnp.int32)
+    seg_j = (j >= one).astype(jnp.int32) + (j >= two).astype(jnp.int32)
+    real = valid_row[:, 0:cols] > 0
+    code = jnp.where(real, seg_j, -1)
+    same = (code == seg_i) & (j <= i)
+    return jnp.where(same | (i == j), 0.0, masked_score)
+
+
+class Swap:
+    def __init__(self, n_seq, dp, sq, send, recv, ssem, rsem):
+        self.n_seq, self.dp, self.sq = n_seq, dp, sq
+        self.send, self.recv, self.ssem, self.rsem = send, recv, ssem, rsem
+
+    def copy(self, d):
+        to = (self.sq + d) % self.n_seq
+        return pltpu.make_async_remote_copy(
+            src_ref=self.send(to), dst_ref=self.recv(self.sq), send_sem=self.ssem(d), recv_sem=self.rsem(d),
+            device_id=(self.dp, to), device_id_type=MESH)
+
+    def start(self):
+        for d in range(1, self.n_seq):
+            self.copy(d).start()
+
+    def wait(self):
+        for d in range(1, self.n_seq):
+            self.copy(d).wait()
+
+
+class Gather:
+    def __init__(self, n_seq, dp, sq, send, recv, ssem, rsem):
+        self.n_seq, self.dp, self.sq = n_seq, dp, sq
+        self.send, self.recv, self.ssem, self.rsem = send, recv, ssem, rsem
+
+    def copy(self, to, slot):
+        return pltpu.make_async_remote_copy(
+            src_ref=self.send(to), dst_ref=self.recv(slot), send_sem=self.ssem(to), recv_sem=self.rsem(slot),
+            device_id=(self.dp, to), device_id_type=MESH)
+
+    def start(self, to):
+        @pl.when(self.sq != to)
+        def _():
+            self.copy(to, self.sq).start()
+
+    def wait(self):
+        for i in range(self.n_seq):
+            @pl.when(self.sq != i)
+            def _():
+                self.copy(i, i).wait()
+
+
+def front_kernel(cfg, lens, hidden, skip, valid_row, n1g, n1s, qw, qb, kw, vw, vb,
+                 normed_out, mixed_out, pair_out, third_out, lse_out,
+                 sp, st, rp, rt, smp, smt, rmp, rmt, bias, ssem, rsem, mssem, mrsem):
+    n_dp, n_seq = cfg
     dp, sq = lax.axis_index("dp"), lax.axis_index("seq")
-    barrier, count = entry_barrier(n_dp, n_seq, dp, sq, False)
+    rows = hidden.shape[0]
+    half = rows // 2
+    barrier = pltpu.get_barrier_semaphore()
+    for d in range(1, n_seq):
+        pl.semaphore_signal(barrier, inc=1, device_id=(dp, (sq + d) % n_seq), device_id_type=MESH)
+    x = hidden[...].astype(jnp.float32)
+    spread = x - jnp.mean(x, axis=-1, keepdims=True)
+    inv = lax.rsqrt(jnp.mean(spread * spread, axis=-1, keepdims=True) + norm_eps)
+    normed = (spread * inv * n1g[...] + n1s[...]).astype(jnp.bfloat16)
+    normed_out[...] = normed
+    swaps = [[Swap(n_seq, dp, sq, lambda to, t=t: sp.at[to, t], lambda me, t=t: rp.at[t, pl.ds(me * rows, rows)],
+                   lambda d, t=t: ssem.at[0, t, d], lambda d, t=t: rsem.at[0, t, d]),
+              Swap(n_seq, dp, sq, lambda to, t=t: st.at[to, t], lambda me, t=t: rt.at[t, me],
+                   lambda d, t=t: ssem.at[1, t, d], lambda d, t=t: rsem.at[1, t, d])] for t in range(3)]
+    first = True
+    for t in range(3):
+        if t == 0:
+            full = (matmul(normed, qw[...]) + qb[...]).astype(jnp.bfloat16)
+        elif t == 1:
+            full = matmul(normed, kw[...]).astype(jnp.bfloat16)
+        else:
+            full = (matmul(normed, vw[...]) + vb[...]).astype(jnp.bfloat16)
+        tiles = [full[:, c * LANES : (c + 1) * LANES] for c in range(full.shape[1] // LANES)]
+        if t == 2:
+            tiles += [skip[:, c * LANES : (c + 1) * LANES] for c in range(skip.shape[1] // LANES)]
+
+        def pair_dst(r, v):
+            sp[r, t] = v
+
+        def third_dst(r, v):
+            st[r, t] = v
+
+        split_tiles(tiles, pair_dst, third_dst, rows, n_seq)
+        if first:
+            pl.semaphore_wait(barrier, n_seq - 1)
+            first = False
+        swaps[t][0].start()
+    for t in range(3):
+        swaps[t][1].start()
+        rp[t, pl.ds(pl.multiple_of(sq * rows, rows), rows)] = sp[sq, t]
+        rt[t, sq] = st[sq, t]
+    for i in range(n_seq):
+        cols = (i + 1) * rows
+        bias[i * rows : (i + 1) * rows, 0:cols] = mask_bias(lens, valid_row, i * rows, rows, cols)
+    back = [Gather(n_seq, dp, sq, lambda to: smp.at[to], lambda s: rmp.at[s], lambda i: mssem.at[0, i], lambda i: mrsem.at[0, i]),
+            Gather(n_seq, dp, sq, lambda to: smt.at[to], lambda s: rmt.at[s], lambda i: mssem.at[1, i], lambda i: mrsem.at[1, i])]
+    low = low_lanes()
+    scale = 1.0 / math.sqrt(HDIM)
+    keep = (jnp.where(low, scale, 0.0).astype(jnp.bfloat16), jnp.where(low, 0.0, scale).astype(jnp.bfloat16))
+
+    def attend(q, k, v, block):
+        scores = matmul_right_t(q, k) + block
+        top = jnp.max(scores, axis=-1, keepdims=True)
+        powered = jnp.exp(scores - top)
+        total = jnp.sum(powered, axis=-1, keepdims=True)
+        probs = (powered * (1.0 / total)).astype(jnp.bfloat16)
+        return matmul(probs, v), top + jnp.log(total)
+
+    for t in range(3):
+        swaps[t][0].wait()
+    lane = lax.broadcasted_iota(jnp.int32, (1, LANES), 1)
+    for i in range(n_seq):
+        here = slice(i * rows, (i + 1) * rows)
+        cols = (i + 1) * rows
+        block = bias[here, 0:cols]
+        q, k, v = rp[0, here], rp[1, 0:cols], rp[2, 0:cols]
+        o0, l0 = attend(q * keep[0], k, v, block)
+        o1, l1 = attend(q * keep[1], k, v, block)
+        smp[i] = jnp.where(low, o0, o1).astype(jnp.bfloat16)
+        lse_out[here] = jnp.where(lane == 0, l0, l1)
+        back[0].start(i)
+    for t in range(3):
+        swaps[t][1].wait()
+        for s in range(n_seq):
+            a, b = unpack_third(rt[t, s])
+            third_out[t, s * rows : s * rows + half] = a
+            third_out[t, s * rows + half : (s + 1) * rows] = b
+    for i in range(n_seq):
+        here = slice(i * rows, (i + 1) * rows)
+        cols = (i + 1) * rows
+        block = bias[here, 0:cols]
+        o2, l2 = attend(third_out[0, here] * keep[0], third_out[1, 0:cols], third_out[2, 0:cols], block)
+        smt[i] = pack_third(o2[:half], o2[half:], False)
+        lse_out[here] = jnp.where(lane == 2, l2, lse_out[here])
+        back[1].start(i)
+    pair_out[...] = rp[...]
+    rmp[sq] = smp[sq]
+    rmt[sq] = smt[sq]
+    back[0].wait()
+    back[1].wait()
+    for r in range(n_seq):
+        c = PAIR_TILE[r] * LANES
+        mixed_out[:, c : c + LANES] = rmp[r]
+    for r in range(0, n_seq, 2):
+        a, b = join_thirds(rmt[r], rmt[r + 1])
+        c = THIRD_TILE[r] * LANES
+        mixed_out[0:half, c : c + LANES] = a
+        mixed_out[half:rows, c : c + LANES] = b
+
+
+def front(mesh, hidden, skip, lens, valid, n1g, n1s, qw, qb, kw, vw, vb, collective_id):
+    n_dp, n_seq = mesh.shape["dp"], mesh.shape["seq"]
+    rows, d = hidden.shape
+    group = rows * n_seq
+    bf, f32 = jnp.bfloat16, jnp.float32
+    vec = lambda v: v.reshape(1, -1)
+    vmem = pl.BlockSpec(memory_space=pltpu.VMEM)
+    half = rows // 2
+    dma = pltpu.SemaphoreType.DMA
+    return pl.pallas_call(
+        functools.partial(front_kernel, (n_dp, n_seq)),
+        in_specs=[pl.BlockSpec(memory_space=pltpu.SMEM)] + [vmem] * 10,
+        out_specs=(vmem,) * 5,
+        out_shape=(jax.ShapeDtypeStruct((rows, d), bf), jax.ShapeDtypeStruct((rows, d), bf),
+                   jax.ShapeDtypeStruct((3, group, LANES), bf), jax.ShapeDtypeStruct((3, group, LANES), bf),
+                   jax.ShapeDtypeStruct((group, LANES), f32)),
+        scratch_shapes=[
+            pltpu.VMEM((n_seq, 3, rows, LANES), bf), pltpu.VMEM((n_seq, 3, half, LANES), bf),
+            pltpu.VMEM((3, group, LANES), bf), pltpu.VMEM((3, n_seq, half, LANES), bf),
+            pltpu.VMEM((n_seq, rows, LANES), bf), pltpu.VMEM((n_seq, half, LANES), bf),
+            pltpu.VMEM((n_seq, rows, LANES), bf), pltpu.VMEM((n_seq, half, LANES), bf),
+            pltpu.VMEM((group, group), f32),
+            dma((2, 3, n_seq)), dma((2, 3, n_seq)), dma((2, n_seq)), dma((2, n_seq))],
+        compiler_params=pltpu.CompilerParams(collective_id=collective_id, has_side_effects=True, vmem_limit_bytes=56 * 2**20),
+        name="front",
+    )(lens, hidden, skip, vec(valid), vec(n1g), vec(n1s), qw, vec(qb), kw, vw, vec(vb))
+
+
+def back_kernel(cfg, lens, valid_row, mixed_grad, pair, third, lse, normed, hidden, n1g, mid_grad, qw, kw, vw, proj_part, small, part1,
+                out, grad_input, grad_skip, small_z, small_out,
+                gs, gst, gp, gt, gthird, bias, dk_acc, dv_acc, dsp, dst, drp, drt, rows_in, part2,
+                acc, recv, gat, sbuf, gssem, grsem, dssem, drsem, send_sem, recv_sem, local_sem, ssend, srecv_sem):
+    n_dp, n_seq, halves, streams, order, marks = cfg
+    dp, sq = lax.axis_index("dp"), lax.axis_index("seq")
+    rows, d = hidden.shape
+    half = rows // 2
+    bf, f32 = jnp.bfloat16, jnp.float32
+    barrier, count = entry_barrier(n_dp, n_seq, dp, sq, True)
+    full = mixed_grad[...]
+    tiles = [full[:, c * LANES : (c + 1) * LANES] for c in range(d // LANES)]
+
+    def pair_dst(r, v):
+        gs[r] = v
+
+    def third_dst(r, v):
+        gst[r] = v
+
+    split_tiles(tiles, pair_dst, third_dst, rows, n_seq)
     pl.semaphore_wait(barrier, count)
+    swap_pair = Swap(n_seq, dp, sq, lambda to: gs.at[to], lambda me: gp.at[pl.ds(me * rows, rows)], lambda i: gssem.at[0, i], lambda i: grsem.at[0, i])
+    swap_third = Swap(n_seq, dp, sq, lambda to: gst.at[to], lambda me: gt.at[me], lambda i: gssem.at[1, i], lambda i: grsem.at[1, i])
+    swap_pair.start()
+    swap_third.start()
     ex = Exchange(streams, halves, dp, sq, (part1, part2), out, acc, recv, gat, (send_sem, recv_sem, local_sem))
     tiny = Small(n_dp, n_seq, dp, sq, sbuf, ssend, srecv_sem, small_z, small_out)
-    for s in range(len(streams)):
-        ex.start(s, 0)
-    tiny.begin(small[...])
-    gap = max(1, len(order) // (len(tiny.dims) + 2))
-    for idx, (_, s, k) in enumerate(order):
+    for s, st in enumerate(streams):
+        if st[0] == 0:
+            ex.start(s, 0)
+    todo = list(order)
+
+    def advance(upto):
+        while todo and todo[0][0] <= upto:
+            _, s, k = todo.pop(0)
+            ex.step(s, k)
+
+    gp[pl.ds(pl.multiple_of(sq * rows, rows), rows)] = gs[sq]
+    gt[sq] = gst[sq]
+    for i in range(n_seq):
+        cols = (i + 1) * rows
+        bias[i * rows : (i + 1) * rows, 0:cols] = mask_bias(lens, valid_row, i * rows, rows, cols)
+    units_d = d // SUB
+    part2[0:units_d] = proj_part[...].reshape(units_d, SUB, WID)
+    send = [Gather(n_seq, dp, sq, lambda to: dsp.at[to], lambda s: drp.at[s], lambda i: dssem.at[0, i], lambda i: drsem.at[0, i]),
+            Gather(n_seq, dp, sq, lambda to: dst.at[to], lambda s: drt.at[s], lambda i: dssem.at[1, i], lambda i: drsem.at[1, i])]
+    low = low_lanes()
+    scale = 1.0 / math.sqrt(HDIM)
+    keep = (jnp.where(low, scale, 0.0).astype(bf), jnp.where(low, 0.0, scale).astype(bf))
+    ones = (jnp.where(low, 1.0, 0.0).astype(bf), jnp.where(low, 0.0, 1.0).astype(bf))
+
+    def backward(q, k, v, g, block, total):
+        probs = jnp.exp(matmul_right_t(q, k) + block - total)
+        prob_grad = matmul_right_t(g, v)
+        centre = jnp.sum(probs * prob_grad, axis=-1, keepdims=True)
+        score_grad = (probs * (prob_grad - centre)).astype(bf)
+        return matmul(score_grad, k), matmul_left_t(score_grad, q), matmul_left_t(probs.astype(bf), g)
+
+    mark = iter(marks)
+    advance(next(mark))
+    swap_pair.wait()
+    for i in reversed(range(n_seq)):
+        here = slice(i * rows, (i + 1) * rows)
+        cols = (i + 1) * rows
+        block = bias[here, 0:cols]
+        q, k, v, g = pair[0, here], pair[1, 0:cols], pair[2, 0:cols], gp[here]
+        dq0, dk0, dv0 = backward(q * keep[0], k, v, g * ones[0], block, lse[here, 0:1])
+        dq1, dk1, dv1 = backward(q * keep[1], k, v, g * ones[1], block, lse[here, 1:2])
+        if i == n_seq - 1:
+            dk_acc[...] = dk0 + dk1
+            dv_acc[...] = dv0 + dv1
+        else:
+            dk_acc[0:cols] = dk_acc[0:cols] + (dk0 + dk1)
+            dv_acc[0:cols] = dv_acc[0:cols] + (dv0 + dv1)
+        dsp[i, 0] = (jnp.where(low, dq0, dq1) * scale).astype(bf)
+        dsp[i, 1] = dk_acc[here].astype(bf)
+        dsp[i, 2] = dv_acc[here].astype(bf)
+        send[0].start(i)
+        advance(next(mark))
+    swap_third.wait()
+    for s in range(n_seq):
+        a, b = unpack_third(gt[s])
+        gthird[s * rows : s * rows + half] = a
+        gthird[s * rows + half : (s + 1) * rows] = b
+    for i in reversed(range(n_seq)):
+        here = slice(i * rows, (i + 1) * rows)
+        cols = (i + 1) * rows
+        block = bias[here, 0:cols]
+        dq, dk, dv = backward(third[0, here] * keep[0], third[1, 0:cols], third[2, 0:cols], gthird[here], block, lse[here, 2:3])
+        if i == n_seq - 1:
+            dk_acc[...] = dk
+            dv_acc[...] = dv
+        else:
+            dk_acc[0:cols] = dk_acc[0:cols] + dk
+            dv_acc[0:cols] = dv_acc[0:cols] + dv
+        dq = dq * scale
+        dst[i, 0] = pack_third(dq[:half], dq[half:], False)
+        for t, a in ((1, dk_acc), (2, dv_acc)):
+            dst[i, t] = pack_third(a[i * rows : i * rows + half], a[i * rows + half : (i + 1) * rows], False)
+        send[1].start(i)
+        advance(next(mark))
+    drp[sq] = dsp[sq]
+    drt[sq] = dst[sq]
+    x = hidden[...].astype(f32)
+    spread = x - jnp.mean(x, axis=-1, keepdims=True)
+    inv = lax.rsqrt(jnp.mean(spread * spread, axis=-1, keepdims=True) + norm_eps)
+    xhat = spread * inv
+    send[0].wait()
+    advance(next(mark))
+    send[1].wait()
+    for t in range(3):
+        for r in range(n_seq):
+            c = PAIR_TILE[r] * LANES
+            rows_in[t, :, c : c + LANES] = drp[r, t]
+        for r in range(0, n_seq, 2):
+            a, b = join_thirds(drt[r, t], drt[r + 1, t])
+            c = THIRD_TILE[r] * LANES
+            rows_in[t, 0:half, c : c + LANES] = a
+            rows_in[t, half:rows, c : c + LANES] = b
+    nl = normed[...]
+    dq, dk, dv = rows_in[0], rows_in[1], rows_in[2]
+    fresh = dv[:, 0:VFRESH]
+    grad_skip[...] = dv[:, VFRESH:]
+    part2[units_d : 2 * units_d] = matmul_left_t(nl, dq).astype(bf).reshape(units_d, SUB, WID)
+    part2[2 * units_d : 3 * units_d] = matmul_left_t(nl, dk).astype(bf).reshape(units_d, SUB, WID)
+    gv = matmul_left_t(nl, fresh).astype(bf)
+    uv = d // 2 // SUB
+    part2[3 * units_d : 3 * units_d + uv, :, 0:VFRESH] = gv[: d // 2].reshape(uv, SUB, VFRESH)
+    part2[3 * units_d : 3 * units_d + uv, :, VFRESH:] = gv[d // 2 :].reshape(uv, SUB, VFRESH)
+    extra = 2 * halves[1] - 3 * units_d - uv
+    if extra:
+        part2[3 * units_d + uv :] = jnp.zeros((extra, SUB, WID), bf)
+    for s, st in enumerate(streams):
+        if st[0] == 1:
+            ex.start(s, 0)
+    advance(next(mark))
+    normed_grad = matmul_right_t(dq, qw[...]) + matmul_right_t(dk, kw[...]) + matmul_right_t(fresh, vw[...])
+    f = normed_grad * n1g[...]
+    centre = jnp.mean(f, axis=-1, keepdims=True)
+    along = jnp.mean(f * xhat, axis=-1, keepdims=True)
+    grad_input[...] = (mid_grad[...] + (f - centre - xhat * along) * inv).astype(bf)
+    sbuf[0] = small[...]
+    sbuf[0, 0:1] = row_sum(normed_grad * xhat)
+    sbuf[0, 1:2] = row_sum(normed_grad)
+    sbuf[0, 2:3] = row_sum(dq.astype(f32))
+    sbuf[0, 3:4, 0:VFRESH] = row_sum(fresh.astype(f32))
+    tiny.copy(0).start()
+    gap = max(1, len(todo) // (len(tiny.dims) + 2))
+    left = 0
+    while todo:
+        _, s, k = todo.pop(0)
         ex.step(s, k)
-        if idx % gap == gap - 1:
+        left += 1
+        if left % gap == 0:
             tiny.step()
     tiny.rest()
 
 
-def all_reduce(mesh, part1, part2, small, shares, collective_id):
+def back(mesh, lens, valid, mixed_grad, pair, third, lse, normed, hidden, n1g, mid_grad, qw, kw, vw, proj_part, small, part1, collective_id):
     n_dp, n_seq = mesh.shape["dp"], mesh.shape["seq"]
-    halves = (part1.shape[0] // 2, part2.shape[0] // 2)
-    streams = plan_streams(n_dp, n_seq, list(zip(halves, shares)), (0.0, 0.0))
-    order = schedule(streams)
+    rows, d = hidden.shape
+    group = rows * n_seq
+    half = rows // 2
+    bf, f32 = jnp.bfloat16, jnp.float32
+    quantum = n_dp * n_seq
+    rows2 = 3 * d + d // 2
+    units2 = -(-rows2 // SUB // quantum) * quantum
+    halves = (part1.shape[0] // 2, units2 // 2)
+    streams = plan_streams(n_dp, n_seq, list(zip(halves, SHARES)), STARTS)
+    order = schedule(streams, (("seq", 9.0),))
     n_st = 2 * (bits_of(n_dp) + bits_of(n_seq))
     n_small = bits_of(n_dp) + bits_of(n_seq)
+    ns = len(streams)
     vmem = pl.BlockSpec(memory_space=pltpu.VMEM)
     hbm = pl.BlockSpec(memory_space=pl.ANY)
-    ns = len(streams)
-    bf = jnp.bfloat16
+    dma = pltpu.SemaphoreType.DMA
     units = lambda n: pltpu.VMEM((n, SUB, WID), bf)
-    sshape = jax.ShapeDtypeStruct(small.shape, small.dtype)
+    sshape = jax.ShapeDtypeStruct(small.shape, f32)
     return pl.pallas_call(
-        functools.partial(ar_kernel, (n_dp, n_seq, halves, streams, order)),
-        out_shape=(jax.ShapeDtypeStruct((2 * sum(halves), SUB, WID), bf), sshape, sshape),
-        in_specs=[hbm, hbm, vmem], out_specs=(hbm, vmem, vmem),
+        functools.partial(back_kernel, (n_dp, n_seq, halves, streams, order, MARKS)),
+        in_specs=[pl.BlockSpec(memory_space=pltpu.SMEM)] + [vmem] * 14 + [hbm],
+        out_specs=(hbm, vmem, vmem, vmem, vmem),
+        out_shape=(jax.ShapeDtypeStruct((2 * sum(halves), SUB, WID), bf), jax.ShapeDtypeStruct((rows, d), bf),
+                   jax.ShapeDtypeStruct((rows, d - VFRESH), bf), sshape, sshape),
         scratch_shapes=[
+            pltpu.VMEM((n_seq, rows, LANES), bf), pltpu.VMEM((n_seq, half, LANES), bf),
+            pltpu.VMEM((group, LANES), bf), pltpu.VMEM((n_seq, half, LANES), bf), pltpu.VMEM((group, LANES), bf),
+            pltpu.VMEM((group, group), f32), pltpu.VMEM((group, LANES), f32), pltpu.VMEM((group, LANES), f32),
+            pltpu.VMEM((n_seq, 3, rows, LANES), bf), pltpu.VMEM((n_seq, 3, half, LANES), bf),
+            pltpu.VMEM((n_seq, 3, rows, LANES), bf), pltpu.VMEM((n_seq, 3, half, LANES), bf),
+            pltpu.VMEM((3, rows, d), bf), units(units2),
             units(sum(halves)), units(Exchange.recv_total(streams, halves)), units(sum(halves)),
-            pltpu.VMEM((2 * n_small,) + small.shape, small.dtype),
-            pltpu.SemaphoreType.DMA((ns, n_st)), pltpu.SemaphoreType.DMA((ns, n_st)), pltpu.SemaphoreType.DMA((ns, 2)),
-            pltpu.SemaphoreType.DMA((n_small,)), pltpu.SemaphoreType.DMA((n_small,))],
-        compiler_params=pltpu.CompilerParams(collective_id=collective_id, has_side_effects=True, vmem_limit_bytes=60 * 2**20),
-        name="grad_all_reduce",
-    )(part1, part2, small)
+            pltpu.VMEM((2 * n_small,) + small.shape, f32),
+            dma((2, n_seq)), dma((2, n_seq)), dma((2, n_seq)), dma((2, n_seq)),
+            dma((ns, n_st)), dma((ns, n_st)), dma((ns, 2)), dma((n_small,)), dma((n_small,))],
+        compiler_params=pltpu.CompilerParams(collective_id=collective_id, has_side_effects=True, vmem_limit_bytes=63 * 2**20),
+        name="back",
+    )(lens, valid.reshape(1, -1), mixed_grad, pair, third, lse, normed, hidden, n1g.reshape(1, -1), mid_grad, qw, kw, vw, proj_part,
+      small, part1)
 
 
 def local(
@@ -653,79 +924,21 @@
     out_w,
     out_b,
 ):
-    tok_rows = hidden_in.shape[0]
     seq_size = lax.axis_size("seq")
     seq_rank = lax.axis_index("seq")
-    group_rows = tok_rows * seq_size
-    heads_here = HEADS // seq_size
-    block_rows = min(512, group_rows)
-    score_scale = 1.0 / math.sqrt(HDIM)
-    head_shape = (group_rows, heads_here, HDIM)
-    segments = segment_ids(doc_lens[0], group_rows)
-    hidden = hidden_in.astype(jnp.float32)
-    normed, norm1_pull = jax.vjp(layer_norm, hidden, norm1_gain, norm1_shift)
-    normed_low = normed.astype(jnp.bfloat16)
-    fresh_values = (matmul(normed_low, value_w) + value_b).astype(jnp.bfloat16)
-    value_rows = jnp.concatenate([fresh_values, skip_values], axis=1)
-    query_rows = (matmul(normed_low, query_w) + query_b).astype(jnp.bfloat16)
-    key_rows = matmul(normed_low, key_w).astype(jnp.bfloat16)
-    query_heads, key_heads, value_heads = (
-        lax.all_to_all(query_rows, "seq", split_axis=1, concat_axis=0, tiled=True),
-        lax.all_to_all(key_rows, "seq", split_axis=1, concat_axis=0, tiled=True),
-        lax.all_to_all(value_rows, "seq", split_axis=1, concat_axis=0, tiled=True),
+    tok_rows = hidden_in.shape[0]
+    valid_col = lax.dynamic_slice_in_dim(valid, seq_rank * tok_rows, tok_rows, 0).astype(jnp.float32)[:, None]
+    normed, mixed, pair, third, lse = front(
+        mesh, hidden_in, skip_values, doc_lens, valid, norm1_gain, norm1_shift, query_w, query_b, key_w, value_w, value_b, 0
     )
-    query_split = query_heads.reshape(head_shape)
-    key_split = key_heads.reshape(head_shape)
-    value_split = value_heads.reshape(head_shape)
-    mixed_heads, log_totals = attend_forward(
-        query_split, key_split, value_split, segments, valid, block_rows, score_scale
+    output, middle_grad, mixed_grad, part, proj_part, small = mlp_block(
+        mixed, hidden_in, out_grad, valid_col, proj_w, proj_b, norm2_gain, norm2_shift, fc_w, fc_b, out_w, out_b
     )
-    mixed_rows = lax.all_to_all(mixed_heads, "seq", split_axis=0, concat_axis=1, tiled=True)
-    valid_col = lax.dynamic_slice_in_dim(valid, seq_rank * tok_rows, tok_rows, 0).astype(jnp.float32)[:, None]
-    output, middle_grad, mixed_grad, part, proj_part, small = mlp_block(
-        mixed_rows, hidden_in, out_grad, valid_col, proj_w, proj_b, norm2_gain, norm2_shift, fc_w, fc_b, out_w, out_b
+    part1 = part.reshape(-1, SUB, WID)
+    summed, grad_input, grad_skip, small_z, small_all = back(
+        mesh, doc_lens, valid, mixed_grad, pair, third, lse, normed, hidden_in, norm1_gain, middle_grad,
+        query_w, key_w, value_w, proj_part, small, part1, 1
     )
-    grad_heads = lax.all_to_all(mixed_grad, "seq", split_axis=1, concat_axis=0, tiled=True)
-    query_grad, key_grad, value_grad = attend_backward(
-        query_split,
-        key_split,
-        value_split,
-        grad_heads.reshape(head_shape),
-        log_totals,
-        segments,
-        valid,
-        block_rows,
-        score_scale,
-    )
-    query_grad_rows, key_grad_rows, value_grad_rows = (
-        lax.all_to_all(query_grad, "seq", split_axis=0, concat_axis=1, tiled=True),
-        lax.all_to_all(key_grad, "seq", split_axis=0, concat_axis=1, tiled=True),
-        lax.all_to_all(value_grad, "seq", split_axis=0, concat_axis=1, tiled=True),
-    )
-    grad_query_w = matmul_left_t(normed_low, query_grad_rows)
-    grad_key_w = matmul_left_t(normed_low, key_grad_rows)
-    grad_query_b = jnp.sum(query_grad_rows.astype(jnp.float32), axis=0)
-    normed_grad = matmul_right_t(query_grad_rows, query_w) + matmul_right_t(key_grad_rows, key_w)
-    fresh_grad = value_grad_rows[:, :VFRESH]
-    grad_skip = value_grad_rows[:, VFRESH:]
-    grad_value_w = matmul_left_t(normed_low, fresh_grad)
-    grad_value_b = jnp.sum(fresh_grad.astype(jnp.float32), axis=0)
-    normed_grad = normed_grad + matmul_right_t(fresh_grad, value_w)
-    hidden_part, grad_norm1_gain, grad_norm1_shift = norm1_pull(normed_grad)
-    grad_input = (middle_grad + hidden_part).astype(jnp.bfloat16)
-    n_dev = lax.axis_size("dp") * seq_size
-    half = D // 2
-    value_part = jnp.concatenate([grad_value_w[:half], grad_value_w[half:]], axis=1)
-    low = jnp.bfloat16
-    part2 = [proj_part, grad_query_w.astype(low), grad_key_w.astype(low), value_part.astype(low)]
-    rows = sum(g.shape[0] for g in part2)
-    quantum = n_dev * SUB
-    padded = -(-rows // quantum) * quantum
-    part2 = jnp.concatenate(part2 + [jnp.zeros((padded - rows, WID), low)]).reshape(-1, SUB, WID)
-    part1 = part.reshape(-1, SUB, WID)
-    head = jnp.stack([grad_norm1_gain, grad_norm1_shift, grad_query_b, jnp.pad(grad_value_b, (0, half))])
-    small = small + jnp.pad(head, ((0, 12), (0, 0)))
-    summed, small_z, small_all = all_reduce(mesh, part1, part2, small, SHARES, 0)
     row0 = part1.shape[0] * SUB
     grad_out_w, grad_fc_w, grad_proj_w, grad_query_w, grad_key_w, grad_value_w = widen(
         summed.reshape(-1, WID), row0, D, fc_w.shape[1], VFRESH

time: 386 us -> 263 us (0.68)
  Pallas kernels: 157 us -> 234 us
  waiting for transfers between devices: 68.9 us -> 0 us
  matrix products: 53.4 us -> 0 us
  starting transfers between devices: 31.7 us -> 0 us
  local copies, waits for them, and re-layouts: 46.5 us -> 24.2 us
  other arithmetic: 21.7 us -> 2.1 us
    pallas_call x1 -> x2, Pallas kernels: 132 us -> 209 us  [the longest x1 165 us: back(): pl.pallas_call(functools.partial(back_kernel, (n_dp, n_seq, halves, strea...]
    all_to_all x8 -> x0, waiting for transfers between devices: 68.9 us -> none  [the longest x1 11.2 us: local(): lax.all_to_all(mixed_grad, 'seq', split_axis=1, concat_axis=0, tiled=True)]
    dot_general x23 -> x0, matrix products: 53.4 us -> none  [the longest x4 12.9 us: block_scores(): jnp.einsum('qhd,khd->hqk', query_block, key_heads, preferred_element_type...]
    all_to_all x8 -> x0, starting transfers between devices: 31.7 us -> none  [the longest x1 6.35 us: local(): lax.all_to_all(value_rows, 'seq', split_axis=1, concat_axis=0, tiled=True)]
    all_to_all x13 -> x0, local copies, waits for them, and re-layouts: 11.1 us -> none  [the longest x2 3.67 us: local(): lax.all_to_all(query_grad, 'seq', split_axis=0, concat_axis=1, tiled=True)]
    reduce_sum x8 -> x0, other arithmetic: 7.98 us -> none  [the longest x2 4.56 us: one_block(): row_totals = jnp.sum(powered, axis=-1, keepdims=True)]
    convert_element_type x5 -> x0, other arithmetic: 5.56 us -> none  [the longest x1 2.03 us: attend_backward(): value_acc.astype(jnp.bfloat16).reshape(flat_shape)]
    unnamed x66 -> x26, local copies, waits for them, and re-layouts: 12.2 us -> 10.7 us
  transfers between devices with their start and end apart: 8 -> 0, of which waited for: 8 -> 0; matrix products, arithmetic and copies ran while one was open for 5% -> 0% of each run, Pallas kernels for 0% -> 0%
where the time goes in v1:
time: 263 us; the launch traced here: 262 us
  Pallas kernels  234 us (89%)
  local copies, waits for them, and re-layouts  24.2 us (9%)
    pallas_call x1, Pallas kernels, back(): pl.pallas_call(functools.partial(back_kernel, (n_dp, n_seq, halves, strea...  165 us
    pallas_call x1, Pallas kernels, front(): pl.pallas_call(functools.partial(front_kernel, (n_dp, n_seq)), in_specs=[...  44.5 us
    pallas_call x1, Pallas kernels, mlp_block(): pl.pallas_call(functools.partial(mlp_kernel, steps), grid=(steps,), in_sp...  15.4 us
    unnamed x26, local copies, waits for them, and re-layouts  10.7 us
    pallas_call x1, Pallas kernels, widen(): pl.pallas_call(functools.partial(widen_kernel, pieces), in_specs=[hbm], o...  9.91 us

profile of v1, /device:TPU:0, one launch (start us, length us, event | category | flops | bytes accessed | tf_op | source)
XLA Modules:
  0.0 262.1 jit_solution(11041705112461425088)
XLA Ops:
  0.7 0.9 dynamic-slice_convert_fusion
  1.6 1.2 reshape.88.vb
  2.8 1.3 reshape.85.n1g
  4.1 1.3 reshape.86.n1s
  5.4 1.3 reshape.87.qb
  6.6 0.7 reshape.89.proj_b
  7.3 0.7 reshape.90.n2g
  8.0 0.7 reshape.91.n2s
  8.7 0.7 reshape.93.out_b
  9.5 44.5 %front.1 = (bf16[256,768]{1,0:T(8,128)(2,1)}, bf16[256,768]{1,0:T(8,128)(2,1)}, bf16[3,1024,128]{2,1,0:T(8,128)(2,1)}, bf16[3,1024,128]{2,1,0:T(8,128)(2,1)}, f32[1024,128]{1,0:T(8,128)}) custom-call(s32[1,3]{1,0:T(1,128)} %lens.3, bf16[256,768]{1,0:T(8,128)(2,1)} %hidden.5, bf16[256,384]{1,0:T(8,128)(2,1)} %skip.1, s32[1,1024]{1,0:T(1,128)} %bitcast.9, ...), custom_call_target="tpu_custom_call" | custom-call | tf_op jit(solution)/shard_map/front/pallas_call | solution.py:684
  54.1 1.0 copy-done.6
  55.0 15.4 %mlp_block.1 = (bf16[256,768]{1,0:T(8,128)(2,1)}, f32[256,768]{1,0:T(8,128)S(1)}, bf16[256,768]{1,0:T(8,128)(2,1)S(1)}, bf16[4,2,768,768]{3,2,1,0:T(8,128)(2,1)}...) custom-call(bf16[256,768]{1,0:T(8,128)(2,1)S(1)} %copy-done.6, bf16[256,768]{1,0:T(8,128)(2,1)S(1)} %copy-done.1, ...), custom_call_target="tpu_custom_call" | custom-call | tf_op jit(solution)/shard_map/mlp_block/pallas_call | solution.py:382
  70.4 1.0 copy-done.3
  71.4 0.9 copy-done.4
  72.3 0.7 copy-done.7
  73.7 164.6 %back.1 = (bf16[576,16,768]{2,1,0:T(8,128)(2,1)}, bf16[256,768]{1,0:T(8,128)(2,1)}, bf16[256,384]{1,0:T(8,128)(2,1)}, f32[16,768]{1,0:T(8,128)}, f32[16,768]{1,0:T(8,128)}) custom-call(s32[1,3]{1,0:T(1,128)} %lens.3, s32[1,1024]{1,0:T(1,128)} %bitcast.10, bf16[256,768]{1,0:T(8,128)(2,1)} %copy-done.7, bf16[3,1024,128]{2,1,0:T(8,128)(2,1)} %get-tuple-element.44.pair, ...), custom_call_target="tpu_custom_call" | custom-call | tf_op jit(solution)/shard_map/back/pallas_call | solution.py:881
  238.3 1.3 slice.48
  240.2 1.2 add_sqrt_fusion
  241.4 1.3 slice_reduce_fusion.7
  242.7 0.7 slice.45
  243.5 1.7 slice_reduce_fusion
  245.7 5.0 %copy-done = bf16[576,16,768]{2,1,0:T(8,128)(2,1)S(1)} copy-done((bf16[576,16,768]{2,1,0:T(8,128)(2,1)S(1)}, bf16[576,16,768]{2,1,0:T(8,128)(2,1)}, u32[]{:S(2)}) %copy-start) | copy-done | bytes 14155800
  250.8 9.9 %widen.1 = (f32[3072,768]{1,0:T(8,128)}, f32[768,3072]{1,0:T(8,128)}, f32[768,768]{1,0:T(8,128)}, f32[768,768]{1,0:T(8,128)}, f32[768,768]{1,0:T(8,128)}, /*index=5*/f32[768,384]{1,0:T(8,128)}) custom-call(bf16[9216,768]{1,0:T(8,128)(2,1)S(1)} %bitcast.6), custom_call_target="tpu_custom_call" | custom-call | tf_op jit(solution)/shard_map/widen/pallas_call | solution.py:459
  260.7 0.7 copy.42
  (22 shorter events, 2.1 us)
Async XLA Ops:
  0.7 53.4 %copy-start.1 = (bf16[256,768]{1,0:T(8,128)(2,1)S(1)}, bf16[256,768]{1,0:T(8,128)(2,1)}, u32[]{:S(2)}) copy-start(bf16[256,768]{1,0:T(8,128)(2,1)} %hidden.5) | copy-start | bytes 1179652
  0.7 53.4 %copy-start.9 = (f32[3072]{0:T(1024)S(1)}, f32[3072]{0:T(1024)}, u32[]{:S(2)}) copy-start(f32[3072]{0:T(1024)} %param.37) | copy-start | bytes 36868
  0.7 53.4 %copy-start.2 = (bf16[768,768]{1,0:T(8,128)(2,1)S(1)}, bf16[768,768]{1,0:T(8,128)(2,1)}, u32[]{:S(2)}) copy-start(bf16[768,768]{1,0:T(8,128)(2,1)} %proj_w.1) | copy-start | bytes 3538948
  0.7 53.4 %copy-start.5 = (bf16[256,768]{1,0:T(8,128)(2,1)S(1)}, bf16[256,768]{1,0:T(8,128)(2,1)}, u32[]{:S(2)}) copy-start(bf16[256,768]{1,0:T(8,128)(2,1)} %og.1) | copy-start | bytes 1179652
  54.0 1.0 copy-start.6
  70.4 1.0 copy-start.3
  71.4 0.9 copy-start.4
  72.3 0.7 copy-start.7
  73.0 0.6 copy-start.8
  245.7 5.0 %copy-start = (bf16[576,16,768]{2,1,0:T(8,128)(2,1)S(1)}, bf16[576,16,768]{2,1,0:T(8,128)(2,1)}, u32[]{:S(2)}) copy-start(bf16[576,16,768]{2,1,0:T(8,128)(2,1)} %get-tuple-element.55) | copy-start | bytes 42467332
  250.8 9.9 %copy-start.10 = (bf16[256,768]{1,0:T(8,128)(2,1)S(1)}, bf16[256,768]{1,0:T(8,128)(2,1)}, u32[]{:S(2)}) copy-start(bf16[256,768]{1,0:T(8,128)(2,1)} %get-tuple-element.90) | copy-start | bytes 1179652
  250.8 10.7 %copy-start.11 = (bf16[256,384]{1,0:T(8,128)(2,1)S(1)}, bf16[256,384]{1,0:T(8,128)(2,1)}, u32[]{:S(2)}) copy-start(bf16[256,384]{1,0:T(8,128)(2,1)} %get-tuple-element.91) | copy-start | bytes 589828

commit v2 on v1

--- a/solution.py
+++ b/solution.py
@@ -24,7 +24,7 @@
 SUB = 16
 WID = 768
 UNIT_BYTES = SUB * WID * 2
-SHARES = ("ababzababzab", "ababab")
+SHARES = ("abababababab", "ababab")
 STARTS = (3.0, 50.0)
 MARKS = (8.0, 13.0, 16.0, 18.0, 19.0, 22.0, 25.0, 27.0, 28.0, 40.0, 50.0)
 
@@ -289,6 +289,10 @@
 GELU_A = 0.044715
 
 
+def flat(ref):
+    return ref[...].reshape(1, -1)
+
+
 def row_sum(v):
     return jnp.sum(v, axis=0, keepdims=True)
 
@@ -301,7 +305,7 @@
     @pl.when(j == 0)
     def _():
         x = hidden[...].astype(jnp.float32)
-        attn = matmul(mixed[...], proj_w[...]) + proj_b[...]
+        attn = matmul(mixed[...], proj_w[...]) + flat(proj_b)
         middle = x + attn
         mid_ref[...] = middle
         v = valid[...]
@@ -310,7 +314,7 @@
         xhat = spread * inv
         xhat_ref[...] = xhat
         inv_ref[...] = jnp.broadcast_to(inv, inv_ref.shape)
-        nt_ref[...] = (xhat * n2g[...] + n2s[...]).astype(jnp.bfloat16)
+        nt_ref[...] = (xhat * flat(n2g) + flat(n2s)).astype(jnp.bfloat16)
         small[...] = jnp.zeros_like(small)
         s0 = row_sum(jnp.sum(x * x, axis=-1, keepdims=True) * v)
         s1 = row_sum(jnp.sum(attn * attn, axis=-1, keepdims=True) * v)
@@ -352,7 +356,7 @@
 
     @pl.when(j == steps - 1)
     def _():
-        mlp_out = mlp_acc[...] + out_b[...]
+        mlp_out = mlp_acc[...] + flat(out_b)
         output[...] = (mid_ref[...] + mlp_out).astype(jnp.bfloat16)
         s2 = row_sum(jnp.sum(mlp_out * mlp_out, axis=-1, keepdims=True) * valid[...])
         lane = lax.broadcasted_iota(jnp.int32, (1, WID), 1)
@@ -361,7 +365,7 @@
         xhat = xhat_ref[...]
         small[5:6, :] = row_sum(two_grad * xhat)
         small[6:7, :] = row_sum(two_grad)
-        e = two_grad * n2g[...]
+        e = two_grad * flat(n2g)
         centre = jnp.mean(e, axis=-1, keepdims=True)
         along = jnp.mean(e * xhat, axis=-1, keepdims=True)
         grad = og[...].astype(jnp.float32) + (e - centre - xhat * along) * inv_ref[:, 0:1]
@@ -382,26 +386,27 @@
     return pl.pallas_call(
         functools.partial(mlp_kernel, steps),
         grid=(steps,),
-        in_specs=[whole((rows, d)), whole((rows, d)), whole((rows, d)), whole((rows, 1)), whole((d, d)), whole((1, d)),
-                  whole((1, d)), whole((1, d)), pl.BlockSpec((d, FCH), lambda j: (0, j)), pl.BlockSpec((1, FCH), lambda j: (0, j)),
-                  pl.BlockSpec((FCH, d), lambda j: (j, 0)), whole((1, d))],
+        in_specs=[whole((rows, d)), whole((rows, d)), whole((rows, d)), whole((rows, 1)), whole((d, d)), whole((d,)),
+                  whole((d,)), whole((d,)), pl.BlockSpec((d, FCH), lambda j: (0, j)), pl.BlockSpec((1, FCH), lambda j: (0, j)),
+                  pl.BlockSpec((FCH, d), lambda j: (j, 0)), whole((d,))],
         out_specs=(whole((rows, d)), whole((rows, d)), whole((rows, d)), pl.BlockSpec((1, 2, FCH, d), lambda j: (j, 0, 0, 0)),
                    whole((d, d)), whole((16, d))),
         out_shape=(jax.ShapeDtypeStruct((rows, d), bf), jax.ShapeDtypeStruct((rows, d), f32), jax.ShapeDtypeStruct((rows, d), bf),
                    jax.ShapeDtypeStruct((steps, 2, FCH, d), bf), jax.ShapeDtypeStruct((d, d), bf), jax.ShapeDtypeStruct((16, d), f32)),
         scratch_shapes=[pltpu.VMEM((rows, d), bf), pltpu.VMEM((rows, d), f32), pltpu.VMEM((rows, 128), f32),
                         pltpu.VMEM((rows, d), f32), pltpu.VMEM((rows, d), f32), pltpu.VMEM((rows, d), f32)],
-        compiler_params=pltpu.CompilerParams(vmem_limit_bytes=48 * 2**20, dimension_semantics=("arbitrary",)),
+        compiler_params=pltpu.CompilerParams(vmem_limit_bytes=62 * 2**20, dimension_semantics=("arbitrary",)),
         name="mlp_block",
-    )(mixed, hidden, og, valid_col, proj_w, vec(proj_b), vec(n2g), vec(n2s), fc_w, vec(fc_b), out_w, vec(out_b))
+    )(mixed, hidden, og, valid_col, proj_w, proj_b, n2g, n2s, fc_w, vec(fc_b), out_w, out_b)
 
 
 PIECE = 384
 
 
-def widen_kernel(pieces, src, *refs):
-    n_out = 6
-    outs, (inbuf, stage, in_sem, out_sem) = refs[:n_out], refs[n_out:]
+def widen_kernel(cfg, src, small, small_z, gi_in, gs_in, *refs):
+    pieces, n_out = cfg
+    outs, vectors, (norms, gi_out, gs_out) = refs[:n_out], refs[n_out : n_out + 9], refs[n_out + 9 : n_out + 12]
+    inbuf, stage, gi_buf, gs_buf, in_sem, out_sem, row_sem = refs[n_out + 12 :]
     depth = inbuf.shape[0]
 
     def fetch(i):
@@ -419,6 +424,10 @@
     n = len(pieces)
     for i in range(min(depth, n)):
         fetch(i).start()
+    row_in = [pltpu.make_async_copy(gi_in, gi_buf, row_sem.at[0]), pltpu.make_async_copy(gs_in, gs_buf, row_sem.at[1])]
+    row_out = [pltpu.make_async_copy(gi_buf, gi_out, row_sem.at[2]), pltpu.make_async_copy(gs_buf, gs_out, row_sem.at[3])]
+    for c in row_in:
+        c.start()
     for i in range(n):
         slot = i % depth
         fetch(i).wait()
@@ -436,12 +445,24 @@
             c.start()
         if i + depth < n:
             fetch(i + depth).start()
+        if i == depth:
+            for a, b in zip(row_in, row_out):
+                a.wait()
+                b.start()
+            for row, v in zip((0, 1, 2, 3, 4, 5, 6, 7), vectors):
+                v[...] = small[row, 0 : v.shape[0]]
+            for q in range(vectors[8].shape[0] // WID):
+                vectors[8][q * WID : (q + 1) * WID] = small[8 + q, :]
+            sums = small_z[12:13, 0:4]
+            norms[...] = jnp.sqrt(sums[:, 0:3] / (sums[:, 3:4] * D) + square_eps)
     for i in range(max(0, n - depth), n):
         for c in put(i):
             c.wait()
-
-
-def widen(summed, row0, d, ff, vf):
+    for c in row_out:
+        c.wait()
+
+
+def widen(summed, small, small_z, grad_input, grad_skip, row0, d, ff, vf):
     pieces = []
     for j in range(ff // FCH):
         for h in range(2):
@@ -452,18 +473,23 @@
         for h in range(2):
             pieces.append((row0 + w * d + h * PIECE, 2 + w, h * PIECE, 0, False))
     pieces.append((row0 + 3 * d, 5, 0, 0, True))
-    f32 = jnp.float32
-    depth = 3
+    f32, bf = jnp.float32, jnp.bfloat16
+    depth = 4
     hbm = pl.BlockSpec(memory_space=pl.ANY)
+    vmem = pl.BlockSpec(memory_space=pltpu.VMEM)
     shapes = [(ff, d), (d, ff), (d, d), (d, d), (d, d), (d, vf)]
+    vectors = [(d,), (d,), (d,), (vf,), (d,), (d,), (d,), (d,), (ff,)]
+    out_shape = [jax.ShapeDtypeStruct(s, f32) for s in shapes + vectors + [(1, 3)]]
+    out_shape += [jax.ShapeDtypeStruct(g.shape, bf) for g in (grad_input, grad_skip)]
     return pl.pallas_call(
-        functools.partial(widen_kernel, pieces),
-        in_specs=[hbm], out_specs=(hbm,) * 6, out_shape=tuple(jax.ShapeDtypeStruct(s, f32) for s in shapes),
-        scratch_shapes=[pltpu.VMEM((depth, PIECE, WID), jnp.bfloat16), pltpu.VMEM((depth, PIECE, WID), f32),
-                        pltpu.SemaphoreType.DMA((depth,)), pltpu.SemaphoreType.DMA((depth, 2))],
-        compiler_params=pltpu.CompilerParams(vmem_limit_bytes=32 * 2**20),
+        functools.partial(widen_kernel, (pieces, len(shapes))),
+        in_specs=[hbm, vmem, vmem, hbm, hbm], out_specs=(hbm,) * 6 + (vmem,) * 10 + (hbm,) * 2, out_shape=tuple(out_shape),
+        scratch_shapes=[pltpu.VMEM((depth, PIECE, WID), bf), pltpu.VMEM((depth, PIECE, WID), f32),
+                        pltpu.VMEM(grad_input.shape, bf), pltpu.VMEM(grad_skip.shape, bf),
+                        pltpu.SemaphoreType.DMA((depth,)), pltpu.SemaphoreType.DMA((depth, 2)), pltpu.SemaphoreType.DMA((4,))],
+        compiler_params=pltpu.CompilerParams(vmem_limit_bytes=62 * 2**20),
         name="widen",
-    )(summed)
+    )(summed, small, small_z, grad_input, grad_skip)
 
 
 LANES = 128
@@ -580,7 +606,7 @@
     x = hidden[...].astype(jnp.float32)
     spread = x - jnp.mean(x, axis=-1, keepdims=True)
     inv = lax.rsqrt(jnp.mean(spread * spread, axis=-1, keepdims=True) + norm_eps)
-    normed = (spread * inv * n1g[...] + n1s[...]).astype(jnp.bfloat16)
+    normed = (spread * inv * flat(n1g) + flat(n1s)).astype(jnp.bfloat16)
     normed_out[...] = normed
     swaps = [[Swap(n_seq, dp, sq, lambda to, t=t: sp.at[to, t], lambda me, t=t: rp.at[t, pl.ds(me * rows, rows)],
                    lambda d, t=t: ssem.at[0, t, d], lambda d, t=t: rsem.at[0, t, d]),
@@ -589,11 +615,11 @@
     first = True
     for t in range(3):
         if t == 0:
-            full = (matmul(normed, qw[...]) + qb[...]).astype(jnp.bfloat16)
+            full = (matmul(normed, qw[...]) + flat(qb)).astype(jnp.bfloat16)
         elif t == 1:
             full = matmul(normed, kw[...]).astype(jnp.bfloat16)
         else:
-            full = (matmul(normed, vw[...]) + vb[...]).astype(jnp.bfloat16)
+            full = (matmul(normed, vw[...]) + flat(vb)).astype(jnp.bfloat16)
         tiles = [full[:, c * LANES : (c + 1) * LANES] for c in range(full.shape[1] // LANES)]
         if t == 2:
             tiles += [skip[:, c * LANES : (c + 1) * LANES] for c in range(skip.shape[1] // LANES)]
@@ -677,7 +703,6 @@
     rows, d = hidden.shape
     group = rows * n_seq
     bf, f32 = jnp.bfloat16, jnp.float32
-    vec = lambda v: v.reshape(1, -1)
     vmem = pl.BlockSpec(memory_space=pltpu.VMEM)
     half = rows // 2
     dma = pltpu.SemaphoreType.DMA
@@ -697,7 +722,7 @@
             dma((2, 3, n_seq)), dma((2, 3, n_seq)), dma((2, n_seq)), dma((2, n_seq))],
         compiler_params=pltpu.CompilerParams(collective_id=collective_id, has_side_effects=True, vmem_limit_bytes=56 * 2**20),
         name="front",
-    )(lens, hidden, skip, vec(valid), vec(n1g), vec(n1s), qw, vec(qb), kw, vw, vec(vb))
+    )(lens, hidden, skip, valid.reshape(1, -1), n1g, n1s, qw, qb, kw, vw, vb)
 
 
 def back_kernel(cfg, lens, valid_row, mixed_grad, pair, third, lse, normed, hidden, n1g, mid_grad, qw, kw, vw, proj_part, small, part1,
@@ -837,7 +862,7 @@
             ex.start(s, 0)
     advance(next(mark))
     normed_grad = matmul_right_t(dq, qw[...]) + matmul_right_t(dk, kw[...]) + matmul_right_t(fresh, vw[...])
-    f = normed_grad * n1g[...]
+    f = normed_grad * flat(n1g)
     centre = jnp.mean(f, axis=-1, keepdims=True)
     along = jnp.mean(f * xhat, axis=-1, keepdims=True)
     grad_input[...] = (mid_grad[...] + (f - centre - xhat * along) * inv).astype(bf)
@@ -897,7 +922,7 @@
             dma((ns, n_st)), dma((ns, n_st)), dma((ns, 2)), dma((n_small,)), dma((n_small,))],
         compiler_params=pltpu.CompilerParams(collective_id=collective_id, has_side_effects=True, vmem_limit_bytes=63 * 2**20),
         name="back",
-    )(lens, valid.reshape(1, -1), mixed_grad, pair, third, lse, normed, hidden, n1g.reshape(1, -1), mid_grad, qw, kw, vw, proj_part,
+    )(lens, valid.reshape(1, -1), mixed_grad, pair, third, lse, normed, hidden, n1g, mid_grad, qw, kw, vw, proj_part,
       small, part1)
 
 
@@ -940,15 +965,11 @@
         query_w, key_w, value_w, proj_part, small, part1, 1
     )
     row0 = part1.shape[0] * SUB
-    grad_out_w, grad_fc_w, grad_proj_w, grad_query_w, grad_key_w, grad_value_w = widen(
-        summed.reshape(-1, WID), row0, D, fc_w.shape[1], VFRESH
-    )
-    grad_norm1_gain, grad_norm1_shift, grad_query_b = small_all[0], small_all[1], small_all[2]
-    grad_value_b = small_all[3, :VFRESH]
-    grad_proj_b, grad_norm2_gain, grad_norm2_shift, grad_out_b = (small_all[i] for i in (4, 5, 6, 7))
-    grad_fc_b = small_all[8:12].reshape(-1)
-    sums = small_z[12, :4]
-    norm_values = jnp.sqrt(sums[:3] / (sums[3] * D) + square_eps)[None, :]
+    (
+        grad_out_w, grad_fc_w, grad_proj_w, grad_query_w, grad_key_w, grad_value_w,
+        grad_norm1_gain, grad_norm1_shift, grad_query_b, grad_value_b, grad_proj_b, grad_norm2_gain, grad_norm2_shift,
+        grad_out_b, grad_fc_b, norm_values, grad_input, grad_skip,
+    ) = widen(summed.reshape(-1, WID), small_all, small_z, grad_input, grad_skip, row0, D, fc_w.shape[1], VFRESH)
     return (
         output,
         grad_input,

time: 263 us -> 226 us (0.86)
  local copies, waits for them, and re-layouts: 24.2 us -> 0.8 us
  Pallas kernels: 234 us -> 223 us
    pallas_call x1, Pallas kernels: 165 us -> 145 us  [back(): pl.pallas_call(functools.partial(back_kernel, (n_dp, n_seq, halves, strea...]
    unnamed x26 -> x0, local copies, waits for them, and re-layouts: 10.7 us -> none
    reshape x9 -> x0, local copies, waits for them, and re-layouts: 8.41 us -> none  [the longest x4 5.04 us: front(): vec = lambda v: v.reshape(1, -1)]
    pallas_call x1, Pallas kernels: 9.91 us -> 16.1 us  [widen(): pl.pallas_call(functools.partial(widen_kernel, (pieces, len(shapes))), in...]
    slice x4 -> x0, local copies, waits for them, and re-layouts: 4.96 us -> none  [the longest x1 1.67 us: local(): small_all[i]]
where the time goes in v2:
time: 226 us; the launch traced here: 225 us
  Pallas kernels  223 us (99%)
    pallas_call x1, Pallas kernels, back(): pl.pallas_call(functools.partial(back_kernel, (n_dp, n_seq, halves, strea...  145 us
    pallas_call x1, Pallas kernels, front(): pl.pallas_call(functools.partial(front_kernel, (n_dp, n_seq)), in_specs=[...  44.4 us
    pallas_call x1, Pallas kernels, mlp_block(): pl.pallas_call(functools.partial(mlp_kernel, steps), grid=(steps,), in_sp...  17.3 us
    pallas_call x1, Pallas kernels, widen(): pl.pallas_call(functools.partial(widen_kernel, (pieces, len(shapes))), in...  16.1 us

profile of v2, /device:TPU:0, one launch (start us, length us, event | category | flops | bytes accessed | tf_op | source)
XLA Modules:
  0.0 225.1 jit_solution(1346141507560481842)
XLA Ops:
  0.7 0.8 dynamic-slice_convert_fusion
  1.4 0.8 copy.39.valid
  2.2 44.4 %front.1 = (bf16[256,768]{1,0:T(8,128)(2,1)}, bf16[256,768]{1,0:T(8,128)(2,1)}, bf16[3,1024,128]{2,1,0:T(8,128)(2,1)}, bf16[3,1024,128]{2,1,0:T(8,128)(2,1)}, f32[1024,128]{1,0:T(8,128)}) custom-call(s32[1,3]{1,0:T(1,128)} %lens.3, bf16[256,768]{1,0:T(8,128)(2,1)} %hidden.5, bf16[256,384]{1,0:T(8,128)(2,1)} %skip.1, s32[1,1024]{1,0:T(1,128)} %bitcast.7, ...), custom_call_target="tpu_custom_call" | custom-call | tf_op jit(solution)/shard_map/front/pallas_call | solution.py:709
  46.7 17.3 %mlp_block.1 = (bf16[256,768]{1,0:T(8,128)(2,1)}, f32[256,768]{1,0:T(8,128)}, bf16[256,768]{1,0:T(8,128)(2,1)}, bf16[4,2,768,768]{3,2,1,0:T(8,128)(2,1)}, bf16[768,768]{1,0:T(8,128)(2,1)}, /*index=5*/f32[16,768]{1,0:T(8,128)}) custom-call(bf16[256,768]{1,0:T(8,128)(2,1)} %get-tuple-element.53.mixed, bf16[256,768]{1,0:T(8,128)(2,1)} %hidden.5, ...), custom_call_target="tpu_custom_call" | custom-call | tf_op jit(solution)/shard_map/mlp_block/pallas_call | solution.py:386
  63.9 144.9 %back.1 = (bf16[576,16,768]{2,1,0:T(8,128)(2,1)}, bf16[256,768]{1,0:T(8,128)(2,1)}, bf16[256,384]{1,0:T(8,128)(2,1)}, f32[16,768]{1,0:T(8,128)}, f32[16,768]{1,0:T(8,128)}) custom-call(s32[1,3]{1,0:T(1,128)} %lens.3, s32[1,1024]{1,0:T(1,128)} %bitcast.8, bf16[256,768]{1,0:T(8,128)(2,1)} %get-tuple-element.55.mixed_grad, ...), custom_call_target="tpu_custom_call" | custom-call | tf_op jit(solution)/shard_map/back/pallas_call | solution.py:906
  208.8 16.1 %widen.1 = (f32[3072,768]{1,0:T(8,128)}, f32[768,3072]{1,0:T(8,128)}, f32[768,768]{1,0:T(8,128)}, f32[768,768]{1,0:T(8,128)}, f32[768,768]{1,0:T(8,128)}, /*inde...) custom-call(bf16[9216,768]{1,0:T(8,128)(2,1)} %bitcast.5, ...), custom_call_target="tpu_custom_call" | custom-call | tf_op jit(solution)/shard_map/widen/pallas_call | solution.py:484

commit v3 on v2

--- a/solution.py
+++ b/solution.py
@@ -21,12 +21,14 @@
 
 
 MESH = pl.DeviceIdType.MESH
-SUB = 16
+SUB = 8
 WID = 768
 UNIT_BYTES = SUB * WID * 2
-SHARES = ("abababababab", "ababab")
-STARTS = (3.0, 50.0)
-MARKS = (8.0, 13.0, 16.0, 18.0, 19.0, 22.0, 25.0, 27.0, 28.0, 40.0, 50.0)
+FCH = 768
+CHUNK = FCH // SUB
+READY = (7.0, 10.5, 14.0, 17.5, 20.5)
+START_TWO = 63.0
+MARKS = (8.0, 12.0, 17.0, 24.0, 26.0, 28.0, 29.0, 30.0, 31.0, 32.0, 33.0, 34.0, 40.0, 48.0, 58.0)
 
 
 def bits_of(n):
@@ -43,23 +45,23 @@
     return bit, (dp, sq + step - 2 * step * bit)
 
 
-def plan_streams(n_dp, n_seq, phases, starts):
+def plan_streams(n_dp, n_seq, halves, steps):
     dpb = [("dp", j) for j in range(1, bits_of(n_dp))]
     sqb = [("seq", j) for j in range(bits_of(n_seq))]
     mid = len(dpb) // 2
-    orders = {"a": dpb + sqb, "b": dpb[mid:] + dpb[:mid] + sqb, "z": sqb + dpb}
+    orders = (dpb + sqb, dpb[mid:] + dpb[:mid] + sqb)
     quantum = (n_dp // 2) * n_seq
     streams = []
-    for phase, (half_units, kinds) in enumerate(phases):
+    for phase, half_units in enumerate(halves):
         total = half_units // quantum
-        first = used = 0
-        for i, kind in enumerate(kinds):
-            upto = round(total * (i + 1) / len(kinds))
-            n = (upto - used) * quantum
-            used = upto
-            if n:
-                streams.append((phase, first, n, orders[kind], starts[phase]))
-                first += n
+        count = max(1, total // 2)
+        first = 0
+        for i in range(count):
+            n = (2 if i < count - 1 else total - 2 * (count - 1)) * quantum
+            chunk = min(steps, (first + n - 1) // CHUNK)
+            start = READY[min(chunk, len(READY) - 1)] if phase == 0 else START_TWO
+            streams.append((phase, first, n, orders[i % 2], start, chunk))
+            first += n
     return streams
 
 
@@ -69,7 +71,7 @@
         free[res] = upto
     out = []
     stages = []
-    for phase, first, n, order, start in streams:
+    for phase, first, n, order, start, _ in streams:
         seq = []
         size = n
         seq.append((("dp", 0), size))
@@ -114,18 +116,19 @@
 
 
 class Exchange:
-    def __init__(self, streams, halves, dp, sq, parts, out, acc, recv, gat, sems):
+    def __init__(self, streams, halves, dp, sq, parts, out, recv, gat, sems):
         self.streams, self.halves = streams, halves
         self.dp, self.sq = dp, sq
-        self.parts, self.out, self.acc, self.recv, self.gat = parts, out, acc, recv, gat
+        self.parts, self.out, self.recv, self.gat = parts, out, recv, gat
         self.send_sem, self.recv_sem, self.local_sem = sems
         self.cbit, self.cdev = partner(("dp", 0), dp, sq)
         self.base = [sum(halves[:p]) for p in range(len(halves))]
-        self.off = [[self.base[s[0]] + s[1]] for s in streams]
+        self.off = [[st[1]] for st in streams]
         self.roff = []
-        r = sum(halves)
-        for phase, first, n, order, _ in streams:
-            rows = [self.base[phase] + first]
+        r = 0
+        for phase, first, n, order, _, _ in streams:
+            rows = [r]
+            r += n
             size = n
             for _ in order:
                 size //= 2
@@ -134,13 +137,12 @@
             self.roff.append(rows)
 
     @staticmethod
-    def recv_total(streams, halves):
-        r = sum(halves)
-        for phase, first, n, order, _ in streams:
-            size = n
-            for _ in order:
-                size //= 2
-                r += size
+    def recv_total(streams):
+        r = 0
+        for phase, first, n, order, _, _ in streams:
+            r += n
+            for i in range(len(order)):
+                r += n >> (i + 1)
         return r
 
     def n_stages(self, s):
@@ -152,32 +154,28 @@
             device_id=dev, device_id_type=MESH)
 
     def copies(self, s, k):
-        phase, first, n, order, _ = self.streams[s]
+        phase, first, n, order, _, _ = self.streams[s]
         depth = len(order)
         half_units, base = self.halves[phase], self.base[phase]
-        here = base + first
+        part = self.parts[phase]
+        own = self.cbit * half_units
         if k == 0:
-            part = self.parts[phase]
             other = (1 - self.cbit) * half_units + first
-            mine = self.cbit * half_units + first
-            return (self.remote(s, k, part.at[pl.ds(other, n)], self.recv.at[pl.ds(here, n)], self.cdev),
-                    pltpu.make_async_copy(part.at[pl.ds(mine, n)], self.acc.at[pl.ds(here, n)], self.local_sem.at[s, 0]))
+            return self.remote(s, k, part.at[pl.ds(other, n)], self.recv.at[pl.ds(self.roff[s][0], n)], self.cdev), None
         if k <= depth:
             half = n >> k
             bit, dev = partner(order[k - 1], self.dp, self.sq)
-            at = self.off[s][k - 1]
-            return (self.remote(s, k, self.acc.at[pl.ds(at + (1 - bit) * half, half)],
-                                self.recv.at[pl.ds(self.roff[s][k], half)], dev), None)
+            at = own + self.off[s][k - 1] + (1 - bit) * half
+            return self.remote(s, k, part.at[pl.ds(at, half)], self.recv.at[pl.ds(self.roff[s][k], half)], dev), None
         g = 2 * depth + 1 - k
         if g >= 1:
             half = n >> g
             bit, dev = partner(order[g - 1], self.dp, self.sq)
-            piece = self.gat.at[pl.ds(self.off[s][g], half)]
-            return (self.remote(s, k, piece, piece, dev), None)
-        piece = self.gat.at[pl.ds(here, n)]
-        there = self.out.at[pl.ds(2 * base + self.cbit * half_units + first, n)]
-        return (self.remote(s, k, piece, there, self.cdev),
-                pltpu.make_async_copy(piece, there, self.local_sem.at[s, 1]))
+            piece = self.gat.at[pl.ds(base + self.off[s][g], half)]
+            return self.remote(s, k, piece, piece, dev), None
+        piece = self.gat.at[pl.ds(base + first, n)]
+        there = self.out.at[pl.ds(2 * base + own + first, n)]
+        return self.remote(s, k, piece, there, self.cdev), pltpu.make_async_copy(piece, there, self.local_sem.at[s])
 
     def start(self, s, k):
         for c in self.copies(s, k):
@@ -185,7 +183,7 @@
                 c.start()
 
     def finish(self, s, k):
-        phase, first, n, order, _ = self.streams[s]
+        phase, first, n, order, _, _ = self.streams[s]
         depth = len(order)
         remote, local = self.copies(s, k)
         remote.wait()
@@ -193,22 +191,22 @@
             local.wait()
         if k <= depth:
             half = n >> k
-            if k == 0:
-                off = self.off[s][0]
-            else:
+            if k > 0:
                 bit, _ = partner(order[k - 1], self.dp, self.sq)
-                off = self.off[s][k - 1] + bit * half
-                self.off[s].append(off)
-            self.add(off, self.roff[s][k], half, self.gat if k == depth else self.acc)
-
-    def add(self, off, roff, n, to):
-        acc, recv = self.acc, self.recv
-        step = 4 if n % 4 == 0 else (3 if n % 3 == 0 else (2 if n % 2 == 0 else 1))
+                self.off[s].append(self.off[s][k - 1] + bit * half)
+            at = self.cbit * self.halves[phase] + self.off[s][k]
+            to = (self.gat, self.base[phase] + self.off[s][k]) if k == depth else (self.parts[phase], at)
+            self.add(self.parts[phase], at, self.roff[s][k], half, to)
+
+    def add(self, part, at, roff, n, to):
+        recv = self.recv
+        dst, first = to
+        step = next(d for d in (8, 6, 4, 3, 2, 1) if n % d == 0)
 
         def body(i, c):
-            a = pl.ds(off + i * step, step)
+            a = pl.ds(at + i * step, step)
             b = pl.ds(roff + i * step, step)
-            to[a] = acc[a] + recv[b]
+            dst[pl.ds(first + i * step, step)] = part[a] + recv[b]
             return c
 
         lax.fori_loop(0, n // step, body, 0)
@@ -285,10 +283,6 @@
     )
 
 
-FCH = 768
-GELU_A = 0.044715
-
-
 def flat(ref):
     return ref[...].reshape(1, -1)
 
@@ -297,110 +291,8 @@
     return jnp.sum(v, axis=0, keepdims=True)
 
 
-def mlp_kernel(steps, mixed, hidden, og, valid, proj_w, proj_b, n2g, n2s, fc_w, fc_b, out_w, out_b,
-               output, mid_grad, mixed_grad, part, proj_part, small,
-               nt_ref, xhat_ref, inv_ref, mid_ref, mlp_acc, two_acc):
-    j = pl.program_id(0)
-
-    @pl.when(j == 0)
-    def _():
-        x = hidden[...].astype(jnp.float32)
-        attn = matmul(mixed[...], proj_w[...]) + flat(proj_b)
-        middle = x + attn
-        mid_ref[...] = middle
-        v = valid[...]
-        spread = middle - jnp.mean(middle, axis=-1, keepdims=True)
-        inv = lax.rsqrt(jnp.mean(spread * spread, axis=-1, keepdims=True) + norm_eps)
-        xhat = spread * inv
-        xhat_ref[...] = xhat
-        inv_ref[...] = jnp.broadcast_to(inv, inv_ref.shape)
-        nt_ref[...] = (xhat * flat(n2g) + flat(n2s)).astype(jnp.bfloat16)
-        small[...] = jnp.zeros_like(small)
-        s0 = row_sum(jnp.sum(x * x, axis=-1, keepdims=True) * v)
-        s1 = row_sum(jnp.sum(attn * attn, axis=-1, keepdims=True) * v)
-        s3 = row_sum(v)
-        lane = lax.broadcasted_iota(jnp.int32, (1, WID), 1)
-        small[12:13, :] = jnp.where(lane == 0, s0, jnp.where(lane == 1, s1, jnp.where(lane == 3, s3, 0.0)))
-        small[7:8, :] = row_sum(og[...].astype(jnp.float32))
-
-    nt = nt_ref[...]
-    fw = fc_w[...]
-    ow = out_w[...]
-    g_low = og[...]
-    pre = matmul(nt, fw) + fc_b[...]
-    sq = pre * pre
-    t = jnp.tanh(tanh_coef * (pre + GELU_A * sq * pre))
-    act = (0.5 * pre * (1.0 + t)).astype(jnp.bfloat16)
-    slope = 0.5 * (1.0 + t) + 0.5 * pre * (1.0 - t * t) * (tanh_coef * (1.0 + 3.0 * GELU_A * sq))
-    pre_grad = matmul_right_t(g_low, ow) * slope
-    fcb = row_sum(pre_grad)
-    for i in range(steps):
-        @pl.when(j == i)
-        def _():
-            small[8 + i : 9 + i, :] = fcb
-    low = pre_grad.astype(jnp.bfloat16)
-    part[0, 0] = matmul_left_t(act, g_low).astype(jnp.bfloat16)
-    part[0, 1] = matmul_left_t(nt, low).astype(jnp.bfloat16)
-    mlp = matmul(act, ow)
-    two = matmul_right_t(low, fw)
-
-    @pl.when(j == 0)
-    def _():
-        mlp_acc[...] = mlp
-        two_acc[...] = two
-
-    @pl.when(j > 0)
-    def _():
-        mlp_acc[...] = mlp_acc[...] + mlp
-        two_acc[...] = two_acc[...] + two
-
-    @pl.when(j == steps - 1)
-    def _():
-        mlp_out = mlp_acc[...] + flat(out_b)
-        output[...] = (mid_ref[...] + mlp_out).astype(jnp.bfloat16)
-        s2 = row_sum(jnp.sum(mlp_out * mlp_out, axis=-1, keepdims=True) * valid[...])
-        lane = lax.broadcasted_iota(jnp.int32, (1, WID), 1)
-        small[12:13, :] = small[12:13, :] + jnp.where(lane == 2, s2, 0.0)
-        two_grad = two_acc[...]
-        xhat = xhat_ref[...]
-        small[5:6, :] = row_sum(two_grad * xhat)
-        small[6:7, :] = row_sum(two_grad)
-        e = two_grad * flat(n2g)
-        centre = jnp.mean(e, axis=-1, keepdims=True)
-        along = jnp.mean(e * xhat, axis=-1, keepdims=True)
-        grad = og[...].astype(jnp.float32) + (e - centre - xhat * along) * inv_ref[:, 0:1]
-        mid_grad[...] = grad
-        small[4:5, :] = row_sum(grad)
-        grad_low = grad.astype(jnp.bfloat16)
-        mixed_grad[...] = matmul_right_t(grad_low, proj_w[...]).astype(jnp.bfloat16)
-        proj_part[...] = matmul_left_t(mixed[...], grad_low).astype(jnp.bfloat16)
-
-
-def mlp_block(mixed, hidden, og, valid_col, proj_w, proj_b, n2g, n2s, fc_w, fc_b, out_w, out_b):
-    rows, d = hidden.shape
-    ff = fc_w.shape[1]
-    steps = ff // FCH
-    whole = lambda shape: pl.BlockSpec(shape, lambda j: (0,) * len(shape))
-    vec = lambda v: v.reshape(1, -1)
-    f32, bf = jnp.float32, jnp.bfloat16
-    return pl.pallas_call(
-        functools.partial(mlp_kernel, steps),
-        grid=(steps,),
-        in_specs=[whole((rows, d)), whole((rows, d)), whole((rows, d)), whole((rows, 1)), whole((d, d)), whole((d,)),
-                  whole((d,)), whole((d,)), pl.BlockSpec((d, FCH), lambda j: (0, j)), pl.BlockSpec((1, FCH), lambda j: (0, j)),
-                  pl.BlockSpec((FCH, d), lambda j: (j, 0)), whole((d,))],
-        out_specs=(whole((rows, d)), whole((rows, d)), whole((rows, d)), pl.BlockSpec((1, 2, FCH, d), lambda j: (j, 0, 0, 0)),
-                   whole((d, d)), whole((16, d))),
-        out_shape=(jax.ShapeDtypeStruct((rows, d), bf), jax.ShapeDtypeStruct((rows, d), f32), jax.ShapeDtypeStruct((rows, d), bf),
-                   jax.ShapeDtypeStruct((steps, 2, FCH, d), bf), jax.ShapeDtypeStruct((d, d), bf), jax.ShapeDtypeStruct((16, d), f32)),
-        scratch_shapes=[pltpu.VMEM((rows, d), bf), pltpu.VMEM((rows, d), f32), pltpu.VMEM((rows, 128), f32),
-                        pltpu.VMEM((rows, d), f32), pltpu.VMEM((rows, d), f32), pltpu.VMEM((rows, d), f32)],
-        compiler_params=pltpu.CompilerParams(vmem_limit_bytes=62 * 2**20, dimension_semantics=("arbitrary",)),
-        name="mlp_block",
-    )(mixed, hidden, og, valid_col, proj_w, proj_b, n2g, n2s, fc_w, vec(fc_b), out_w, out_b)
-
-
 PIECE = 384
+VPIECE = 192
 
 
 def widen_kernel(cfg, src, small, small_z, gi_in, gs_in, *refs):
@@ -410,15 +302,16 @@
     depth = inbuf.shape[0]
 
     def fetch(i):
-        return pltpu.make_async_copy(src.at[pl.ds(pieces[i][0], PIECE)], inbuf.at[i % depth], in_sem.at[i % depth])
+        size = VPIECE if pieces[i][4] else PIECE
+        return pltpu.make_async_copy(src.at[pl.ds(pieces[i][0], size)], inbuf.at[i % depth, pl.ds(0, size)], in_sem.at[i % depth])
 
     def put(i):
         slot = i % depth
-        _, which, row, col, half = pieces[i]
+        _, which, row, col, split = pieces[i]
         out = outs[which]
-        if half:
-            return [pltpu.make_async_copy(stage.at[slot, :, pl.ds(h * PIECE, PIECE)],
-                                          out.at[pl.ds(h * PIECE, PIECE)], out_sem.at[slot, h]) for h in range(2)]
+        if split:
+            return [pltpu.make_async_copy(stage.at[slot, pl.ds(0, VPIECE), pl.ds(h * VFRESH, VFRESH)],
+                                          out.at[pl.ds(row + h * VFRESH, VPIECE)], out_sem.at[slot, h]) for h in range(2)]
         return [pltpu.make_async_copy(stage.at[slot], out.at[pl.ds(row, PIECE), pl.ds(col, WID)], out_sem.at[slot, 0])]
 
     n = len(pieces)
@@ -440,7 +333,7 @@
             stage[slot, rows] = inbuf[slot, rows].astype(jnp.float32)
             return c
 
-        lax.fori_loop(0, PIECE // 32, body, 0)
+        lax.fori_loop(0, (VPIECE if pieces[i][4] else PIECE) // 32, body, 0)
         for c in put(i):
             c.start()
         if i + depth < n:
@@ -462,17 +355,19 @@
         c.wait()
 
 
-def widen(summed, small, small_z, grad_input, grad_skip, row0, d, ff, vf):
+def widen(summed, small, small_z, grad_input, grad_skip, halves, d, ff, vf):
+    one, two = halves[0] * SUB, halves[1] * SUB
     pieces = []
-    for j in range(ff // FCH):
+    for j in range(ff // PIECE):
+        pieces.append((j * PIECE, 0, j * PIECE, 0, False))
+        pieces.append((one + j * PIECE, 1, (j % 2) * PIECE, j // 2 * FCH, False))
+    for h in range(2):
+        pieces.append((h * one + ff, 2, h * PIECE, 0, False))
+    for w in range(2):
         for h in range(2):
-            pieces.append((j * 2 * FCH + h * PIECE, 0, j * FCH + h * PIECE, 0, False))
-        for h in range(2):
-            pieces.append((j * 2 * FCH + FCH + h * PIECE, 1, h * PIECE, j * FCH, False))
-    for w in range(3):
-        for h in range(2):
-            pieces.append((row0 + w * d + h * PIECE, 2 + w, h * PIECE, 0, False))
-    pieces.append((row0 + 3 * d, 5, 0, 0, True))
+            pieces.append((2 * one + w * two + h * PIECE, 3 + w, h * PIECE, 0, False))
+    for h in range(2):
+        pieces.append((2 * one + h * two + d, 5, h * VPIECE, 0, True))
     f32, bf = jnp.float32, jnp.bfloat16
     depth = 4
     hbm = pl.BlockSpec(memory_space=pl.ANY)
@@ -611,8 +506,26 @@
     swaps = [[Swap(n_seq, dp, sq, lambda to, t=t: sp.at[to, t], lambda me, t=t: rp.at[t, pl.ds(me * rows, rows)],
                    lambda d, t=t: ssem.at[0, t, d], lambda d, t=t: rsem.at[0, t, d]),
               Swap(n_seq, dp, sq, lambda to, t=t: st.at[to, t], lambda me, t=t: rt.at[t, me],
-                   lambda d, t=t: ssem.at[1, t, d], lambda d, t=t: rsem.at[1, t, d])] for t in range(3)]
-    first = True
+                   lambda d, t=t: ssem.at[1, t, d], lambda d, t=t: rsem.at[1, t, d])] for t in range(2)]
+    swaps.append([Gather(n_seq, dp, sq, lambda to: sp.at[to, 2], lambda s: rp.at[2, pl.ds(s * rows, rows)],
+                         lambda i: ssem.at[0, 2, i], lambda i: rsem.at[0, 2, i]),
+                  Gather(n_seq, dp, sq, lambda to: st.at[to, 2], lambda s: rt.at[2, s],
+                         lambda i: ssem.at[1, 2, i], lambda i: rsem.at[1, 2, i])])
+
+    def lanes_of(v, tile):
+        return v[:, tile * LANES : (tile + 1) * LANES]
+
+    def place(t, r, pair, tile):
+        sp[r, t] = pair
+        st[r, t] = pack_third(tile[:half], tile[half:], r % 2)
+
+    fresh_tiles = VFRESH // LANES
+    reused = [r for r in range(n_seq) if PAIR_TILE[r] >= fresh_tiles]
+    for r in reused:
+        place(2, r, lanes_of(skip, PAIR_TILE[r] - fresh_tiles), lanes_of(skip, THIRD_TILE[r] - fresh_tiles))
+    pl.semaphore_wait(barrier, n_seq - 1)
+    for r in reused:
+        swaps[2][0].start(r)
     for t in range(3):
         if t == 0:
             full = (matmul(normed, qw[...]) + flat(qb)).astype(jnp.bfloat16)
@@ -620,23 +533,21 @@
             full = matmul(normed, kw[...]).astype(jnp.bfloat16)
         else:
             full = (matmul(normed, vw[...]) + flat(vb)).astype(jnp.bfloat16)
-        tiles = [full[:, c * LANES : (c + 1) * LANES] for c in range(full.shape[1] // LANES)]
-        if t == 2:
-            tiles += [skip[:, c * LANES : (c + 1) * LANES] for c in range(skip.shape[1] // LANES)]
-
-        def pair_dst(r, v):
-            sp[r, t] = v
-
-        def third_dst(r, v):
-            st[r, t] = v
-
-        split_tiles(tiles, pair_dst, third_dst, rows, n_seq)
-        if first:
-            pl.semaphore_wait(barrier, n_seq - 1)
-            first = False
-        swaps[t][0].start()
+        for r in range(n_seq):
+            if t < 2 or r not in reused:
+                place(t, r, lanes_of(full, PAIR_TILE[r]), lanes_of(full, THIRD_TILE[r]))
+        if t < 2:
+            swaps[t][0].start()
+        else:
+            for r in range(n_seq):
+                if r not in reused:
+                    swaps[2][0].start(r)
     for t in range(3):
-        swaps[t][1].start()
+        if t < 2:
+            swaps[t][1].start()
+        else:
+            for r in range(n_seq):
+                swaps[2][1].start(r)
         rp[t, pl.ds(pl.multiple_of(sq * rows, rows), rows)] = sp[sq, t]
         rt[t, sq] = st[sq, t]
     for i in range(n_seq):
@@ -725,52 +636,146 @@
     )(lens, hidden, skip, valid.reshape(1, -1), n1g, n1s, qw, qb, kw, vw, vb)
 
 
-def back_kernel(cfg, lens, valid_row, mixed_grad, pair, third, lse, normed, hidden, n1g, mid_grad, qw, kw, vw, proj_part, small, part1,
-                out, grad_input, grad_skip, small_z, small_out,
+GELU_A = 0.044715
+
+
+def back_kernel(cfg, lens, valid_row, mixed, hidden, og, valid_col, proj_w, proj_b, n2g, n2s, fc_b, out_b, n1g, lse, normed,
+                pair_in, third_in, fc_w, out_w, qw, kw, vw,
+                out, output, grad_input, grad_skip, small_z, small_out,
+                nt_ref, xhat_ref, mid_ref, mlp_acc, two_acc, inv_ref, wf, wo, pair, third, part1,
                 gs, gst, gp, gt, gthird, bias, dk_acc, dv_acc, dsp, dst, drp, drt, rows_in, part2,
-                acc, recv, gat, sbuf, gssem, grsem, dssem, drsem, send_sem, recv_sem, local_sem, ssend, srecv_sem):
-    n_dp, n_seq, halves, streams, order, marks = cfg
+                recv, gat, sbuf, load_sem, gssem, grsem, dssem, drsem, send_sem, recv_sem, local_sem, ssend, srecv_sem):
+    n_dp, n_seq, halves, streams, order, marks, steps = cfg
     dp, sq = lax.axis_index("dp"), lax.axis_index("seq")
     rows, d = hidden.shape
     half = rows // 2
     bf, f32 = jnp.bfloat16, jnp.float32
     barrier, count = entry_barrier(n_dp, n_seq, dp, sq, True)
-    full = mixed_grad[...]
-    tiles = [full[:, c * LANES : (c + 1) * LANES] for c in range(d // LANES)]
-
-    def pair_dst(r, v):
-        gs[r] = v
-
-    def third_dst(r, v):
-        gst[r] = v
-
-    split_tiles(tiles, pair_dst, third_dst, rows, n_seq)
+
+    def weight_copies(j):
+        cols = pl.ds(j * FCH, FCH)
+        return [pltpu.make_async_copy(fc_w.at[:, cols], wf.at[j % 2], load_sem.at[0, j]),
+                pltpu.make_async_copy(out_w.at[cols], wo.at[j % 2], load_sem.at[1, j])]
+
+    extra = [pltpu.make_async_copy(pair_in, pair, load_sem.at[2, 0]), pltpu.make_async_copy(third_in, third, load_sem.at[2, 1])]
+    late = [pltpu.make_async_copy(qw, wf.at[0], load_sem.at[3, 0]), pltpu.make_async_copy(kw, wf.at[1], load_sem.at[3, 1]),
+            pltpu.make_async_copy(vw, wo.at[0, :, pl.ds(0, VFRESH)], load_sem.at[3, 2])]
+    for j in range(2):
+        for copy in weight_copies(j):
+            copy.start()
+    for copy in extra:
+        copy.start()
+    x = hidden[...].astype(f32)
+    attn = matmul(mixed[...], proj_w[...]) + flat(proj_b)
+    middle = x + attn
+    mid_ref[...] = middle
+    real = valid_col[...]
+    spread = middle - jnp.mean(middle, axis=-1, keepdims=True)
+    inv = lax.rsqrt(jnp.mean(spread * spread, axis=-1, keepdims=True) + norm_eps)
+    xhat = spread * inv
+    xhat_ref[...] = xhat
+    inv_ref[...] = jnp.broadcast_to(inv, inv_ref.shape)
+    nt_ref[...] = (xhat * flat(n2g) + flat(n2s)).astype(bf)
+    s0 = row_sum(jnp.sum(x * x, axis=-1, keepdims=True) * real)
+    s1 = row_sum(jnp.sum(attn * attn, axis=-1, keepdims=True) * real)
+    s3 = row_sum(real)
+    word = lax.broadcasted_iota(jnp.int32, (1, WID), 1)
+    sums = jnp.where(word == 0, s0, jnp.where(word == 1, s1, jnp.where(word == 3, s3, 0.0)))
+    sbuf[0] = jnp.zeros_like(sbuf[0])
+    sbuf[0, 7:8] = row_sum(og[...].astype(f32))
     pl.semaphore_wait(barrier, count)
+    ex = Exchange(streams, halves, dp, sq, (part1, part2), out, recv, gat, (send_sem, recv_sem, local_sem))
+    tiny = Small(n_dp, n_seq, dp, sq, sbuf, ssend, srecv_sem, small_z, small_out)
+    todo = list(order)
+    mark = iter(marks)
+
+    def advance():
+        upto = next(mark)
+        while todo and todo[0][0] <= upto:
+            _, s, k = todo.pop(0)
+            ex.step(s, k)
+
+    def begin(phase, chunk):
+        for s, st in enumerate(streams):
+            if st[0] == phase and (chunk is None or st[5] == chunk):
+                ex.start(s, 0)
+
+    h1, h2 = halves
+    for j in range(steps):
+        for copy in weight_copies(j):
+            copy.wait()
+        slot = j % 2
+        pre = matmul(nt_ref[...], wf[slot]) + fc_b[:, j * FCH : (j + 1) * FCH]
+        sq_pre = pre * pre
+        t = jnp.tanh(tanh_coef * (pre + GELU_A * sq_pre * pre))
+        act = (0.5 * pre * (1.0 + t)).astype(bf)
+        slope = 0.5 * (1.0 + t) + 0.5 * pre * (1.0 - t * t) * (tanh_coef * (1.0 + 3.0 * GELU_A * sq_pre))
+        pre_grad = matmul_right_t(og[...], wo[slot]) * slope
+        sbuf[0, 8 + j : 9 + j] = row_sum(pre_grad)
+        pre_low = pre_grad.astype(bf)
+        part1[j * CHUNK : (j + 1) * CHUNK] = matmul_left_t(act, og[...]).astype(bf).reshape(CHUNK, SUB, WID)
+        part1[h1 + j * CHUNK : h1 + (j + 1) * CHUNK] = matmul_left_t(nt_ref[...], pre_low).astype(bf).reshape(CHUNK, SUB, WID)
+        begin(0, j)
+        mlp = matmul(act, wo[slot])
+        two = matmul_right_t(pre_low, wf[slot])
+        if j == 0:
+            mlp_acc[...] = mlp
+            two_acc[...] = two
+        else:
+            mlp_acc[...] = mlp_acc[...] + mlp
+            two_acc[...] = two_acc[...] + two
+        if j + 2 < steps:
+            for copy in weight_copies(j + 2):
+                copy.start()
+        if j > 0 and j < steps - 1:
+            advance()
+    for copy in late:
+        copy.start()
+    two_grad = two_acc[...]
+    xhat = xhat_ref[...]
+    sbuf[0, 5:6] = row_sum(two_grad * xhat)
+    sbuf[0, 6:7] = row_sum(two_grad)
+    e = two_grad * flat(n2g)
+    centre = jnp.mean(e, axis=-1, keepdims=True)
+    along = jnp.mean(e * xhat, axis=-1, keepdims=True)
+    grad = og[...].astype(f32) + (e - centre - xhat * along) * inv_ref[:, 0:1]
+    grad_low = grad.astype(bf)
+    full = matmul_right_t(grad_low, proj_w[...]).astype(bf)
+    for r in range(n_seq):
+        c = PAIR_TILE[r] * LANES
+        gs[r] = full[:, c : c + LANES]
+        c = THIRD_TILE[r] * LANES
+        gst[r] = pack_third(full[:half, c : c + LANES], full[half:, c : c + LANES], r % 2)
     swap_pair = Swap(n_seq, dp, sq, lambda to: gs.at[to], lambda me: gp.at[pl.ds(me * rows, rows)], lambda i: gssem.at[0, i], lambda i: grsem.at[0, i])
     swap_third = Swap(n_seq, dp, sq, lambda to: gst.at[to], lambda me: gt.at[me], lambda i: gssem.at[1, i], lambda i: grsem.at[1, i])
     swap_pair.start()
     swap_third.start()
-    ex = Exchange(streams, halves, dp, sq, (part1, part2), out, acc, recv, gat, (send_sem, recv_sem, local_sem))
-    tiny = Small(n_dp, n_seq, dp, sq, sbuf, ssend, srecv_sem, small_z, small_out)
-    for s, st in enumerate(streams):
-        if st[0] == 0:
-            ex.start(s, 0)
-    todo = list(order)
-
-    def advance(upto):
-        while todo and todo[0][0] <= upto:
-            _, s, k = todo.pop(0)
-            ex.step(s, k)
-
+    mlp_out = mlp_acc[...] + flat(out_b)
+    output[...] = (mid_ref[...] + mlp_out).astype(bf)
+    s2 = row_sum(jnp.sum(mlp_out * mlp_out, axis=-1, keepdims=True) * valid_col[...])
+    sbuf[0, 12:13] = sums + jnp.where(word == 2, s2, 0.0)
+    sbuf[0, 4:5] = row_sum(grad)
+    mid_ref[...] = grad
+    gw = matmul_left_t(mixed[...], grad_low).astype(bf)
+    top = d // 2 // SUB
+    at = steps * CHUNK
+    part1[at : at + top] = gw[: d // 2].reshape(top, SUB, WID)
+    part1[h1 + at : h1 + at + top] = gw[d // 2 :].reshape(top, SUB, WID)
+    if h1 > at + top:
+        for h in range(2):
+            part1[h * h1 + at + top : (h + 1) * h1] = jnp.zeros((h1 - at - top, SUB, WID), bf)
+    begin(0, steps)
+    advance()
     gp[pl.ds(pl.multiple_of(sq * rows, rows), rows)] = gs[sq]
     gt[sq] = gst[sq]
     for i in range(n_seq):
         cols = (i + 1) * rows
-        bias[i * rows : (i + 1) * rows, 0:cols] = mask_bias(lens, valid_row, i * rows, rows, cols)
-    units_d = d // SUB
-    part2[0:units_d] = proj_part[...].reshape(units_d, SUB, WID)
+        bias[i * rows : (i + 1) * rows, 0:cols] = mask_bias(lens, valid_row, i * rows, rows, cols).astype(bf)
     send = [Gather(n_seq, dp, sq, lambda to: dsp.at[to], lambda s: drp.at[s], lambda i: dssem.at[0, i], lambda i: drsem.at[0, i]),
             Gather(n_seq, dp, sq, lambda to: dst.at[to], lambda s: drt.at[s], lambda i: dssem.at[1, i], lambda i: drsem.at[1, i])]
+    advance()
+    for copy in extra:
+        copy.wait()
     low = low_lanes()
     scale = 1.0 / math.sqrt(HDIM)
     keep = (jnp.where(low, scale, 0.0).astype(bf), jnp.where(low, 0.0, scale).astype(bf))
@@ -783,13 +788,11 @@
         score_grad = (probs * (prob_grad - centre)).astype(bf)
         return matmul(score_grad, k), matmul_left_t(score_grad, q), matmul_left_t(probs.astype(bf), g)
 
-    mark = iter(marks)
-    advance(next(mark))
     swap_pair.wait()
     for i in reversed(range(n_seq)):
         here = slice(i * rows, (i + 1) * rows)
         cols = (i + 1) * rows
-        block = bias[here, 0:cols]
+        block = bias[here, 0:cols].astype(f32)
         q, k, v, g = pair[0, here], pair[1, 0:cols], pair[2, 0:cols], gp[here]
         dq0, dk0, dv0 = backward(q * keep[0], k, v, g * ones[0], block, lse[here, 0:1])
         dq1, dk1, dv1 = backward(q * keep[1], k, v, g * ones[1], block, lse[here, 1:2])
@@ -803,7 +806,7 @@
         dsp[i, 1] = dk_acc[here].astype(bf)
         dsp[i, 2] = dv_acc[here].astype(bf)
         send[0].start(i)
-        advance(next(mark))
+        advance()
     swap_third.wait()
     for s in range(n_seq):
         a, b = unpack_third(gt[s])
@@ -812,7 +815,7 @@
     for i in reversed(range(n_seq)):
         here = slice(i * rows, (i + 1) * rows)
         cols = (i + 1) * rows
-        block = bias[here, 0:cols]
+        block = bias[here, 0:cols].astype(f32)
         dq, dk, dv = backward(third[0, here] * keep[0], third[1, 0:cols], third[2, 0:cols], gthird[here], block, lse[here, 2:3])
         if i == n_seq - 1:
             dk_acc[...] = dk
@@ -825,15 +828,16 @@
         for t, a in ((1, dk_acc), (2, dv_acc)):
             dst[i, t] = pack_third(a[i * rows : i * rows + half], a[i * rows + half : (i + 1) * rows], False)
         send[1].start(i)
-        advance(next(mark))
+        advance()
     drp[sq] = dsp[sq]
     drt[sq] = dst[sq]
     x = hidden[...].astype(f32)
     spread = x - jnp.mean(x, axis=-1, keepdims=True)
     inv = lax.rsqrt(jnp.mean(spread * spread, axis=-1, keepdims=True) + norm_eps)
     xhat = spread * inv
+    advance()
     send[0].wait()
-    advance(next(mark))
+    advance()
     send[1].wait()
     for t in range(3):
         for r in range(n_seq):
@@ -848,25 +852,27 @@
     dq, dk, dv = rows_in[0], rows_in[1], rows_in[2]
     fresh = dv[:, 0:VFRESH]
     grad_skip[...] = dv[:, VFRESH:]
-    part2[units_d : 2 * units_d] = matmul_left_t(nl, dq).astype(bf).reshape(units_d, SUB, WID)
-    part2[2 * units_d : 3 * units_d] = matmul_left_t(nl, dk).astype(bf).reshape(units_d, SUB, WID)
+    units_d = d // SUB
+    uv = d // 4 // SUB
+    part2[0:units_d] = matmul_left_t(nl, dq).astype(bf).reshape(units_d, SUB, WID)
+    part2[h2 : h2 + units_d] = matmul_left_t(nl, dk).astype(bf).reshape(units_d, SUB, WID)
     gv = matmul_left_t(nl, fresh).astype(bf)
-    uv = d // 2 // SUB
-    part2[3 * units_d : 3 * units_d + uv, :, 0:VFRESH] = gv[: d // 2].reshape(uv, SUB, VFRESH)
-    part2[3 * units_d : 3 * units_d + uv, :, VFRESH:] = gv[d // 2 :].reshape(uv, SUB, VFRESH)
-    extra = 2 * halves[1] - 3 * units_d - uv
-    if extra:
-        part2[3 * units_d + uv :] = jnp.zeros((extra, SUB, WID), bf)
-    for s, st in enumerate(streams):
-        if st[0] == 1:
-            ex.start(s, 0)
-    advance(next(mark))
-    normed_grad = matmul_right_t(dq, qw[...]) + matmul_right_t(dk, kw[...]) + matmul_right_t(fresh, vw[...])
+    for h in range(2):
+        for side in range(2):
+            r0 = side * (d // 2) + h * (d // 4)
+            part2[h * h2 + units_d : h * h2 + units_d + uv, :, side * VFRESH : (side + 1) * VFRESH] = (
+                gv[r0 : r0 + d // 4].reshape(uv, SUB, VFRESH))
+        if h2 > units_d + uv:
+            part2[h * h2 + units_d + uv : (h + 1) * h2] = jnp.zeros((h2 - units_d - uv, SUB, WID), bf)
+    begin(1, None)
+    advance()
+    for copy in late:
+        copy.wait()
+    normed_grad = matmul_right_t(dq, wf[0]) + matmul_right_t(dk, wf[1]) + matmul_right_t(fresh, wo[0, :, 0:VFRESH])
     f = normed_grad * flat(n1g)
     centre = jnp.mean(f, axis=-1, keepdims=True)
     along = jnp.mean(f * xhat, axis=-1, keepdims=True)
-    grad_input[...] = (mid_grad[...] + (f - centre - xhat * along) * inv).astype(bf)
-    sbuf[0] = small[...]
+    grad_input[...] = (mid_ref[...] + (f - centre - xhat * along) * inv).astype(bf)
     sbuf[0, 0:1] = row_sum(normed_grad * xhat)
     sbuf[0, 1:2] = row_sum(normed_grad)
     sbuf[0, 2:3] = row_sum(dq.astype(f32))
@@ -883,18 +889,19 @@
     tiny.rest()
 
 
-def back(mesh, lens, valid, mixed_grad, pair, third, lse, normed, hidden, n1g, mid_grad, qw, kw, vw, proj_part, small, part1, collective_id):
+def back(mesh, lens, valid, mixed, hidden, og, valid_col, proj_w, proj_b, n2g, n2s, fc_b, out_b, n1g, lse, normed,
+         pair, third, fc_w, out_w, qw, kw, vw, collective_id):
     n_dp, n_seq = mesh.shape["dp"], mesh.shape["seq"]
     rows, d = hidden.shape
     group = rows * n_seq
     half = rows // 2
+    steps = fc_w.shape[1] // FCH
     bf, f32 = jnp.bfloat16, jnp.float32
-    quantum = n_dp * n_seq
-    rows2 = 3 * d + d // 2
-    units2 = -(-rows2 // SUB // quantum) * quantum
-    halves = (part1.shape[0] // 2, units2 // 2)
-    streams = plan_streams(n_dp, n_seq, list(zip(halves, SHARES)), STARTS)
-    order = schedule(streams, (("seq", 9.0),))
+    quantum = n_dp // 2 * n_seq
+    needed = (steps * CHUNK + d // 2 // SUB, d // SUB + d // 4 // SUB)
+    halves = tuple(-(-n // quantum) * quantum for n in needed)
+    streams = plan_streams(n_dp, n_seq, halves, steps)
+    order = schedule(streams)
     n_st = 2 * (bits_of(n_dp) + bits_of(n_seq))
     n_small = bits_of(n_dp) + bits_of(n_seq)
     ns = len(streams)
@@ -902,28 +909,34 @@
     hbm = pl.BlockSpec(memory_space=pl.ANY)
     dma = pltpu.SemaphoreType.DMA
     units = lambda n: pltpu.VMEM((n, SUB, WID), bf)
-    sshape = jax.ShapeDtypeStruct(small.shape, f32)
-    return pl.pallas_call(
-        functools.partial(back_kernel, (n_dp, n_seq, halves, streams, order, MARKS)),
-        in_specs=[pl.BlockSpec(memory_space=pltpu.SMEM)] + [vmem] * 14 + [hbm],
-        out_specs=(hbm, vmem, vmem, vmem, vmem),
+    wide = lambda: pltpu.VMEM((rows, d), f32)
+    sshape = jax.ShapeDtypeStruct((16, WID), f32)
+    args = (lens, valid.reshape(1, -1), mixed, hidden, og, valid_col, proj_w, proj_b, n2g, n2s, fc_b.reshape(1, -1), out_b, n1g, lse, normed,
+            pair, third, fc_w, out_w, qw, kw, vw)
+    outs = pl.pallas_call(
+        functools.partial(back_kernel, (n_dp, n_seq, halves, streams, order, MARKS, steps)),
+        in_specs=[pl.BlockSpec(memory_space=pltpu.SMEM)] + [vmem] * 14 + [hbm] * 7,
+        out_specs=(hbm, vmem, vmem, vmem, vmem, vmem),
         out_shape=(jax.ShapeDtypeStruct((2 * sum(halves), SUB, WID), bf), jax.ShapeDtypeStruct((rows, d), bf),
-                   jax.ShapeDtypeStruct((rows, d - VFRESH), bf), sshape, sshape),
+                   jax.ShapeDtypeStruct((rows, d), bf), jax.ShapeDtypeStruct((rows, d - VFRESH), bf), sshape, sshape),
         scratch_shapes=[
+            pltpu.VMEM((rows, d), bf), wide(), wide(), wide(), wide(), pltpu.VMEM((rows, LANES), f32),
+            pltpu.VMEM((2, d, FCH), bf), pltpu.VMEM((2, FCH, d), bf),
+            pltpu.VMEM((3, group, LANES), bf), pltpu.VMEM((3, group, LANES), bf), units(2 * halves[0]),
             pltpu.VMEM((n_seq, rows, LANES), bf), pltpu.VMEM((n_seq, half, LANES), bf),
             pltpu.VMEM((group, LANES), bf), pltpu.VMEM((n_seq, half, LANES), bf), pltpu.VMEM((group, LANES), bf),
-            pltpu.VMEM((group, group), f32), pltpu.VMEM((group, LANES), f32), pltpu.VMEM((group, LANES), f32),
+            pltpu.VMEM((group, group), bf), pltpu.VMEM((group, LANES), f32), pltpu.VMEM((group, LANES), f32),
             pltpu.VMEM((n_seq, 3, rows, LANES), bf), pltpu.VMEM((n_seq, 3, half, LANES), bf),
             pltpu.VMEM((n_seq, 3, rows, LANES), bf), pltpu.VMEM((n_seq, 3, half, LANES), bf),
-            pltpu.VMEM((3, rows, d), bf), units(units2),
-            units(sum(halves)), units(Exchange.recv_total(streams, halves)), units(sum(halves)),
-            pltpu.VMEM((2 * n_small,) + small.shape, f32),
+            pltpu.VMEM((3, rows, d), bf), units(2 * halves[1]),
+            units(Exchange.recv_total(streams)), units(sum(halves)),
+            pltpu.VMEM((2 * n_small, 16, WID), f32), dma((4, max(4, steps))),
             dma((2, n_seq)), dma((2, n_seq)), dma((2, n_seq)), dma((2, n_seq)),
-            dma((ns, n_st)), dma((ns, n_st)), dma((ns, 2)), dma((n_small,)), dma((n_small,))],
-        compiler_params=pltpu.CompilerParams(collective_id=collective_id, has_side_effects=True, vmem_limit_bytes=63 * 2**20),
+            dma((ns, n_st)), dma((ns, n_st)), dma((ns,)), dma((n_small,)), dma((n_small,))],
+        compiler_params=pltpu.CompilerParams(collective_id=collective_id, has_side_effects=True, vmem_limit_bytes=67043328),
         name="back",
-    )(lens, valid.reshape(1, -1), mixed_grad, pair, third, lse, normed, hidden, n1g, mid_grad, qw, kw, vw, proj_part,
-      small, part1)
+    )(*args)
+    return outs, halves
 
 
 def local(
@@ -956,20 +969,15 @@
     normed, mixed, pair, third, lse = front(
         mesh, hidden_in, skip_values, doc_lens, valid, norm1_gain, norm1_shift, query_w, query_b, key_w, value_w, value_b, 0
     )
-    output, middle_grad, mixed_grad, part, proj_part, small = mlp_block(
-        mixed, hidden_in, out_grad, valid_col, proj_w, proj_b, norm2_gain, norm2_shift, fc_w, fc_b, out_w, out_b
+    (summed, output, grad_input, grad_skip, small_z, small_all), halves = back(
+        mesh, doc_lens, valid, mixed, hidden_in, out_grad, valid_col, proj_w, proj_b, norm2_gain, norm2_shift, fc_b, out_b,
+        norm1_gain, lse, normed, pair, third, fc_w, out_w, query_w, key_w, value_w, 1
     )
-    part1 = part.reshape(-1, SUB, WID)
-    summed, grad_input, grad_skip, small_z, small_all = back(
-        mesh, doc_lens, valid, mixed_grad, pair, third, lse, normed, hidden_in, norm1_gain, middle_grad,
-        query_w, key_w, value_w, proj_part, small, part1, 1
-    )
-    row0 = part1.shape[0] * SUB
     (
         grad_out_w, grad_fc_w, grad_proj_w, grad_query_w, grad_key_w, grad_value_w,
         grad_norm1_gain, grad_norm1_shift, grad_query_b, grad_value_b, grad_proj_b, grad_norm2_gain, grad_norm2_shift,
         grad_out_b, grad_fc_b, norm_values, grad_input, grad_skip,
-    ) = widen(summed.reshape(-1, WID), small_all, small_z, grad_input, grad_skip, row0, D, fc_w.shape[1], VFRESH)
+    ) = widen(summed.reshape(-1, WID), small_all, small_z, grad_input, grad_skip, halves, D, fc_w.shape[1], VFRESH)
     return (
         output,
         grad_input,

time: 226 us -> 213 us (0.942)
  Pallas kernels: 223 us -> 209 us
    pallas_call x1 -> x0, Pallas kernels: 17.3 us -> none  [mlp_block(): pl.pallas_call(functools.partial(mlp_kernel, steps), grid=(steps,), in_sp...]
    pallas_call x1, Pallas kernels: 145 us -> 149 us  [back(): pl.pallas_call(functools.partial(back_kernel, (n_dp, n_seq, halves, strea...]
where the time goes in v3:
time: 213 us; the launch traced here: 212 us
  Pallas kernels  209 us (98%)
    pallas_call x1, Pallas kernels, back(): pl.pallas_call(functools.partial(back_kernel, (n_dp, n_seq, halves, strea...  149 us
    pallas_call x1, Pallas kernels, front(): pl.pallas_call(functools.partial(front_kernel, (n_dp, n_seq)), in_specs=[...  44.3 us
    pallas_call x1, Pallas kernels, widen(): pl.pallas_call(functools.partial(widen_kernel, (pieces, len(shapes))), in...  15.9 us

profile of v3, /device:TPU:0, one launch (start us, length us, event | category | flops | bytes accessed | tf_op | source)
XLA Modules:
  0.0 212.5 jit_solution(6631455868098494175)
XLA Ops:
  0.7 0.8 dynamic-slice_convert_fusion
  1.4 0.8 copy.39.valid_col
  2.2 44.3 %front.1 = (bf16[256,768]{1,0:T(8,128)(2,1)}, bf16[256,768]{1,0:T(8,128)(2,1)}, bf16[3,1024,128]{2,1,0:T(8,128)(2,1)}, bf16[3,1024,128]{2,1,0:T(8,128)(2,1)}, f32[1024,128]{1,0:T(8,128)}) custom-call(s32[1,3]{1,0:T(1,128)} %lens.3, bf16[256,768]{1,0:T(8,128)(2,1)} %hidden.3, bf16[256,384]{1,0:T(8,128)(2,1)} %skip.1, s32[1,1024]{1,0:T(1,128)} %bitcast.5, ...), custom_call_target="tpu_custom_call" | custom-call | tf_op jit(solution)/shard_map/front/pallas_call | solution.py:620
  46.6 149.2 %back.1 = (bf16[1120,8,768]{2,1,0:T(8,128)(2,1)}, bf16[256,768]{1,0:T(8,128)(2,1)}, bf16[256,768]{1,0:T(8,128)(2,1)}, bf16[256,384]{1,0:T(8,128)(2,1)}, f32[16,768]{1,0:T(8,128)}, /*index=5*/f32[16,768]{1,0:T(8,128)}) custom-call(s32[1,3]{1,0:T(1,128)} %lens.3, s32[1,1024]{1,0:T(1,128)} %bitcast.6, bf16[256,768]{1,0:T(8,128)(2,1)} %get-tuple-element.48.mixed, ...), custom_call_target="tpu_custom_call" | custom-call | tf_op jit(solution)/shard_map/back/pallas_call | solution.py:916
  195.8 0.0 copy-start
  195.8 15.9 %widen.1 = (f32[3072,768]{1,0:T(8,128)}, f32[768,3072]{1,0:T(8,128)}, f32[768,768]{1,0:T(8,128)}, f32[768,768]{1,0:T(8,128)}, f32[768,768]{1,0:T(8,128)}, /*inde...) custom-call(bf16[8960,768]{1,0:T(8,128)(2,1)} %bitcast.4, ...), custom_call_target="tpu_custom_call" | custom-call | tf_op jit(solution)/shard_map/widen/pallas_call | solution.py:379
  211.7 0.0 copy-done
  211.7 0.7 copy.41
Async XLA Ops:
  195.8 16.0 %copy-start = (bf16[256,768]{1,0:T(8,128)(2,1)S(1)}, bf16[256,768]{1,0:T(8,128)(2,1)}, u32[]{:S(2)}) copy-start(bf16[256,768]{1,0:T(8,128)(2,1)} %get-tuple-element.96) | copy-start | bytes 1179652

commit v4 on v3

--- a/solution.py
+++ b/solution.py
@@ -26,9 +26,16 @@
 UNIT_BYTES = SUB * WID * 2
 FCH = 768
 CHUNK = FCH // SUB
-READY = (7.0, 10.5, 14.0, 17.5, 20.5)
-START_TWO = 63.0
-MARKS = (8.0, 12.0, 17.0, 24.0, 26.0, 28.0, 29.0, 30.0, 31.0, 32.0, 33.0, 34.0, 40.0, 48.0, 58.0)
+MLP_TIMES = (2.2, 1.1)
+TASKS = (2.5, 2.5, 1.5, 2.3, 1.7, 1.2, 0.7, 1.6, 0.9, 0.7, 0.5, 0.8, 4.5, 3.0)
+ENTRY = 3.5
+MARGIN = 0.5
+SIZES = ((2,) * 12 + (3,), (2,) * 4)
+KINDS = (1, 1, 0, 0, 1, 1, 0, 0, 1, 1, 0, 1, 0, 2, 2, 3, 1)
+HOLDS = (38.3, 64.6, 49.9, 44.9, 39.2, 11.0, 0.0, 28.0, 2.6, 7.4, 2.0, 55.0, 54.9, 0.0, 71.8, 28.5, 11.9)
+LINK = 0.045
+LATENCY = 2.0
+AR_COST = 0.25
 
 
 def bits_of(n):
@@ -49,70 +56,100 @@
     dpb = [("dp", j) for j in range(1, bits_of(n_dp))]
     sqb = [("seq", j) for j in range(bits_of(n_seq))]
     mid = len(dpb) // 2
-    orders = (dpb + sqb, dpb[mid:] + dpb[:mid] + sqb)
+    one, two = dpb[:mid], dpb[mid:]
+    orders = (one + two + sqb, two + one + sqb, one + sqb + two, two + sqb + one, sqb + one + two, sqb + two + one)
     quantum = (n_dp // 2) * n_seq
     streams = []
     for phase, half_units in enumerate(halves):
         total = half_units // quantum
-        count = max(1, total // 2)
+        sizes = SIZES[phase]
+        if sum(sizes) != total:
+            sizes = (2,) * (total // 2) + (1,) * (total % 2)
         first = 0
-        for i in range(count):
-            n = (2 if i < count - 1 else total - 2 * (count - 1)) * quantum
+        for size in sizes:
+            n = size * quantum
             chunk = min(steps, (first + n - 1) // CHUNK)
-            start = READY[min(chunk, len(READY) - 1)] if phase == 0 else START_TWO
-            streams.append((phase, first, n, orders[i % 2], start, chunk))
+            streams.append((phase, first, n, orders[KINDS[len(streams) % len(KINDS)]], chunk if phase == 0 else -1))
             first += n
     return streams
 
 
-def schedule(streams, busy=()):
+def schedule(streams, steps, rows):
     free = {}
-    for res, upto in busy:
-        free[res] = upto
-    out = []
     stages = []
-    for phase, first, n, order, start, _ in streams:
-        seq = []
+    for phase, first, n, order, _ in streams:
+        seq = [(("dp", 0), n)]
         size = n
-        seq.append((("dp", 0), size))
         for d in order:
             size //= 2
             seq.append((d, size))
         for d in reversed(order):
             seq.append((d, size))
             size *= 2
-        seq.append((("dp", 0), size))
-        stages.append(seq)
-    at = [0] * len(streams)
-    waiting = [(st[4], s) for s, st in enumerate(streams)]
-    pending = []
-
-    def launch(s, t):
-        d, size = stages[s][at[s]]
+        stages.append(seq + [(("dp", 0), n)])
+
+    def flow(needs, t):
+        begin = max([t] + [free.get(r, 0.0) for r, _ in needs])
+        for r, dur in needs:
+            free[r] = begin + dur
+        return begin + max(dur for _, dur in needs) + LATENCY
+
+    flying = []
+
+    def launch(s, k, t):
+        d, size = stages[s][k]
         b = size * UNIT_BYTES / 1e6
         if d == ("dp", 0):
-            res, dur = "c", b / 0.5
+            needs = [("c", b / 0.5)]
         elif d[0] == "dp":
-            res, dur = d, b / 0.045
+            needs = [(d, b / LINK)]
+        elif d[1] == 0:
+            needs = [("end", b / LINK)]
         else:
-            res, dur = "seq", b / 0.045 * (1 << d[1])
-        st = max(t, free.get(res, 0.0))
-        free[res] = st + dur
-        pending.append((st + dur + 2.0, s))
-
-    while pending or waiting:
-        pending.sort()
-        waiting.sort()
-        if waiting and (not pending or waiting[0][0] <= pending[0][0]):
-            t, s = waiting.pop(0)
-            launch(s, t)
+            needs = [("mid", 2 * b / LINK), ("end", b / LINK)]
+        end = flow(needs, t)
+        flying.append((max(end, HOLDS[s % len(HOLDS)]) if k == 0 else end, s, k))
+
+    block = rows * LANES * 2 / 1e6 / LINK
+    arrive = {}
+    durations = [MLP_TIMES[i % 2] for i in range(2 * steps)] + list(TASKS)
+    n_tasks = len(durations)
+    plan = [[] for _ in range(n_tasks + 1)]
+    t, task = ENTRY, 0
+    while task < n_tasks or flying:
+        ready = None
+        at_task = task - 2 * steps
+        if task < n_tasks:
+            needs = {3: ("grad pair",), 7: ("grad third",), 11: ("pair",), 12: ("third",)}.get(at_task, ())
+            ready = max([0.0] + [arrive[x] for x in needs])
+        flying.sort()
+        arrived = flying and flying[0][0] + MARGIN <= t
+        if ready is not None and not arrived and (ready <= t or not flying or ready <= flying[0][0]):
+            t = max(t, ready) + durations[task]
+            begun = []
+            if at_task < 0 and task % 2 == 0:
+                begun = [s for s, st in enumerate(streams) if st[0] == 0 and st[4] == task // 2]
+            if at_task == 0:
+                arrive["grad pair"] = flow([("mid", 4 * block), ("end", 3 * block)], t)
+                arrive["grad third"] = flow([("mid", 2 * block), ("end", 1.5 * block)], t)
+            if at_task == 1:
+                begun = [s for s, st in enumerate(streams) if st[0] == 0 and st[4] == steps]
+            if 3 <= at_task <= 6:
+                arrive["pair"] = flow([("mid", 3 * block), ("end", 2.25 * block)], t) + 2.0
+            if 7 <= at_task <= 10:
+                arrive["third"] = flow([("mid", 1.5 * block), ("end", 1.125 * block)], t) + 2.0
+            if at_task == 12:
+                begun = [s for s, st in enumerate(streams) if st[0] == 1]
+            for s in begun:
+                launch(s, 0, t)
+            task += 1
             continue
-        t, s = pending.pop(0)
-        out.append((t, s, at[s]))
-        at[s] += 1
-        if at[s] < len(stages[s]):
-            launch(s, t + 0.3)
-    return out
+        at, s, k = flying.pop(0)
+        plan[task].append((s, k))
+        t = max(t, at) + AR_COST
+        if k + 1 < len(stages[s]):
+            launch(s, k + 1, t)
+    return plan, t
 
 
 class Exchange:
@@ -126,7 +163,7 @@
         self.off = [[st[1]] for st in streams]
         self.roff = []
         r = 0
-        for phase, first, n, order, _, _ in streams:
+        for phase, first, n, order, _ in streams:
             rows = [r]
             r += n
             size = n
@@ -139,7 +176,7 @@
     @staticmethod
     def recv_total(streams):
         r = 0
-        for phase, first, n, order, _, _ in streams:
+        for phase, first, n, order, _ in streams:
             r += n
             for i in range(len(order)):
                 r += n >> (i + 1)
@@ -154,7 +191,7 @@
             device_id=dev, device_id_type=MESH)
 
     def copies(self, s, k):
-        phase, first, n, order, _, _ = self.streams[s]
+        phase, first, n, order, _ = self.streams[s]
         depth = len(order)
         half_units, base = self.halves[phase], self.base[phase]
         part = self.parts[phase]
@@ -183,7 +220,7 @@
                 c.start()
 
     def finish(self, s, k):
-        phase, first, n, order, _, _ = self.streams[s]
+        phase, first, n, order, _ = self.streams[s]
         depth = len(order)
         remote, local = self.copies(s, k)
         remote.wait()
@@ -645,7 +682,7 @@
                 nt_ref, xhat_ref, mid_ref, mlp_acc, two_acc, inv_ref, wf, wo, pair, third, part1,
                 gs, gst, gp, gt, gthird, bias, dk_acc, dv_acc, dsp, dst, drp, drt, rows_in, part2,
                 recv, gat, sbuf, load_sem, gssem, grsem, dssem, drsem, send_sem, recv_sem, local_sem, ssend, srecv_sem):
-    n_dp, n_seq, halves, streams, order, marks, steps = cfg
+    n_dp, n_seq, halves, streams, plan, steps = cfg
     dp, sq = lax.axis_index("dp"), lax.axis_index("seq")
     rows, d = hidden.shape
     half = rows // 2
@@ -686,18 +723,15 @@
     pl.semaphore_wait(barrier, count)
     ex = Exchange(streams, halves, dp, sq, (part1, part2), out, recv, gat, (send_sem, recv_sem, local_sem))
     tiny = Small(n_dp, n_seq, dp, sq, sbuf, ssend, srecv_sem, small_z, small_out)
-    todo = list(order)
-    mark = iter(marks)
+    task = iter(range(1, len(plan)))
 
     def advance():
-        upto = next(mark)
-        while todo and todo[0][0] <= upto:
-            _, s, k = todo.pop(0)
+        for s, k in plan[next(task)]:
             ex.step(s, k)
 
     def begin(phase, chunk):
         for s, st in enumerate(streams):
-            if st[0] == phase and (chunk is None or st[5] == chunk):
+            if st[0] == phase and (chunk is None or st[4] == chunk):
                 ex.start(s, 0)
 
     h1, h2 = halves
@@ -716,6 +750,7 @@
         part1[j * CHUNK : (j + 1) * CHUNK] = matmul_left_t(act, og[...]).astype(bf).reshape(CHUNK, SUB, WID)
         part1[h1 + j * CHUNK : h1 + (j + 1) * CHUNK] = matmul_left_t(nt_ref[...], pre_low).astype(bf).reshape(CHUNK, SUB, WID)
         begin(0, j)
+        advance()
         mlp = matmul(act, wo[slot])
         two = matmul_right_t(pre_low, wf[slot])
         if j == 0:
@@ -727,8 +762,7 @@
         if j + 2 < steps:
             for copy in weight_copies(j + 2):
                 copy.start()
-        if j > 0 and j < steps - 1:
-            advance()
+        advance()
     for copy in late:
         copy.start()
     two_grad = two_acc[...]
@@ -750,6 +784,7 @@
     swap_third = Swap(n_seq, dp, sq, lambda to: gst.at[to], lambda me: gt.at[me], lambda i: gssem.at[1, i], lambda i: grsem.at[1, i])
     swap_pair.start()
     swap_third.start()
+    advance()
     mlp_out = mlp_acc[...] + flat(out_b)
     output[...] = (mid_ref[...] + mlp_out).astype(bf)
     s2 = row_sum(jnp.sum(mlp_out * mlp_out, axis=-1, keepdims=True) * valid_col[...])
@@ -835,14 +870,14 @@
     spread = x - jnp.mean(x, axis=-1, keepdims=True)
     inv = lax.rsqrt(jnp.mean(spread * spread, axis=-1, keepdims=True) + norm_eps)
     xhat = spread * inv
-    advance()
     send[0].wait()
-    advance()
-    send[1].wait()
     for t in range(3):
         for r in range(n_seq):
             c = PAIR_TILE[r] * LANES
             rows_in[t, :, c : c + LANES] = drp[r, t]
+    advance()
+    send[1].wait()
+    for t in range(3):
         for r in range(0, n_seq, 2):
             a, b = join_thirds(drt[r, t], drt[r + 1, t])
             c = THIRD_TILE[r] * LANES
@@ -878,13 +913,11 @@
     sbuf[0, 2:3] = row_sum(dq.astype(f32))
     sbuf[0, 3:4, 0:VFRESH] = row_sum(fresh.astype(f32))
     tiny.copy(0).start()
+    todo = plan[next(task)]
     gap = max(1, len(todo) // (len(tiny.dims) + 2))
-    left = 0
-    while todo:
-        _, s, k = todo.pop(0)
+    for left, (s, k) in enumerate(todo):
         ex.step(s, k)
-        left += 1
-        if left % gap == 0:
+        if left % gap == gap - 1:
             tiny.step()
     tiny.rest()
 
@@ -901,7 +934,7 @@
     needed = (steps * CHUNK + d // 2 // SUB, d // SUB + d // 4 // SUB)
     halves = tuple(-(-n // quantum) * quantum for n in needed)
     streams = plan_streams(n_dp, n_seq, halves, steps)
-    order = schedule(streams)
+    plan, _ = schedule(streams, steps, rows)
     n_st = 2 * (bits_of(n_dp) + bits_of(n_seq))
     n_small = bits_of(n_dp) + bits_of(n_seq)
     ns = len(streams)
@@ -914,7 +947,7 @@
     args = (lens, valid.reshape(1, -1), mixed, hidden, og, valid_col, proj_w, proj_b, n2g, n2s, fc_b.reshape(1, -1), out_b, n1g, lse, normed,
             pair, third, fc_w, out_w, qw, kw, vw)
     outs = pl.pallas_call(
-        functools.partial(back_kernel, (n_dp, n_seq, halves, streams, order, MARKS, steps)),
+        functools.partial(back_kernel, (n_dp, n_seq, halves, streams, plan, steps)),
         in_specs=[pl.BlockSpec(memory_space=pltpu.SMEM)] + [vmem] * 14 + [hbm] * 7,
         out_specs=(hbm, vmem, vmem, vmem, vmem, vmem),
         out_shape=(jax.ShapeDtypeStruct((2 * sum(halves), SUB, WID), bf), jax.ShapeDtypeStruct((rows, d), bf),

time: 213 us -> 206 us (0.967)
  Pallas kernels: 209 us -> 203 us
    pallas_call x1, Pallas kernels: 149 us -> 143 us  [back(): pl.pallas_call(functools.partial(back_kernel, (n_dp, n_seq, halves, strea...]
where the time goes in v4:
time: 206 us
  Pallas kernels  203 us (99%)
    pallas_call x1, Pallas kernels, back(): pl.pallas_call(functools.partial(back_kernel, (n_dp, n_seq, halves, strea...  143 us
    pallas_call x1, Pallas kernels, front(): pl.pallas_call(functools.partial(front_kernel, (n_dp, n_seq)), in_specs=[...  44.3 us
    pallas_call x1, Pallas kernels, widen(): pl.pallas_call(functools.partial(widen_kernel, (pieces, len(shapes))), in...  15.9 us

profile of v4, /device:TPU:0, one launch (start us, length us, event | category | flops | bytes accessed | tf_op | source)
XLA Modules:
  0.0 205.9 jit_solution(7094274861415398020)
XLA Ops:
  0.7 0.8 dynamic-slice_convert_fusion
  1.4 0.8 copy.39.valid_col
  2.2 44.3 %front.1 = (bf16[256,768]{1,0:T(8,128)(2,1)}, bf16[256,768]{1,0:T(8,128)(2,1)}, bf16[3,1024,128]{2,1,0:T(8,128)(2,1)}, bf16[3,1024,128]{2,1,0:T(8,128)(2,1)}, f32[1024,128]{1,0:T(8,128)}) custom-call(s32[1,3]{1,0:T(1,128)} %lens.3, bf16[256,768]{1,0:T(8,128)(2,1)} %hidden.3, bf16[256,384]{1,0:T(8,128)(2,1)} %skip.1, s32[1,1024]{1,0:T(1,128)} %bitcast.5, ...), custom_call_target="tpu_custom_call" | custom-call | tf_op jit(solution)/shard_map/front/pallas_call | solution.py:657
  46.6 142.6 %back.1 = (bf16[1120,8,768]{2,1,0:T(8,128)(2,1)}, bf16[256,768]{1,0:T(8,128)(2,1)}, bf16[256,768]{1,0:T(8,128)(2,1)}, bf16[256,384]{1,0:T(8,128)(2,1)}, f32[16,768]{1,0:T(8,128)}, /*index=5*/f32[16,768]{1,0:T(8,128)}) custom-call(s32[1,3]{1,0:T(1,128)} %lens.3, s32[1,1024]{1,0:T(1,128)} %bitcast.6, bf16[256,768]{1,0:T(8,128)(2,1)} %get-tuple-element.48.mixed, ...), custom_call_target="tpu_custom_call" | custom-call | tf_op jit(solution)/shard_map/back/pallas_call | solution.py:949
  189.2 0.0 copy-start
  189.2 15.9 %widen.1 = (f32[3072,768]{1,0:T(8,128)}, f32[768,3072]{1,0:T(8,128)}, f32[768,768]{1,0:T(8,128)}, f32[768,768]{1,0:T(8,128)}, f32[768,768]{1,0:T(8,128)}, /*inde...) custom-call(bf16[8960,768]{1,0:T(8,128)(2,1)} %bitcast.4, ...), custom_call_target="tpu_custom_call" | custom-call | tf_op jit(solution)/shard_map/widen/pallas_call | solution.py:416
  205.2 0.0 copy-done
  205.2 0.7 copy.41
Async XLA Ops:
  189.2 16.0 %copy-start = (bf16[256,768]{1,0:T(8,128)(2,1)S(1)}, bf16[256,768]{1,0:T(8,128)(2,1)}, u32[]{:S(2)}) copy-start(bf16[256,768]{1,0:T(8,128)(2,1)} %get-tuple-element.96) | copy-start | bytes 1179652

commit v5 on v4

--- a/solution.py
+++ b/solution.py
@@ -29,10 +29,11 @@
 MLP_TIMES = (2.2, 1.1)
 TASKS = (2.5, 2.5, 1.5, 2.3, 1.7, 1.2, 0.7, 1.6, 0.9, 0.7, 0.5, 0.8, 4.5, 3.0)
 ENTRY = 3.5
-MARGIN = 0.5
-SIZES = ((2,) * 12 + (3,), (2,) * 4)
-KINDS = (1, 1, 0, 0, 1, 1, 0, 0, 1, 1, 0, 1, 0, 2, 2, 3, 1)
-HOLDS = (38.3, 64.6, 49.9, 44.9, 39.2, 11.0, 0.0, 28.0, 2.6, 7.4, 2.0, 55.0, 54.9, 0.0, 71.8, 28.5, 11.9)
+MARGIN = 1.5
+TASK_HOLDS = (0.0, 0.0, 0.0, 0.0, 0.0, 0.0, 0.0, 0.0, 0.0, 0.0, 0.0, 0.0, 0.0, 0.0)
+SIZES = ((2, 2, 2, 2, 2, 2, 2, 2, 2, 2, 2, 2, 3), (2, 2, 2, 2))
+KINDS = (1, 0, 0, 1, 1, 0, 1, 0, 0, 1, 1, 1, 0, 1, 3, 0, 2)
+HOLDS = (7.9, 37.1, 25.1, 62.4, 39.0, 7.3, 27.8, 41.0, 59.4, 8.5, 57.8, 22.0, 45.0, 0, 0.8, 10.9, 45.9)
 LINK = 0.045
 LATENCY = 2.0
 AR_COST = 0.25
@@ -121,7 +122,7 @@
         at_task = task - 2 * steps
         if task < n_tasks:
             needs = {3: ("grad pair",), 7: ("grad third",), 11: ("pair",), 12: ("third",)}.get(at_task, ())
-            ready = max([0.0] + [arrive[x] for x in needs])
+            ready = max([TASK_HOLDS[at_task] if at_task >= 0 else 0.0] + [arrive[x] for x in needs])
         flying.sort()
         arrived = flying and flying[0][0] + MARGIN <= t
         if ready is not None and not arrived and (ready <= t or not flying or ready <= flying[0][0]):
@@ -406,7 +407,7 @@
     for h in range(2):
         pieces.append((2 * one + h * two + d, 5, h * VPIECE, 0, True))
     f32, bf = jnp.float32, jnp.bfloat16
-    depth = 4
+    depth = 8
     hbm = pl.BlockSpec(memory_space=pl.ANY)
     vmem = pl.BlockSpec(memory_space=pltpu.VMEM)
     shapes = [(ff, d), (d, ff), (d, d), (d, d), (d, d), (d, vf)]

time: 206 us -> 203 us (0.985)
  Pallas kernels: 203 us -> 199 us
    pallas_call x1, Pallas kernels: 143 us -> 140 us  [back(): pl.pallas_call(functools.partial(back_kernel, (n_dp, n_seq, halves, strea...]
where the time goes in v5:
time: 203 us; the launch traced here: 202 us
  Pallas kernels  199 us (98%)
    pallas_call x1, Pallas kernels, back(): pl.pallas_call(functools.partial(back_kernel, (n_dp, n_seq, halves, strea...  140 us
    pallas_call x1, Pallas kernels, front(): pl.pallas_call(functools.partial(front_kernel, (n_dp, n_seq)), in_specs=[...  44.3 us
    pallas_call x1, Pallas kernels, widen(): pl.pallas_call(functools.partial(widen_kernel, (pieces, len(shapes))), in...  15.2 us

profile of v5, /device:TPU:0, one launch (start us, length us, event | category | flops | bytes accessed | tf_op | source)
XLA Modules:
  0.0 202.4 jit_solution(13535164411342551190)
XLA Ops:
  0.7 0.8 dynamic-slice_convert_fusion
  1.4 0.8 copy.39.valid_col
  2.2 44.3 %front.1 = (bf16[256,768]{1,0:T(8,128)(2,1)}, bf16[256,768]{1,0:T(8,128)(2,1)}, bf16[3,1024,128]{2,1,0:T(8,128)(2,1)}, bf16[3,1024,128]{2,1,0:T(8,128)(2,1)}, f32[1024,128]{1,0:T(8,128)}) custom-call(s32[1,3]{1,0:T(1,128)} %lens.3, bf16[256,768]{1,0:T(8,128)(2,1)} %hidden.3, bf16[256,384]{1,0:T(8,128)(2,1)} %skip.1, s32[1,1024]{1,0:T(1,128)} %bitcast.5, ...), custom_call_target="tpu_custom_call" | custom-call | tf_op jit(solution)/shard_map/front/pallas_call | solution.py:658
  46.6 139.9 %back.1 = (bf16[1120,8,768]{2,1,0:T(8,128)(2,1)}, bf16[256,768]{1,0:T(8,128)(2,1)}, bf16[256,768]{1,0:T(8,128)(2,1)}, bf16[256,384]{1,0:T(8,128)(2,1)}, f32[16,768]{1,0:T(8,128)}, /*index=5*/f32[16,768]{1,0:T(8,128)}) custom-call(s32[1,3]{1,0:T(1,128)} %lens.3, s32[1,1024]{1,0:T(1,128)} %bitcast.6, bf16[256,768]{1,0:T(8,128)(2,1)} %get-tuple-element.48.mixed, ...), custom_call_target="tpu_custom_call" | custom-call | tf_op jit(solution)/shard_map/back/pallas_call | solution.py:950
  186.5 0.0 copy-start
  186.5 15.2 %widen.1 = (f32[3072,768]{1,0:T(8,128)}, f32[768,3072]{1,0:T(8,128)}, f32[768,768]{1,0:T(8,128)}, f32[768,768]{1,0:T(8,128)}, f32[768,768]{1,0:T(8,128)}, /*inde...) custom-call(bf16[8960,768]{1,0:T(8,128)(2,1)} %bitcast.4, ...), custom_call_target="tpu_custom_call" | custom-call | tf_op jit(solution)/shard_map/widen/pallas_call | solution.py:417
  201.7 0.0 copy-done
  201.7 0.7 copy.41
Async XLA Ops:
  186.5 15.2 %copy-start = (bf16[256,768]{1,0:T(8,128)(2,1)S(1)}, bf16[256,768]{1,0:T(8,128)(2,1)}, u32[]{:S(2)}) copy-start(bf16[256,768]{1,0:T(8,128)(2,1)} %get-tuple-element.96) | copy-start | bytes 1179652

commit v6 on v5

--- a/solution.py
+++ b/solution.py
@@ -34,9 +34,9 @@
 SIZES = ((2, 2, 2, 2, 2, 2, 2, 2, 2, 2, 2, 2, 3), (2, 2, 2, 2))
 KINDS = (1, 0, 0, 1, 1, 0, 1, 0, 0, 1, 1, 1, 0, 1, 3, 0, 2)
 HOLDS = (7.9, 37.1, 25.1, 62.4, 39.0, 7.3, 27.8, 41.0, 59.4, 8.5, 57.8, 22.0, 45.0, 0, 0.8, 10.9, 45.9)
-LINK = 0.045
-LATENCY = 2.0
-AR_COST = 0.25
+LINK = 0.044
+LATENCY = 2.3
+AR_COST = 0.35
 
 
 def bits_of(n):

time: 203 us -> 202 us (level)
  no operation moved by 1% of the time
where the time goes in v6:
time: 202 us
  Pallas kernels  199 us (99%)
    pallas_call x1, Pallas kernels, back(): pl.pallas_call(functools.partial(back_kernel, (n_dp, n_seq, halves, strea...  139 us
    pallas_call x1, Pallas kernels, front(): pl.pallas_call(functools.partial(front_kernel, (n_dp, n_seq)), in_specs=[...  44.3 us
    pallas_call x1, Pallas kernels, widen(): pl.pallas_call(functools.partial(widen_kernel, (pieces, len(shapes))), in...  15.2 us

profile of v6, /device:TPU:0, one launch (start us, length us, event | category | flops | bytes accessed | tf_op | source)
XLA Modules:
  0.0 201.6 jit_solution(15432783631738204721)
XLA Ops:
  0.7 0.8 dynamic-slice_convert_fusion
  1.4 0.8 copy.39.valid_col
  2.2 44.3 %front.1 = (bf16[256,768]{1,0:T(8,128)(2,1)}, bf16[256,768]{1,0:T(8,128)(2,1)}, bf16[3,1024,128]{2,1,0:T(8,128)(2,1)}, bf16[3,1024,128]{2,1,0:T(8,128)(2,1)}, f32[1024,128]{1,0:T(8,128)}) custom-call(s32[1,3]{1,0:T(1,128)} %lens.3, bf16[256,768]{1,0:T(8,128)(2,1)} %hidden.3, bf16[256,384]{1,0:T(8,128)(2,1)} %skip.1, s32[1,1024]{1,0:T(1,128)} %bitcast.5, ...), custom_call_target="tpu_custom_call" | custom-call | tf_op jit(solution)/shard_map/front/pallas_call | solution.py:658
  46.6 139.1 %back.1 = (bf16[1120,8,768]{2,1,0:T(8,128)(2,1)}, bf16[256,768]{1,0:T(8,128)(2,1)}, bf16[256,768]{1,0:T(8,128)(2,1)}, bf16[256,384]{1,0:T(8,128)(2,1)}, f32[16,768]{1,0:T(8,128)}, /*index=5*/f32[16,768]{1,0:T(8,128)}) custom-call(s32[1,3]{1,0:T(1,128)} %lens.3, s32[1,1024]{1,0:T(1,128)} %bitcast.6, bf16[256,768]{1,0:T(8,128)(2,1)} %get-tuple-element.48.mixed, ...), custom_call_target="tpu_custom_call" | custom-call | tf_op jit(solution)/shard_map/back/pallas_call | solution.py:950
  185.7 0.0 copy-start
  185.7 15.2 %widen.1 = (f32[3072,768]{1,0:T(8,128)}, f32[768,3072]{1,0:T(8,128)}, f32[768,768]{1,0:T(8,128)}, f32[768,768]{1,0:T(8,128)}, f32[768,768]{1,0:T(8,128)}, /*inde...) custom-call(bf16[8960,768]{1,0:T(8,128)(2,1)} %bitcast.4, ...), custom_call_target="tpu_custom_call" | custom-call | tf_op jit(solution)/shard_map/widen/pallas_call | solution.py:417
  200.9 0.0 copy-done
  200.9 0.7 copy.41
Async XLA Ops:
  185.7 15.2 %copy-start = (bf16[256,768]{1,0:T(8,128)(2,1)S(1)}, bf16[256,768]{1,0:T(8,128)(2,1)}, u32[]{:S(2)}) copy-start(bf16[256,768]{1,0:T(8,128)(2,1)} %get-tuple-element.96) | copy-start | bytes 1179652
